TPU v7x, 512 devices: a whole 4x8x8 slice. The times are simulated.
512 devices in a mesh: orbit: 8 (over z), lon: 16 (over y, core), lat: 4 (over x).
Axes of the slice: x: 4, y: 8, z: 8, core: 2. Of those that a mesh axis runs over, the one named last changes fastest.
Arguments:
- observed: float32 [65536, 64], P(('orbit', 'lon', 'lat')), may hold values from -6 to 6
- ray_start: int32 [65536], P(('orbit', 'lon', 'lat')), may hold values from 0 to 2
- tile_cells: int32 [327680, 16], P(('orbit', 'lon', 'lat')), may hold values from 0 to 4095, as said below
- tile_lengths: float32 [327680, 16], P(('orbit', 'lon', 'lat')), may hold values from 0.05 to 0.2
- channel_kernel: float32 [7, 64], replicated, may hold values from -0.75 to 0.75
- noise_weight: float32 [64], replicated, may hold values from 0.25 to 4
- prior_weight: float32 [7], replicated, may hold values from 0.05 to 0.5
Outputs:
- solution_field: float32 [7, 64, 32, 128], P(None, 'lon', 'lat')
- residual: float32 [7, 64, 32, 128], P(None, 'lon', 'lat')
Inputs may be any that keep to these rules, and one draw needn't show every extreme that they name: `tile_cells`: each row is a path through the block: its segments move across the block's longitudes at one latitude, their level falling to a tangent level and rising again, one level a segment.
All inputs are finite; a program needn't handle non-finite values.
Results may differ from a plain program's by a relative error of at most 0.0045.
Values sent between devices are 32-bit elements; how exact they have to be, the bound alone decides.
No kernel may reach another device: no remote copies, remote signals or barrier semaphores. Data moves between devices by JAX's collectives and lax.ppermute only.
A program may use at most 64 MiB of HBM per device.

v0:
```python
import jax
import jax.numpy as jnp
from jax import lax
from jax.sharding import PartitionSpec as P

CLON = 4
CLAT = 8
LEV = 128
NT = 3
ITERS = 4


highest = lax.Precision.HIGHEST


def padded_2(array, sides, width):
    for axis, dim in sides:
        size, length = (lax.axis_size(axis), array.shape[dim])
        up = [(i, (i + 1) % size) for i in range(size)]
        down = [(j, i) for i, j in up]
        last = lax.slice_in_dim(array, length - width, length, axis=dim)
        first = lax.slice_in_dim(array, 0, width, axis=dim)
        before = lax.ppermute(last, axis, up)
        after = lax.ppermute(first, axis, down)
        array = jnp.concatenate([before, array, after], axis=dim)
    return array


def passed_along(block, axis, distance):
    devices = range(lax.axis_size(axis))
    route = [((i - distance) % len(devices), i) for i in devices]
    return lax.ppermute(block, axis, route)


def prior_term(field_part, lower_level, upper_level, prior_weight):
    padded = padded_2(field_part, (("lon", 1), ("lat", 2)), 1)
    lat_count = field_part.shape[2]
    lat_rows = lax.broadcasted_iota(jnp.int32, (1, 1, lat_count, 1), 2)
    lat_index = lax.axis_index("lat")
    south_side = jnp.where((lat_rows == 0) & (lat_index == 0), 0.0, padded[:, 1:-1, :-2, :])
    north_side = jnp.where(
        (lat_rows == lat_count - 1) & (lat_index == lax.axis_size("lat") - 1),
        0.0,
        padded[:, 1:-1, 2:, :],
    )
    neighbours = padded[:, :-2, 1:-1, :] + padded[:, 2:, 1:-1, :]
    neighbours = neighbours + south_side + north_side + lower_level + upper_level
    return prior_weight[:, None, None, None] * (6.0 * field_part - neighbours)


def body(observed, ray_start, tile_cells, tile_lengths, channel_kernel, noise_weight, prior_weight):
    ray_count = ray_start.shape[0]
    species = channel_kernel.shape[0]
    reach = NT - 1
    span = 2 * NT - 1
    cell_count = CLON * CLAT * LEV
    field_shape = (species, CLON, CLAT, LEV)
    slot_rows = jnp.arange(span, dtype=jnp.int32)[:, None]
    crossing = (
        (ray_start[None, :] <= slot_rows) & (ray_start[None, :] + reach >= slot_rows)
    ).astype(jnp.float32)
    cells_across = jnp.transpose(tile_cells)
    lengths_across = jnp.transpose(tile_lengths)
    cell_places = cells_across.reshape(-1)
    weighted = channel_kernel * noise_weight[None, :]
    channel_gram = jnp.dot(weighted, channel_kernel.T, precision=highest)

    def spread(ray_image):
        arrived = []
        for slot in range(span):
            offset = slot - reach
            outgoing = ray_image * crossing[slot][None, :]
            if offset == 0:
                arrived.append(outgoing)
            else:
                arrived.append(passed_along(outgoing, "lon", offset))
        stacked = jnp.stack(arrived, axis=1).reshape(species, span * ray_count)
        amounts = (stacked[:, None, :] * lengths_across[None]).reshape(species, -1)
        deposited = jnp.zeros((species, cell_count), jnp.float32).at[:, cell_places].add(amounts)
        return deposited.reshape(field_shape)

    slab_size = LEV
    slab_start = 0

    def global_sums(terms):
        return lax.psum((terms[0],), ("lon", "lat"))

    ray_source = lax.dot_general(weighted, observed, (((1,), (1,)), ((), ())), precision=highest)
    rhs_full = lax.psum(spread(ray_source), "orbit")
    solution = jnp.zeros_like(rhs_full)
    residual = rhs_full
    direction = rhs_full
    (norm_now,) = global_sums((jnp.sum(residual * residual),))
    for turn_index in range(ITERS):
        operand = rhs_full if turn_index == 0 else direction
        flat_field = operand.reshape(species, cell_count)
        values = flat_field[:, cells_across]
        tile_totals = jnp.sum(values * lengths_across[None], axis=1).reshape(
            species, span, ray_count
        )
        projected = jnp.zeros((species, ray_count), jnp.float32)
        for normal_slot in range(span):
            normal_offset = normal_slot - reach
            piece = tile_totals[:, normal_slot]
            if normal_offset != 0:
                piece = passed_along(piece, "lon", -normal_offset)
            projected = projected + piece * crossing[normal_slot][None, :]
        partial_image = spread(jnp.dot(channel_gram, projected, precision=highest))
        summed = lax.psum(partial_image, "orbit")
        padded = jnp.pad(operand, ((0, 0), (0, 0), (0, 0), (1, 1)))
        lower_level = lax.dynamic_slice_in_dim(padded, slab_start, slab_size, 3)
        upper_level = lax.dynamic_slice_in_dim(padded, slab_start + 2, slab_size, 3)
        image_field = summed + prior_term(operand, lower_level, upper_level, prior_weight)
        (curvature,) = global_sums((jnp.sum(direction * image_field),))
        step_size = norm_now / curvature
        solution = solution + step_size * direction
        residual = residual - step_size * image_field
        (norm_next,) = global_sums((jnp.sum(residual * residual),))
        direction = residual + norm_next / norm_now * direction
        norm_now = norm_next
    return (solution, residual)


def solution(mesh):
    return jax.shard_map(
        body,
        mesh=mesh,
        in_specs=(
            P(("orbit", "lon", "lat"), None),
            P(("orbit", "lon", "lat")),
            P(("orbit", "lon", "lat"), None),
            P(("orbit", "lon", "lat"), None),
            P(),
            P(),
            P(),
        ),
        out_specs=(P(None, "lon", "lat", None), P(None, "lon", "lat", None)),
        check_vma=False,
    )
```

profile of v0, /device:TPU:1, one launch (start us, length us, event | category | flops | bytes accessed | tf_op | source)
XLA Modules:
  0.0 1863.1 jit_solution(10023135325228196446)
XLA Ops:
  25.6 10.6 bitcast_multiply_fusion.4
  36.2 50.7 %scatter_custom_fusion = f32[7,4096]{0,1:T(8,128)S(1)} fusion(s32[10240]{0:T(1024)S(1)} %bitcast.241, f32[7,10240]{0,1:T(8,128)} %bitcast_multiply_fusion.4, f32[]{:T(128)} %constant.8.clone.1), kind=kCustom, calls=%fused_computation.21 | custom fusion | flops 71680 | bytes 401412 | tf_op jit(solution)/shard_map/scatter-add | solution.py:79
  88.3 72.4 %all-reduce.11.cloned.1.call-done = f32[7,4,8,128]{3,2,1,0:T(8,128)} async-done(((f32[7,4,8,128]{3,2,1,0:T(8,128)}), f32[7,4,8,128]{3,2,1,0:T(8,128)}) %all-reduce.11.cloned.1.call-update) | async-done | bytes 114704 | tf_op jit(solution)/shard_map/psum | solution.py:89
  162.3 34.3 %gather_fusion = f32[10240,7]{1,0:T(8,128)} fusion(f32[7,4096]{0,1:T(8,128)S(1)} %bitcast.210, s32[10240]{0:T(1024)S(1)} %broadcast_clamp_fusion), kind=kCustom, calls=%fused_computation | custom fusion | bytes 614400 | tf_op jit(solution)/shard_map/gather | solution.py:97
  229.5 10.6 bitcast_multiply_fusion.3
  240.1 50.7 %scatter_custom_fusion.1 = f32[7,4096]{0,1:T(8,128)S(1)} fusion(s32[10240]{0:T(1024)S(1)} %bitcast.242, f32[7,10240]{0,1:T(8,128)} %bitcast_multiply_fusion.3, f32[]{:T(128)} %constant.8.clone.1), kind=kCustom, calls=%fused_computation.18 | custom fusion | flops 71680 | bytes 401412 | tf_op jit(solution)/shard_map/scatter-add | solution.py:79
  302.3 59.4 %all-reduce.13.cloned.1.call-done = f32[7,4,8,128]{3,2,1,0:T(8,128)} async-done(((f32[7,4,8,128]{3,2,1,0:T(8,128)}), f32[7,4,8,128]{3,2,1,0:T(8,128)}) %all-reduce.13.cloned.1.call-update) | async-done | bytes 114704 | tf_op jit(solution)/shard_map/psum | solution.py:109
  363.4 126.6 %all-reduce.4 = (f32[]{:T(128)}, f32[]{:T(128)}) all-reduce(f32[]{:T(128)} %get-tuple-element.3, f32[]{:T(128)} %get-tuple-element.2), channel_id=1, replica_groups=mesh['orbit'=8,'lon'=16,'lat'=4] {'lon','lat'}, use_global_device_ids=true, to_apply=%region_3.0 | all-reduce | flops 2 | bytes 16 | tf_op jit(solution)/shard_map/psum | solution.py:86
  492.0 125.5 %psum.95 = f32[]{:T(128)} all-reduce(f32[]{:T(128)} %multiply_reduce_fusion.9), channel_id=1, replica_groups=mesh['orbit'=8,'lon'=16,'lat'=4] {'lon','lat'}, use_global_device_ids=true, to_apply=%region_10.11 | all-reduce | flops 1 | bytes 8 | tf_op jit(solution)/shard_map/psum | solution.py:86
  619.5 34.3 %gather_fusion.1 = f32[10240,7]{1,0:T(8,128)} fusion(f32[7,4096]{0,1:T(8,128)S(1)} %bitcast.211, s32[10240]{0:T(1024)S(1)} %broadcast_clamp_fusion), kind=kCustom, calls=%fused_computation.1 | custom fusion | bytes 614400 | tf_op jit(solution)/shard_map/gather | solution.py:97
  695.7 50.7 %scatter_custom_fusion.2 = f32[7,4096]{0,1:T(8,128)S(1)} fusion(s32[10240]{0:T(1024)S(1)} %bitcast.243, f32[7,10240]{0,1:T(8,128)} %bitcast_multiply_fusion.2, f32[]{:T(128)} %constant.8.clone.1), kind=kCustom, calls=%fused_computation.15 | custom fusion | flops 71680 | bytes 401412 | tf_op jit(solution)/shard_map/scatter-add | solution.py:79
  755.5 60.8 %all-reduce.15.cloned.1.call-done = f32[7,4,8,128]{3,2,1,0:T(8,128)} async-done(((f32[7,4,8,128]{3,2,1,0:T(8,128)}), f32[7,4,8,128]{3,2,1,0:T(8,128)}) %all-reduce.15.cloned.1.call-update) | async-done | bytes 114704 | tf_op jit(solution)/shard_map/psum | solution.py:109
  818.0 126.6 %psum.97 = f32[]{:T(128)} all-reduce(f32[]{:T(128)} %get-tuple-element.14), channel_id=1, replica_groups=mesh['orbit'=8,'lon'=16,'lat'=4] {'lon','lat'}, use_global_device_ids=true, to_apply=%region_15.16 | all-reduce | flops 1 | bytes 8 | tf_op jit(solution)/shard_map/psum | solution.py:86
  946.6 125.5 %psum.98 = f32[]{:T(128)} all-reduce(f32[]{:T(128)} %get-tuple-element.12), channel_id=1, replica_groups=mesh['orbit'=8,'lon'=16,'lat'=4] {'lon','lat'}, use_global_device_ids=true, to_apply=%region_17.18 | all-reduce | flops 1 | bytes 8 | tf_op jit(solution)/shard_map/psum | solution.py:86
  1074.1 34.3 %gather_fusion.2 = f32[10240,7]{1,0:T(8,128)} fusion(f32[7,4096]{0,1:T(8,128)S(1)} %bitcast.212, s32[10240]{0:T(1024)S(1)} %broadcast_clamp_fusion), kind=kCustom, calls=%fused_computation.2 | custom fusion | bytes 614400 | tf_op jit(solution)/shard_map/gather | solution.py:97
  1139.8 10.6 bitcast_multiply_fusion.1
  1150.3 50.7 %scatter_custom_fusion.3 = f32[7,4096]{0,1:T(8,128)S(1)} fusion(s32[10240]{0:T(1024)S(1)} %bitcast.244, f32[7,10240]{0,1:T(8,128)} %bitcast_multiply_fusion.1, f32[]{:T(128)} %constant.8.clone.1), kind=kCustom, calls=%fused_computation.12 | custom fusion | flops 71680 | bytes 401412 | tf_op jit(solution)/shard_map/scatter-add | solution.py:79
  1210.1 60.8 %all-reduce.17.cloned.1.call-done = f32[7,4,8,128]{3,2,1,0:T(8,128)} async-done(((f32[7,4,8,128]{3,2,1,0:T(8,128)}), f32[7,4,8,128]{3,2,1,0:T(8,128)}) %all-reduce.17.cloned.1.call-update) | async-done | bytes 114704 | tf_op jit(solution)/shard_map/psum | solution.py:109
  1272.6 126.6 %psum.100 = f32[]{:T(128)} all-reduce(f32[]{:T(128)} %get-tuple-element.10), channel_id=1, replica_groups=mesh['orbit'=8,'lon'=16,'lat'=4] {'lon','lat'}, use_global_device_ids=true, to_apply=%region_22.23 | all-reduce | flops 1 | bytes 8 | tf_op jit(solution)/shard_map/psum | solution.py:86
  1401.2 125.5 %psum.101 = f32[]{:T(128)} all-reduce(f32[]{:T(128)} %get-tuple-element.8), channel_id=1, replica_groups=mesh['orbit'=8,'lon'=16,'lat'=4] {'lon','lat'}, use_global_device_ids=true, to_apply=%region_24.25 | all-reduce | flops 1 | bytes 8 | tf_op jit(solution)/shard_map/psum | solution.py:86
  1528.7 34.3 %gather_fusion.3 = f32[10240,7]{1,0:T(8,128)} fusion(f32[7,4096]{0,1:T(8,128)S(1)} %bitcast.209, s32[10240]{0:T(1024)S(1)} %broadcast_clamp_fusion), kind=kCustom, calls=%fused_computation.3 | custom fusion | bytes 614400 | tf_op jit(solution)/shard_map/gather | solution.py:97
  1605.0 50.7 %scatter_custom_fusion.4 = f32[7,4096]{0,1:T(8,128)S(1)} fusion(s32[10240]{0:T(1024)S(1)} %bitcast.245, f32[7,10240]{0,1:T(8,128)} %bitcast_multiply_fusion, f32[]{:T(128)} %constant.8.clone.1), kind=kCustom, calls=%fused_computation.9 | custom fusion | flops 71680 | bytes 401412 | tf_op jit(solution)/shard_map/scatter-add | solution.py:79
  1664.8 60.9 %all-reduce.19.cloned.1.call-done = f32[7,4,8,128]{3,2,1,0:T(8,128)} async-done(((f32[7,4,8,128]{3,2,1,0:T(8,128)}), f32[7,4,8,128]{3,2,1,0:T(8,128)}) %all-reduce.19.cloned.1.call-update) | async-done | bytes 114704 | tf_op jit(solution)/shard_map/psum | solution.py:109
  1727.3 126.6 %psum.103 = f32[]{:T(128)} all-reduce(f32[]{:T(128)} %get-tuple-element.6), channel_id=1, replica_groups=mesh['orbit'=8,'lon'=16,'lat'=4] {'lon','lat'}, use_global_device_ids=true, to_apply=%region_29.30 | all-reduce | flops 1 | bytes 8 | tf_op jit(solution)/shard_map/psum | solution.py:86
  (220 shorter events, 219.4 us)
Async XLA Ops:
  7.2 153.5 %all-reduce.11.cloned.1.call-start = ((), (), s32[]{:S(2)}) async-start(), calls=%async_computation | async-start | bytes 229376 | tf_op jit(solution)/shard_map/psum | solution.py:89
  9.4 14.9 collective-permute-start
  15.3 9.0 collective-permute-start.1
  88.2 273.5 %all-reduce.13.cloned.1.call-start = ((), (), s32[]{:S(2)}) async-start(), calls=%async_computation.1 | async-start | bytes 229376 | tf_op jit(solution)/shard_map/psum | solution.py:109
  200.8 12.3 collective-permute-start.7
  205.3 7.8 collective-permute-start.6
  220.0 72.1 %collective-permute-start.12 = (f32[7,1,8,128]{3,2,1,0:T(8,128)S(1)}, f32[7,1,8,128]{3,2,1,0:T(8,128)S(1)}, u32[]{:S(2)}, u32[]{:S(2)}) collective-permute-start(f32[7,1,8,128]{3,2,1,0:T(8,128)S(1)} %get-tuple-element.32), channel_id=1, source_target_pairs={{0,4},{4,8},{8,12},{12,16},{16,20},{20,24},{24,28},{28,32},{32,36}... | collective-permute-start | bytes 86024 | tf_op jit(solution)/shard_map/ppermute | solution.py:23
  222.0 70.2 %collective-permute-start.13 = (f32[7,1,8,128]{3,2,1,0:T(8,128)S(1)}, f32[7,1,8,128]{3,2,1,0:T(8,128)S(1)}, u32[]{:S(2)}, u32[]{:S(2)}) collective-permute-start(f32[7,1,8,128]{3,2,1,0:T(8,128)S(1)} %get-tuple-element.31), channel_id=1, source_target_pairs={{4,0},{8,4},{12,8},{16,12},{20,16},{24,20},{28,24},{32,28},{36,32}... | collective-permute-start | bytes 86024 | tf_op jit(solution)/shard_map/ppermute | solution.py:24
  292.1 524.3 %all-reduce.15.cloned.1.call-start = ((), (), s32[]{:S(2)}) async-start(), calls=%async_computation.2 | async-start | bytes 229376 | tf_op jit(solution)/shard_map/psum | solution.py:109
  658.0 10.6 collective-permute-start.19
  659.9 8.7 collective-permute-start.18
  674.2 73.6 %collective-permute-start.25 = (f32[7,1,8,128]{3,2,1,0:T(8,128)S(1)}, f32[7,1,8,128]{3,2,1,0:T(8,128)S(1)}, u32[]{:S(2)}, u32[]{:S(2)}) collective-permute-start(f32[7,1,8,128]{3,2,1,0:T(8,128)S(1)} %get-tuple-element.30), channel_id=1, source_target_pairs={{4,0},{8,4},{12,8},{16,12},{20,16},{24,20},{28,24},{32,28},{36,32}... | collective-permute-start | bytes 86024 | tf_op jit(solution)/shard_map/ppermute | solution.py:24
  674.2 73.6 %collective-permute-start.24 = (f32[7,1,8,128]{3,2,1,0:T(8,128)S(1)}, f32[7,1,8,128]{3,2,1,0:T(8,128)S(1)}, u32[]{:S(2)}, u32[]{:S(2)}) collective-permute-start(f32[7,1,8,128]{3,2,1,0:T(8,128)S(1)} %get-tuple-element.29), channel_id=1, source_target_pairs={{0,4},{4,8},{8,12},{12,16},{16,20},{20,24},{24,28},{28,32},{32,36}... | collective-permute-start | bytes 86024 | tf_op jit(solution)/shard_map/ppermute | solution.py:23
  677.7 7.3 collective-permute-start.23
  747.8 523.2 %all-reduce.17.cloned.1.call-start = ((), (), s32[]{:S(2)}) async-start(), calls=%async_computation.3 | async-start | bytes 229376 | tf_op jit(solution)/shard_map/psum | solution.py:109
  1112.6 10.6 collective-permute-start.31
  1114.5 8.7 collective-permute-start.30
  1128.8 73.6 %collective-permute-start.37 = (f32[7,1,8,128]{3,2,1,0:T(8,128)S(1)}, f32[7,1,8,128]{3,2,1,0:T(8,128)S(1)}, u32[]{:S(2)}, u32[]{:S(2)}) collective-permute-start(f32[7,1,8,128]{3,2,1,0:T(8,128)S(1)} %get-tuple-element.28), channel_id=1, source_target_pairs={{4,0},{8,4},{12,8},{16,12},{20,16},{24,20},{28,24},{32,28},{36,32}... | collective-permute-start | bytes 86024 | tf_op jit(solution)/shard_map/ppermute | solution.py:24
  1128.8 73.6 %collective-permute-start.36 = (f32[7,1,8,128]{3,2,1,0:T(8,128)S(1)}, f32[7,1,8,128]{3,2,1,0:T(8,128)S(1)}, u32[]{:S(2)}, u32[]{:S(2)}) collective-permute-start(f32[7,1,8,128]{3,2,1,0:T(8,128)S(1)} %get-tuple-element.27), channel_id=1, source_target_pairs={{0,4},{4,8},{8,12},{12,16},{16,20},{20,24},{24,28},{28,32},{32,36}... | collective-permute-start | bytes 86024 | tf_op jit(solution)/shard_map/ppermute | solution.py:23
  1202.4 523.3 %all-reduce.19.cloned.1.call-start = ((), (), s32[]{:S(2)}) async-start(), calls=%async_computation.4 | async-start | bytes 229376 | tf_op jit(solution)/shard_map/psum | solution.py:109
  1567.2 10.6 collective-permute-start.43
  1569.2 8.7 collective-permute-start.42
  1583.4 73.6 %collective-permute-start.49 = (f32[7,1,8,128]{3,2,1,0:T(8,128)S(1)}, f32[7,1,8,128]{3,2,1,0:T(8,128)S(1)}, u32[]{:S(2)}, u32[]{:S(2)}) collective-permute-start(f32[7,1,8,128]{3,2,1,0:T(8,128)S(1)} %get-tuple-element.26), channel_id=1, source_target_pairs={{4,0},{8,4},{12,8},{16,12},{20,16},{24,20},{28,24},{32,28},{36,32}... | collective-permute-start | bytes 86024 | tf_op jit(solution)/shard_map/ppermute | solution.py:24
  1583.5 73.6 %collective-permute-start.48 = (f32[7,1,8,128]{3,2,1,0:T(8,128)S(1)}, f32[7,1,8,128]{3,2,1,0:T(8,128)S(1)}, u32[]{:S(2)}, u32[]{:S(2)}) collective-permute-start(f32[7,1,8,128]{3,2,1,0:T(8,128)S(1)} %get-tuple-element.25), channel_id=1, source_target_pairs={{0,4},{4,8},{8,12},{12,16},{16,20},{20,24},{24,28},{28,32},{32,36}... | collective-permute-start | bytes 86024 | tf_op jit(solution)/shard_map/ppermute | solution.py:23
  (40 other events, 974.8 us)
Sparse Core Ops, SparseCore 0:
  88.3 72.3 all-reduce.10
  292.2 69.4 all-reduce.12
  747.9 68.4 all-reduce.14
  1202.5 68.4 all-reduce.16
  1657.1 68.4 all-reduce.18
where the time goes:
time: 1870 us; the launch traced here: 1860 us
  blocking collectives  883 us (47%)
  waiting for transfers between devices  355 us (19%)
  other arithmetic  335 us (18%)
  local copies, waits for them, and re-layouts  150 us (8%)
  starting transfers between devices  114 us (6%)
  between operations  24.1 us (1%)
    psum x7, blocking collectives, global_sums(): return lax.psum((terms[0],), ('lon', 'lat'))  883 us
    scatter-add x5, other arithmetic, spread(): jnp.zeros((species, cell_count), jnp.float32).at[:, cell_places]  253 us
    psum x4, waiting for transfers between devices, body(): summed = lax.psum(partial_image, 'orbit')  242 us
    gather x4, local copies, waits for them, and re-layouts, body(): values = flat_field[:, cells_across]  137 us
    ppermute x36, starting transfers between devices, passed_along(): return lax.ppermute(block, axis, route)  84.6 us
    psum x1, waiting for transfers between devices, body(): rhs_full = lax.psum(spread(ray_source), 'orbit')  72.4 us
    mul x5, other arithmetic, spread(): amounts = (stacked[:, None, :] * lengths_across[None]).reshape(species, -1)  52.9 us
  transfers between devices with their start and end apart: 57, of which 18 were waited for; matrix products, arithmetic and copies ran while one was open for 14% of the time, Pallas kernels for 0%

commit v1 on v0

v1 whole, which is shorter than its diff:
```python
import jax
import jax.numpy as jnp
from jax import lax
from jax.experimental import pallas as pl
from jax.experimental.pallas import tpu as pltpu
from jax.sharding import PartitionSpec as P

S = 7
CLON = 4
CLAT = 8
LEV = 128
NT = 3
TILE = 16
ITERS = 4
SPAN = 5
ORB = 8
RAYS = 128
SLOT = ORB * RAYS
CELL = CLON * LEV
SHARD = SPAN * 2 * TILE + 8
F32 = jnp.float32
BF16 = jnp.bfloat16
highest = lax.Precision.HIGHEST
VMEM = pltpu.VMEM
LIMIT = pltpu.CompilerParams(vmem_limit_bytes=48 << 20)


def vspec():
    return pl.BlockSpec(memory_space=pltpu.VMEM)


def sspec():
    return pl.BlockSpec(memory_space=pltpu.SMEM)


def shift(block, axis, distance):
    size = lax.axis_size(axis)
    return lax.ppermute(block, axis, [(i, (i + distance) % size) for i in range(size)])


def split(values):
    high = values.astype(BF16)
    low = (values - high.astype(F32)).astype(BF16)
    return high, low


def start_kernel(prior_ref, obs_ref, start_ref, cells_ref, lengths_ref, kern_ref, noise_ref, shard_ref, gram_ref, prior_out, scale_out, pad):
    for slot in range(SPAN):
        rows = pl.ds(slot * RAYS, RAYS)
        base = slot * 2 * TILE
        shard_ref[base:base + TILE, :] = cells_ref[rows, :].astype(F32).T
        shard_ref[base + TILE:base + 2 * TILE, :] = lengths_ref[rows, :].T
    pad[...] = jnp.zeros_like(pad)
    pad[0:S, :] = kern_ref[...]
    kern = pad[...]
    weighted = kern * noise_ref[...]
    source = lax.dot_general(weighted, obs_ref[...], (((1,), (1,)), ((), ())), precision=highest, preferred_element_type=F32)
    base = SPAN * 2 * TILE
    sub = lax.broadcasted_iota(jnp.int32, (8, RAYS), 0)
    start = jnp.broadcast_to(start_ref[...].astype(F32), (8, RAYS))
    shard_ref[base:base + 8, :] = jnp.where(sub == S, start, source)
    wide = jnp.concatenate([kern] * CLAT, axis=0)
    wide_weighted = jnp.concatenate([weighted] * CLAT, axis=0)
    gram = lax.dot_general(wide_weighted, wide, (((1,), (1,)), ((), ())), precision=highest, preferred_element_type=F32)
    row = lax.broadcasted_iota(jnp.int32, gram.shape, 0)
    col = lax.broadcasted_iota(jnp.int32, gram.shape, 1)
    trace = jnp.sum(jnp.where((row == col) & (row < 8), gram, 0.0))
    top = prior_ref[0]
    for s in range(1, S):
        top = jnp.maximum(top, prior_ref[s])
    bound = jnp.full((8, 128), trace * 128.0 + 12.0 * top, F32)
    scale = 1.0 / bound
    scale_out[...] = scale
    gram_ref[...] = jnp.where((row >> 3) == (col >> 3), gram, 0.0) * scale[0:1, 0:1]
    species = lax.broadcasted_iota(jnp.int32, (CLAT * 8, 128), 0) & 7
    prior = jnp.zeros((CLAT * 8, 128), F32)
    for s in range(S):
        prior = jnp.where(species == s, prior_ref[s], prior)
    prior_out[...] = prior * scale[0:1, 0:1]


def gather_kernel(orbit_ref, *refs):
    shards, out = refs[:ORB], refs[ORB]
    base = SPAN * 2 * TILE
    for k in range(ORB):
        spot = lax.rem(orbit_ref[0] + (ORB - k), ORB)
        out[:, pl.ds(pl.multiple_of(spot * RAYS, RAYS), RAYS)] = shards[k][base:base + 8, :]


def build_kernel(orbit_ref, *refs):
    shards, (w_ref, lat_ref) = refs[:ORB], refs[ORB:]
    sub = lax.broadcasted_iota(jnp.int32, (8, RAYS), 0)
    odd = (sub & 1) == 1
    for k in range(ORB):
        spot = pl.multiple_of(lax.rem(orbit_ref[0] + (ORB - k), ORB) * RAYS, RAYS)

        def slot_body(slot, carry):
            base = pl.multiple_of(slot * 2 * TILE, 2 * TILE)
            cells = shards[k][pl.ds(base, TILE), :].astype(jnp.int32)
            lengths = shards[k][pl.ds(base + TILE, TILE), :]
            lat_ref[slot, :, pl.ds(spot, RAYS)] = jnp.broadcast_to((cells[0:1, :] >> 7) & 7, (8, RAYS))
            places = ((cells >> 10) << 7) | (cells & 127)
            first = jnp.broadcast_to(cells[0:1, :] & 1, (8, RAYS)) == 1
            swap = first != odd
            keys = []
            sizes = []
            for j in range(TILE // 2):
                even_key = jnp.broadcast_to(places[2 * j:2 * j + 1, :], (8, RAYS))
                odd_key = jnp.broadcast_to(places[2 * j + 1:2 * j + 2, :], (8, RAYS))
                keys.append(jnp.where(swap, odd_key, even_key) - sub)
                even_len = jnp.broadcast_to(lengths[2 * j:2 * j + 1, :], (8, RAYS))
                odd_len = jnp.broadcast_to(lengths[2 * j + 1:2 * j + 2, :], (8, RAYS))
                sizes.append(jnp.where(swap, odd_len, even_len))
            for pair in range(CELL // 16):
                parts = []
                for half in range(2):
                    offset = pair * 16 + half * 8
                    terms = [jnp.where(key == offset, size, 0.0) for key, size in zip(keys, sizes)]
                    while len(terms) > 1:
                        terms = [a + b for a, b in zip(terms[::2], terms[1::2])]
                    parts.append(terms[0])
                high, low = split(jnp.concatenate(parts, axis=0))
                w_ref[slot, pl.ds(pair * 16, 16), pl.ds(spot, RAYS)] = high
                w_ref[slot, pl.ds(CELL + pair * 16, 16), pl.ds(spot, RAYS)] = low
            return carry

        lax.fori_loop(0, SPAN, slot_body, 0)


def masked_rows(values, lat):
    rows = jnp.concatenate([jnp.where(lat == l, values, 0.0) for l in range(CLAT)], axis=0)
    return jnp.concatenate(split(rows), axis=0)


def back_all(sums, lats, w_ref):
    total = None
    for slot in range(SPAN):
        part = lax.dot_general(
            masked_rows(sums[slot], lats[slot]), w_ref[slot], (((1,), (1,)), ((), ())), preferred_element_type=F32
        )
        total = part if total is None else total + part
    total = total[:, :CELL] + total[:, CELL:]
    return total[:64] + total[64:]


def project_all(v, lats, w_ref, outs):
    own_ref, left_ref, right_ref, left2_ref, right2_ref, down_ref, up_ref = outs
    halves = jnp.concatenate(split(v), axis=0)
    rows = jnp.concatenate([halves, halves], axis=1)
    for slot in range(SPAN):
        wide = jnp.dot(rows, w_ref[slot], preferred_element_type=F32)
        wide = wide[:64] + wide[64:]
        lat = lats[slot]
        total = jnp.where(lat == 0, wide[0:8], 0.0)
        for l in range(1, CLAT):
            total = total + jnp.where(lat == l, wide[8 * l:8 * l + 8], 0.0)
        own_ref[slot] = total
        if slot >= 1:
            left_ref[slot - 1] = total
        if slot <= 3:
            right_ref[slot] = total
        if slot >= 2:
            left2_ref[slot - 2] = total
        if slot <= 2:
            right2_ref[slot] = total
    for l in range(CLAT):
        left_ref[4, :, pl.ds(l * LEV, LEV)] = v[8 * l:8 * l + 8, 0:LEV]
        right_ref[4, :, pl.ds(l * LEV, LEV)] = v[8 * l:8 * l + 8, CELL - LEV:]
    down_ref[...] = v[0:8]
    up_ref[...] = v[56:64]


def init_kernel(z2, z0, z1, z3, z4, lat_ref, w_ref, v_ref, mask_ref, *outs):
    sums, lats = [], []
    for slot, z in enumerate((z0, z1, z2, z3, z4)):
        begin = jnp.broadcast_to(z[S:S + 1, :], (8, SLOT))
        present = (begin <= slot) & (begin + (NT - 1) >= slot)
        lat = jnp.where(present, lat_ref[slot], -1)
        mask_ref[slot] = lat
        lats.append(lat)
        sub = lax.broadcasted_iota(jnp.int32, (8, SLOT), 0)
        sums.append(jnp.where(sub < S, z[...], 0.0))
    v = back_all(sums, lats, w_ref)
    v_ref[...] = v
    project_all(v, lats, w_ref, outs)


def next_vector(v_ref, own_ref, plus1, minus1, plus2, minus2, south, north, mask_ref, w_ref, gram_ref, prior_ref):
    sums = []
    for slot in range(SPAN):
        total = own_ref[slot]
        if slot <= 3:
            total = total + plus1[slot]
        if slot >= 1:
            total = total + minus1[slot - 1]
        if slot <= 2:
            total = total + plus2[slot]
        if slot >= 2:
            total = total + minus2[slot - 2]
        sums.append(total)
    lats = [mask_ref[slot] for slot in range(SPAN)]
    image = back_all(sums, lats, w_ref)
    image = jnp.dot(gram_ref[...], image, precision=highest, preferred_element_type=F32)
    v = v_ref[...]
    west = jnp.concatenate([minus1[4, :, l * LEV:(l + 1) * LEV] for l in range(CLAT)], axis=0)
    east = jnp.concatenate([plus1[4, :, l * LEV:(l + 1) * LEV] for l in range(CLAT)], axis=0)
    cols = [west] + [v[:, c * LEV:(c + 1) * LEV] for c in range(CLON)] + [east]
    lane = lax.broadcasted_iota(jnp.int32, (64, LEV), 1)
    pieces = []
    for c in range(CLON):
        here = cols[c + 1]
        below = jnp.where(lane == 0, 0.0, pltpu.roll(here, 1, 1))
        above = jnp.where(lane == LEV - 1, 0.0, pltpu.roll(here, LEV - 1, 1))
        south_side = jnp.concatenate([south[:, c * LEV:(c + 1) * LEV], here[:56]], axis=0)
        north_side = jnp.concatenate([here[8:], north[:, c * LEV:(c + 1) * LEV]], axis=0)
        near = cols[c] + cols[c + 2] + below + above + south_side + north_side
        pieces.append(prior_ref[...] * (6.0 * here - near))
    return image + jnp.concatenate(pieces, axis=1), lats


def step_kernel(*refs):
    v, lats = next_vector(*refs[:12])
    refs[12][...] = v
    project_all(v, lats, refs[9], refs[13:])


PAIRS = [(i, j) for i in range(ITERS + 1) for j in range(i, ITERS + 1) if (i, j) != (ITERS, ITERS)]


def last_kernel(*refs):
    v, _ = next_vector(*refs[:12])
    earlier = refs[12:12 + ITERS - 1]
    out_ref, pair_ref = refs[12 + ITERS - 1:]
    out_ref[...] = v
    vectors = [ref[...] for ref in earlier] + [refs[0][...], v]
    pair_ref[...] = jnp.zeros_like(pair_ref)
    for n, (i, j) in enumerate(PAIRS):
        product = vectors[i] * vectors[j]
        product = jnp.sum(product, axis=0, keepdims=True)
        fold = product[:, 0:LEV]
        for c in range(1, CLON):
            fold = fold + product[:, c * LEV:(c + 1) * LEV]
        pair_ref[n:n + 1, :] = fold


def combine_kernel(scale_ref, *refs):
    sums_ref, vector_refs, (x_ref, r_ref, spread) = refs[0], refs[1:ITERS + 2], refs[ITERS + 2:]
    sums = jnp.sum(sums_ref[...], axis=1, keepdims=True)
    table = {}
    for n, (i, j) in enumerate(PAIRS):
        table[i, j] = table[j, i] = sums[n:n + 1, :]
    scale = scale_ref[0:1, 0:1]
    zero, one = jnp.zeros((1, 1), F32), jnp.ones((1, 1), F32)
    x = [zero] * (ITERS + 1)
    r = [one] + [zero] * ITERS
    d = list(r)

    def form(a, b, na, nb, off):
        total = None
        for i in range(na):
            inner = None
            for j in range(nb):
                term = b[j] * table[i, j + off]
                inner = term if inner is None else inner + term
            term = a[i] * inner
            total = term if total is None else total + term
        return total

    norm = table[0, 0]
    for k in range(ITERS):
        alpha = norm / form(d, d, k + 1, k + 1, 1)
        for i in range(k + 1):
            x[i] = x[i] + alpha * d[i]
            r[i + 1] = r[i + 1] - alpha * d[i]
        if k < ITERS - 1:
            after = form(r, r, k + 2, k + 2, 0)
            ratio = after / norm
            d = [r[i] + ratio * d[i] for i in range(ITERS + 1)]
            norm = after
    x = [scale * value for value in x]
    for c in range(CLON):
        parts = [ref[:, c * LEV:(c + 1) * LEV] for ref in vector_refs]
        total = x[0] * parts[0]
        for i in range(1, ITERS):
            total = total + x[i] * parts[i]
        spread[0, c] = total
        total = r[0] * parts[0]
        for i in range(1, ITERS + 1):
            total = total + r[i] * parts[i]
        spread[1, c] = total
        for s in range(S):
            x_ref[s, c] = spread[0, c, pl.ds(s, CLAT, stride=8), :]
            r_ref[s, c] = spread[1, c, pl.ds(s, CLAT, stride=8), :]


def shape(*dims, dtype=F32):
    return jax.ShapeDtypeStruct(dims, dtype)


def call(kernel, outs, n_in, scalar=False, scratch=()):
    return pl.pallas_call(
        kernel,
        out_shape=outs,
        in_specs=([sspec()] if scalar else []) + [vspec()] * n_in,
        out_specs=[vspec()] * len(outs),
        scratch_shapes=scratch,
        compiler_params=LIMIT,
    )


SENT = (
    shape(SPAN, 8, SLOT), shape(5, 8, SLOT), shape(5, 8, SLOT), shape(3, 8, SLOT), shape(3, 8, SLOT), shape(8, CELL), shape(8, CELL),
)


def exchange(own, left, right, left2, right2, down, up):
    n_lat = lax.axis_size("lat")
    plus2 = shift(left2, "lon", -2)
    minus2 = shift(right2, "lon", 2)
    plus1 = shift(left, "lon", -1)
    minus1 = shift(right, "lon", 1)
    south = lax.ppermute(up, "lat", [(i, i + 1) for i in range(n_lat - 1)])
    north = lax.ppermute(down, "lat", [(i + 1, i) for i in range(n_lat - 1)])
    return own, plus1, minus1, plus2, minus2, south, north


def total_over(array, axis):
    size = lax.axis_size(axis)
    step = 1
    while step < size:
        others = [shift(array, axis, step * k) for k in (1, 2, 3)]
        array = (array + others[0]) + (others[1] + others[2])
        step *= 4
    return array


def body(observed, ray_start, tile_cells, tile_lengths, channel_kernel, noise_weight, prior_weight):
    orbit = lax.axis_index("orbit").astype(jnp.int32).reshape(1)
    shard, gram, prior, scale = call(
        start_kernel,
        (shape(SHARD, RAYS), shape(64, 64), shape(64, LEV), shape(8, LEV)),
        6,
        True,
        [pltpu.VMEM((8, 64), F32)],
    )(prior_weight, observed, ray_start.reshape(1, RAYS), tile_cells, tile_lengths, channel_kernel, noise_weight.reshape(1, -1))
    shards = [shard] + [shift(shard, "orbit", k) for k in range(1, ORB)]
    (z,) = call(gather_kernel, (shape(8, SLOT),), ORB, True)(orbit, *shards)
    z1, z3 = shift(z, "lon", -1), shift(z, "lon", 1)
    z0, z4 = shift(z, "lon", -2), shift(z, "lon", 2)
    w, lat = call(
        build_kernel, (shape(SPAN, 2 * CELL, SLOT, dtype=BF16), shape(SPAN, 8, SLOT, dtype=jnp.int32)), ORB, True
    )(orbit, *shards)
    v, mask, *sent = call(init_kernel, (shape(64, CELL), shape(SPAN, 8, SLOT, dtype=jnp.int32)) + SENT, 7)(z, z0, z1, z3, z4, lat, w)
    vectors = [v]
    for turn in range(ITERS - 1):
        v, *sent = call(step_kernel, (shape(64, CELL),) + SENT, 12)(v, *exchange(*sent), mask, w, gram, prior)
        vectors.append(v)
    v, pairs = call(last_kernel, (shape(64, CELL), shape(16, LEV)), 12 + ITERS - 1)(
        v, *exchange(*sent), mask, w, gram, prior, *vectors[:-1]
    )
    vectors.append(v)
    pairs = total_over(total_over(pairs, "lat"), "lon")
    field = shape(S, CLON, CLAT, LEV)
    return tuple(call(combine_kernel, (field, field), ITERS + 3, False, [pltpu.VMEM((2, CLON, 64, LEV), F32)])(scale, pairs, *vectors))


def solution(mesh):
    return jax.shard_map(
        body,
        mesh=mesh,
        in_specs=(
            P(("orbit", "lon", "lat"), None),
            P(("orbit", "lon", "lat")),
            P(("orbit", "lon", "lat"), None),
            P(("orbit", "lon", "lat"), None),
            P(),
            P(),
            P(),
        ),
        out_specs=(P(None, "lon", "lat", None), P(None, "lon", "lat", None)),
        check_vma=False,
    )
```

time: 1870 us -> 231 us (0.12)
  blocking collectives: 883 us -> 0 us
  other arithmetic: 335 us -> 0.02 us
  waiting for transfers between devices: 355 us -> 34.3 us
  local copies, waits for them, and re-layouts: 150 us -> 5.38 us
  Pallas kernels: 0 us -> 60.9 us
  between operations: 24.1 us -> 1.13 us
    psum x7 -> x0, blocking collectives: 883 us -> none  [global_sums(): return lax.psum((terms[0],), ('lon', 'lat'))]
    psum x5 -> x0, waiting for transfers between devices: 314 us -> none  [the longest x4 242 us: body(): summed = lax.psum(partial_image, 'orbit')]
    scatter-add x5 -> x0, other arithmetic: 253 us -> none  [spread(): jnp.zeros((species, cell_count), jnp.float32).at[:, cell_places]]
    gather x4 -> x0, local copies, waits for them, and re-layouts: 137 us -> none  [body(): values = flat_field[:, cells_across]]
    pallas_call x0 -> x9, Pallas kernels: none -> 60.9 us  [the longest x3 27.9 us: body(): call(step_kernel, (shape(64, CELL),) + SENT, 12)]
    mul x5 -> x0, other arithmetic: 52.9 us -> none  [spread(): amounts = (stacked[:, None, :] * lengths_across[None]).reshape(species, -1)]
    reduce_sum x11 -> x0, other arithmetic: 24.8 us -> none  [the longest x4 16.3 us: body(): jnp.sum(values * lengths_across[None], axis=1)]
    ppermute x52 -> x44, starting transfers between devices: 114 us -> 127 us  [the longest x36 108 us: shift(): lax.ppermute(block, axis, [(i, (i + distance) % size) for i in range(size)])]
  transfers between devices with their start and end apart: 57 -> 44, of which waited for: 18 -> 16; matrix products, arithmetic and copies ran while one was open for 14% -> 0% of each run, Pallas kernels for 0% -> 6%
where the time goes in v1:
time: 231 us; the launch traced here: 229 us
  starting transfers between devices  127 us (55%)
  Pallas kernels  60.9 us (26%)
  waiting for transfers between devices  34.3 us (15%)
  local copies, waits for them, and re-layouts  5.38 us (2%)
    ppermute x36, starting transfers between devices, shift(): lax.ppermute(block, axis, [(i, (i + distance) % size) for i in range(size)])  108 us
    pallas_call x3, Pallas kernels, body(): call(step_kernel, (shape(64, CELL),) + SENT, 12)  27.9 us
    ppermute x36, waiting for transfers between devices, shift(): lax.ppermute(block, axis, [(i, (i + distance) % size) for i in range(size)])  16.7 us
    ppermute x4, waiting for transfers between devices, exchange(): north = lax.ppermute(down, 'lat', [(i + 1, i) for i in range(n_lat - 1)])  14.2 us
    pallas_call x1, Pallas kernels, body(): call(build_kernel, (shape(SPAN, 2 * CELL, SLOT, dtype=BF16), shape(SPAN,...  14.2 us
    ppermute x4, starting transfers between devices, exchange(): south = lax.ppermute(up, 'lat', [(i, i + 1) for i in range(n_lat - 1)])  13.5 us
    pallas_call x1, Pallas kernels, body(): call(init_kernel, (shape(64, CELL), shape(SPAN, 8, SLOT, dtype=jnp.int32)...  9.03 us
    pallas_call x1, Pallas kernels, body(): call(last_kernel, (shape(64, CELL), shape(16, LEV)), 12 + ITERS - 1)  7.9 us
  transfers between devices with their start and end apart: 44, of which 16 were waited for; matrix products, arithmetic and copies ran while one was open for 0% of the time, Pallas kernels for 6%

profile of v1, /device:TPU:1, one launch (start us, length us, event | category | flops | bytes accessed | tf_op | source)
XLA Modules:
  0.0 228.9 jit_solution(4219457587121163034)
XLA Ops:
  7.0 11.5 %collective-permute-start.6 = (f32[168,128]{1,0:T(8,128)S(1)}, f32[168,128]{1,0:T(8,128)S(1)}, u32[]{:S(2)}, u32[]{:S(2)}) collective-permute-start(f32[168,128]{1,0:T(8,128)S(1)} %get-tuple-element.44.refs_0_), channel_id=1, source_target_pairs={{0,448},{64,0},{128,64},{192,128},{256,192},{320,256},{384,320},{4... | collective-permute-start | bytes 258056 | tf_op jit(solution)/shard_map/ppermute | solution.py:38
  22.6 7.3 %collective-permute-start.3 = (f32[168,128]{1,0:T(8,128)S(1)}, f32[168,128]{1,0:T(8,128)S(1)}, u32[]{:S(2)}, u32[]{:S(2)}) collective-permute-start(f32[168,128]{1,0:T(8,128)S(1)} %get-tuple-element.44.refs_0_), channel_id=1, source_target_pairs={{0,256},{64,320},{128,384},{192,448},{256,0},{320,64},{384,128},{4... | collective-permute-start | bytes 258056 | tf_op jit(solution)/shard_map/ppermute | solution.py:38
  38.4 5.5 %collective-permute-done.1.refs_2_ = f32[168,128]{1,0:T(8,128)S(1)} collective-permute-done((f32[168,128]{1,0:T(8,128)S(1)}, f32[168,128]{1,0:T(8,128)S(1)}, u32[]{:S(2)}, u32[]{:S(2)}) %collective-permute-start.1) | collective-permute-done | bytes 86048 | tf_op jit(solution)/shard_map/ppermute | solution.py:38
  55.1 14.2 %shard_map.88 = (bf16[5,1024,1024]{2,1,0:T(8,128)(2,1)}, s32[5,8,1024]{2,1,0:T(8,128)S(1)}) custom-call(s32[1]{0:T(128)} %bitcast.2.orbit_ref, f32[168,128]{1,0:T(8,128)S(1)} %get-tuple-element.44.refs_0_, f32[168,128]{1,0:T(8,128)S(1)} %collective-permute-done.refs_1_, f32[168,128]{1,0:T(8,128)S(1)} %collective-permute-done.1.refs_2_, ...), custom_call_target="tpu_custom_call" | custom-call | tf_op jit(solution)/shard_map/pallas_call | solution.py:350
  69.3 9.0 %shard_map.89 = (f32[64,512]{1,0:T(8,128)S(1)}, s32[5,8,1024]{2,1,0:T(8,128)S(1)}, f32[5,8,1024]{2,1,0:T(8,128)S(1)}, f32[5,8,1024]{2,1,0:T(8,128)S(1)}, f32[5,8...) custom-call(f32[8,1024]{1,0:T(8,128)S(1)} %shard_map.87.z2, ...), custom_call_target="tpu_custom_call" | custom-call | tf_op jit(solution)/shard_map/pallas_call | solution.py:353
  80.4 3.6 %collective-permute-start.13 = (f32[3,8,1024]{2,1,0:T(8,128)S(1)}, f32[3,8,1024]{2,1,0:T(8,128)S(1)}, u32[]{:S(2)}, u32[]{:S(2)}) collective-permute-start(f32[3,8,1024]{2,1,0:T(8,128)S(1)} %get-tuple-element.51), channel_id=1, source_target_pairs={{0,56},{4,60},{8,0},{12,4},{16,8},{20,12},{24,16},{28,20},{32,24},... | collective-permute-start | bytes 294920 | tf_op jit(solution)/shard_map/ppermute | solution.py:38
  91.3 3.7 %collective-permute-done.16.refs_7_ = f32[8,512]{1,0:T(8,128)S(1)} collective-permute-done((f32[8,512]{1,0:T(8,128)S(1)}, f32[8,512]{1,0:T(8,128)S(1)}, u32[]{:S(2)}, u32[]{:S(2)}) %collective-permute-start.16) | collective-permute-done | bytes 16416 | tf_op jit(solution)/shard_map/ppermute | solution.py:323
  95.0 9.3 %shard_map.90 = (f32[64,512]{1,0:T(8,128)S(1)}, f32[5,8,1024]{2,1,0:T(8,128)S(1)}, f32[5,8,1024]{2,1,0:T(8,128)S(1)}, f32[5,8,1024]{2,1,0:T(8,128)S(1)}, f32[3,8...) custom-call(f32[64,512]{1,0:T(8,128)S(1)} %get-tuple-element.47.refs_0_.refs_12_.re, ...), custom_call_target="tpu_custom_call" | custom-call | tf_op jit(solution)/shard_map/pallas_call | solution.py:356
  106.9 4.7 %collective-permute-start.19 = (f32[3,8,1024]{2,1,0:T(8,128)S(1)}, f32[3,8,1024]{2,1,0:T(8,128)S(1)}, u32[]{:S(2)}, u32[]{:S(2)}) collective-permute-start(f32[3,8,1024]{2,1,0:T(8,128)S(1)} %get-tuple-element.62), channel_id=1, source_target_pairs={{0,56},{4,60},{8,0},{12,4},{16,8},{20,12},{24,16},{28,20},{32,24},... | collective-permute-start | bytes 294920 | tf_op jit(solution)/shard_map/ppermute | solution.py:38
  119.2 3.6 %collective-permute-done.22.refs_7_ = f32[8,512]{1,0:T(8,128)S(1)} collective-permute-done((f32[8,512]{1,0:T(8,128)S(1)}, f32[8,512]{1,0:T(8,128)S(1)}, u32[]{:S(2)}, u32[]{:S(2)}) %collective-permute-start.22) | collective-permute-done | bytes 16416 | tf_op jit(solution)/shard_map/ppermute | solution.py:323
  122.8 9.3 %shard_map.91 = (f32[64,512]{1,0:T(8,128)S(1)}, f32[5,8,1024]{2,1,0:T(8,128)S(1)}, f32[5,8,1024]{2,1,0:T(8,128)S(1)}, f32[5,8,1024]{2,1,0:T(8,128)S(1)}, f32[3,8...) custom-call(f32[64,512]{1,0:T(8,128)S(1)} %get-tuple-element.58.refs_0_.refs_13_.re, ...), custom_call_target="tpu_custom_call" | custom-call | tf_op jit(solution)/shard_map/pallas_call | solution.py:356
  134.1 5.2 %collective-permute-start.25 = (f32[3,8,1024]{2,1,0:T(8,128)S(1)}, f32[3,8,1024]{2,1,0:T(8,128)S(1)}, u32[]{:S(2)}, u32[]{:S(2)}) collective-permute-start(f32[3,8,1024]{2,1,0:T(8,128)S(1)} %get-tuple-element.70), channel_id=1, source_target_pairs={{0,56},{4,60},{8,0},{12,4},{16,8},{20,12},{24,16},{28,20},{32,24},... | collective-permute-start | bytes 294920 | tf_op jit(solution)/shard_map/ppermute | solution.py:38
  146.8 3.4 %collective-permute-done.28.refs_7_ = f32[8,512]{1,0:T(8,128)S(1)} collective-permute-done((f32[8,512]{1,0:T(8,128)S(1)}, f32[8,512]{1,0:T(8,128)S(1)}, u32[]{:S(2)}, u32[]{:S(2)}) %collective-permute-start.28) | collective-permute-done | bytes 16416 | tf_op jit(solution)/shard_map/ppermute | solution.py:323
  150.2 9.3 %shard_map.92 = (f32[64,512]{1,0:T(8,128)S(1)}, f32[5,8,1024]{2,1,0:T(8,128)S(1)}, f32[5,8,1024]{2,1,0:T(8,128)S(1)}, f32[5,8,1024]{2,1,0:T(8,128)S(1)}, f32[3,8...) custom-call(f32[64,512]{1,0:T(8,128)S(1)} %get-tuple-element.66.refs_0_.refs_14_.re, ...), custom_call_target="tpu_custom_call" | custom-call | tf_op jit(solution)/shard_map/pallas_call | solution.py:356
  162.3 4.8 %collective-permute-start.31 = (f32[3,8,1024]{2,1,0:T(8,128)S(1)}, f32[3,8,1024]{2,1,0:T(8,128)S(1)}, u32[]{:S(2)}, u32[]{:S(2)}) collective-permute-start(f32[3,8,1024]{2,1,0:T(8,128)S(1)} %get-tuple-element.78), channel_id=1, source_target_pairs={{0,56},{4,60},{8,0},{12,4},{16,8},{20,12},{24,16},{28,20},{32,24},... | collective-permute-start | bytes 294920 | tf_op jit(solution)/shard_map/ppermute | solution.py:38
  169.1 3.6 %collective-permute-start.33 = (f32[8,512]{1,0:T(8,128)S(1)}, f32[8,512]{1,0:T(8,128)S(1)}, u32[]{:S(2)}, u32[]{:S(2)}) collective-permute-start(f32[8,512]{1,0:T(8,128)S(1)} %get-tuple-element.80), channel_id=1, source_target_pairs={{0,1},{1,2},{2,3},{4,5},{5,6},{6,7},{8,9},{9,10},{10,11},{12,13},{... | collective-permute-start | bytes 49160 | tf_op jit(solution)/shard_map/ppermute | solution.py:322
  174.8 3.4 %collective-permute-done.34.refs_7_ = f32[8,512]{1,0:T(8,128)S(1)} collective-permute-done((f32[8,512]{1,0:T(8,128)S(1)}, f32[8,512]{1,0:T(8,128)S(1)}, u32[]{:S(2)}, u32[]{:S(2)}) %collective-permute-start.34) | collective-permute-done | bytes 16416 | tf_op jit(solution)/shard_map/ppermute | solution.py:323
  178.3 7.9 %shard_map.93 = (f32[64,512]{1,0:T(8,128)S(1)}, f32[16,128]{1,0:T(8,128)S(1)}) custom-call(f32[64,512]{1,0:T(8,128)S(1)} %get-tuple-element.74.refs_0_.refs_4_, f32[5,8,1024]{2,1,0:T(8,128)S(1)} %get-tuple-element.75.refs_1_, f32[5,8,1024]{2,1,0:T(8,128)S(1)} %collective-permute-done.29.refs_2_, f32[5,8,1024]{2,1,0:T(8,128)S(1)} %collective-permute-done.30.refs_3_, ...), custom_call_target="tpu_custom_call" | custom-call | tf_op jit(solution)/shard_map/pallas_call | solution.py:358
  186.2 3.5 %collective-permute-start.37 = (f32[16,128]{1,0:T(8,128)S(1)}, f32[16,128]{1,0:T(8,128)S(1)}, u32[]{:S(2)}, u32[]{:S(2)}) collective-permute-start(f32[16,128]{1,0:T(8,128)S(1)} %get-tuple-element.82), channel_id=1, source_target_pairs={{0,3},{1,0},{2,1},{3,2},{4,7},{5,4},{6,5},{7,6},{8,11},{9,8},{10,9... | collective-permute-start | bytes 24584 | tf_op jit(solution)/shard_map/ppermute | solution.py:38
  189.7 3.6 %collective-permute-start.36 = (f32[16,128]{1,0:T(8,128)S(1)}, f32[16,128]{1,0:T(8,128)S(1)}, u32[]{:S(2)}, u32[]{:S(2)}) collective-permute-start(f32[16,128]{1,0:T(8,128)S(1)} %get-tuple-element.82), channel_id=1, source_target_pairs={{0,2},{1,3},{2,0},{3,1},{4,6},{5,7},{6,4},{7,5},{8,10},{9,11},{10,... | collective-permute-start | bytes 24584 | tf_op jit(solution)/shard_map/ppermute | solution.py:38
  199.2 7.5 %collective-permute-start.40 = (f32[16,128]{1,0:T(8,128)S(1)}, f32[16,128]{1,0:T(8,128)S(1)}, u32[]{:S(2)}, u32[]{:S(2)}) collective-permute-start(f32[16,128]{1,0:T(8,128)S(1)} %add_add_fusion.2), channel_id=1, source_target_pairs={{0,12},{4,16},{8,20},{12,24},{16,28},{20,32},{24,36},{28,40},{32,4... | collective-permute-start | bytes 24584 | tf_op jit(solution)/shard_map/ppermute | solution.py:38
  206.7 4.9 %collective-permute-start.39 = (f32[16,128]{1,0:T(8,128)S(1)}, f32[16,128]{1,0:T(8,128)S(1)}, u32[]{:S(2)}, u32[]{:S(2)}) collective-permute-start(f32[16,128]{1,0:T(8,128)S(1)} %add_add_fusion.2), channel_id=1, source_target_pairs={{0,8},{4,12},{8,16},{12,20},{16,24},{20,28},{24,32},{28,36},{32,40... | collective-permute-start | bytes 24584 | tf_op jit(solution)/shard_map/ppermute | solution.py:38
  215.7 5.7 %collective-permute-start.42 = (f32[16,128]{1,0:T(8,128)S(1)}, f32[16,128]{1,0:T(8,128)S(1)}, u32[]{:S(2)}, u32[]{:S(2)}) collective-permute-start(f32[16,128]{1,0:T(8,128)S(1)} %add_add_fusion.1), channel_id=1, source_target_pairs={{0,32},{4,36},{8,40},{12,44},{16,48},{20,52},{24,56},{28,60},{32,0... | collective-permute-start | bytes 24584 | tf_op jit(solution)/shard_map/ppermute | solution.py:38
  224.0 3.9 %collective-permute-done.41 = f32[16,128]{1,0:T(8,128)S(1)} collective-permute-done((f32[16,128]{1,0:T(8,128)S(1)}, f32[16,128]{1,0:T(8,128)S(1)}, u32[]{:S(2)}, u32[]{:S(2)}) %collective-permute-start.41) | collective-permute-done | bytes 8224 | tf_op jit(solution)/shard_map/ppermute | solution.py:38
  (87 shorter events, 79.2 us)
Async XLA Ops:
  7.0 24.8 %collective-permute-start.6 = (f32[168,128]{1,0:T(8,128)S(1)}, f32[168,128]{1,0:T(8,128)S(1)}, u32[]{:S(2)}, u32[]{:S(2)}) collective-permute-start(f32[168,128]{1,0:T(8,128)S(1)} %get-tuple-element.44.refs_0_), channel_id=1, source_target_pairs={{0,448},{64,0},{128,64},{192,128},{256,192},{320,256},{384,320},{4... | collective-permute-start | bytes 258056 | tf_op jit(solution)/shard_map/ppermute | solution.py:38
  18.5 16.4 %collective-permute-start.5 = (f32[168,128]{1,0:T(8,128)S(1)}, f32[168,128]{1,0:T(8,128)S(1)}, u32[]{:S(2)}, u32[]{:S(2)}) collective-permute-start(f32[168,128]{1,0:T(8,128)S(1)} %get-tuple-element.44.refs_0_), channel_id=1, source_target_pairs={{0,384},{64,448},{128,0},{192,64},{256,128},{320,192},{384,256},{4... | collective-permute-start | bytes 258056 | tf_op jit(solution)/shard_map/ppermute | solution.py:38
  20.6 17.6 %collective-permute-start.4 = (f32[168,128]{1,0:T(8,128)S(1)}, f32[168,128]{1,0:T(8,128)S(1)}, u32[]{:S(2)}, u32[]{:S(2)}) collective-permute-start(f32[168,128]{1,0:T(8,128)S(1)} %get-tuple-element.44.refs_0_), channel_id=1, source_target_pairs={{0,320},{64,384},{128,448},{192,0},{256,64},{320,128},{384,192},{4... | collective-permute-start | bytes 258056 | tf_op jit(solution)/shard_map/ppermute | solution.py:38
  22.6 15.7 %collective-permute-start.3 = (f32[168,128]{1,0:T(8,128)S(1)}, f32[168,128]{1,0:T(8,128)S(1)}, u32[]{:S(2)}, u32[]{:S(2)}) collective-permute-start(f32[168,128]{1,0:T(8,128)S(1)} %get-tuple-element.44.refs_0_), channel_id=1, source_target_pairs={{0,256},{64,320},{128,384},{192,448},{256,0},{320,64},{384,128},{4... | collective-permute-start | bytes 258056 | tf_op jit(solution)/shard_map/ppermute | solution.py:38
  31.8 12.1 %collective-permute-start.1 = (f32[168,128]{1,0:T(8,128)S(1)}, f32[168,128]{1,0:T(8,128)S(1)}, u32[]{:S(2)}, u32[]{:S(2)}) collective-permute-start(f32[168,128]{1,0:T(8,128)S(1)} %get-tuple-element.44.refs_0_), channel_id=1, source_target_pairs={{0,128},{64,192},{128,256},{192,320},{256,384},{320,448},{384,0},{... | collective-permute-start | bytes 258056 | tf_op jit(solution)/shard_map/ppermute | solution.py:38
  45.9 23.4 %collective-permute-start.10 = (f32[8,1024]{1,0:T(8,128)S(1)}, f32[8,1024]{1,0:T(8,128)S(1)}, u32[]{:S(2)}, u32[]{:S(2)}) collective-permute-start(f32[8,1024]{1,0:T(8,128)S(1)} %shard_map.87.z2), channel_id=1, source_target_pairs={{0,8},{4,12},{8,16},{12,20},{16,24},{20,28},{24,32},{28,36},{32,40... | collective-permute-start | bytes 98312 | tf_op jit(solution)/shard_map/ppermute | solution.py:38
  48.9 20.5 %collective-permute-start.9 = (f32[8,1024]{1,0:T(8,128)S(1)}, f32[8,1024]{1,0:T(8,128)S(1)}, u32[]{:S(2)}, u32[]{:S(2)}) collective-permute-start(f32[8,1024]{1,0:T(8,128)S(1)} %shard_map.87.z2), channel_id=1, source_target_pairs={{0,4},{4,8},{8,12},{12,16},{16,20},{20,24},{24,28},{28,32},{32,36}... | collective-permute-start | bytes 98312 | tf_op jit(solution)/shard_map/ppermute | solution.py:38
  51.8 17.5 %collective-permute-start.8 = (f32[8,1024]{1,0:T(8,128)S(1)}, f32[8,1024]{1,0:T(8,128)S(1)}, u32[]{:S(2)}, u32[]{:S(2)}) collective-permute-start(f32[8,1024]{1,0:T(8,128)S(1)} %shard_map.87.z2), channel_id=1, source_target_pairs={{0,60},{4,0},{8,4},{12,8},{16,12},{20,16},{24,20},{28,24},{32,28},... | collective-permute-start | bytes 98312 | tf_op jit(solution)/shard_map/ppermute | solution.py:38
  51.9 17.5 %collective-permute-start.7 = (f32[8,1024]{1,0:T(8,128)S(1)}, f32[8,1024]{1,0:T(8,128)S(1)}, u32[]{:S(2)}, u32[]{:S(2)}) collective-permute-start(f32[8,1024]{1,0:T(8,128)S(1)} %shard_map.87.z2), channel_id=1, source_target_pairs={{0,56},{4,60},{8,0},{12,4},{16,8},{20,12},{24,16},{28,20},{32,24},... | collective-permute-start | bytes 98312 | tf_op jit(solution)/shard_map/ppermute | solution.py:38
  78.4 16.6 %collective-permute-start.11 = (f32[5,8,1024]{2,1,0:T(8,128)S(1)}, f32[5,8,1024]{2,1,0:T(8,128)S(1)}, u32[]{:S(2)}, u32[]{:S(2)}) collective-permute-start(f32[5,8,1024]{2,1,0:T(8,128)S(1)} %get-tuple-element.49), channel_id=1, source_target_pairs={{0,60},{4,0},{8,4},{12,8},{16,12},{20,16},{24,20},{28,24},{32,28},... | collective-permute-start | bytes 491528 | tf_op jit(solution)/shard_map/ppermute | solution.py:38
  79.5 15.5 %collective-permute-start.12 = (f32[5,8,1024]{2,1,0:T(8,128)S(1)}, f32[5,8,1024]{2,1,0:T(8,128)S(1)}, u32[]{:S(2)}, u32[]{:S(2)}) collective-permute-start(f32[5,8,1024]{2,1,0:T(8,128)S(1)} %get-tuple-element.50), channel_id=1, source_target_pairs={{0,4},{4,8},{8,12},{12,16},{16,20},{20,24},{24,28},{28,32},{32,36}... | collective-permute-start | bytes 491528 | tf_op jit(solution)/shard_map/ppermute | solution.py:38
  80.4 14.6 %collective-permute-start.13 = (f32[3,8,1024]{2,1,0:T(8,128)S(1)}, f32[3,8,1024]{2,1,0:T(8,128)S(1)}, u32[]{:S(2)}, u32[]{:S(2)}) collective-permute-start(f32[3,8,1024]{2,1,0:T(8,128)S(1)} %get-tuple-element.51), channel_id=1, source_target_pairs={{0,56},{4,60},{8,0},{12,4},{16,8},{20,12},{24,16},{28,20},{32,24},... | collective-permute-start | bytes 294920 | tf_op jit(solution)/shard_map/ppermute | solution.py:38
  104.3 18.4 %collective-permute-start.17 = (f32[5,8,1024]{2,1,0:T(8,128)S(1)}, f32[5,8,1024]{2,1,0:T(8,128)S(1)}, u32[]{:S(2)}, u32[]{:S(2)}) collective-permute-start(f32[5,8,1024]{2,1,0:T(8,128)S(1)} %get-tuple-element.60), channel_id=1, source_target_pairs={{0,60},{4,0},{8,4},{12,8},{16,12},{20,16},{24,20},{28,24},{32,28},... | collective-permute-start | bytes 491528 | tf_op jit(solution)/shard_map/ppermute | solution.py:38
  105.9 16.9 %collective-permute-start.18 = (f32[5,8,1024]{2,1,0:T(8,128)S(1)}, f32[5,8,1024]{2,1,0:T(8,128)S(1)}, u32[]{:S(2)}, u32[]{:S(2)}) collective-permute-start(f32[5,8,1024]{2,1,0:T(8,128)S(1)} %get-tuple-element.61), channel_id=1, source_target_pairs={{0,4},{4,8},{8,12},{12,16},{16,20},{20,24},{24,28},{28,32},{32,36}... | collective-permute-start | bytes 491528 | tf_op jit(solution)/shard_map/ppermute | solution.py:38
  106.9 15.9 %collective-permute-start.19 = (f32[3,8,1024]{2,1,0:T(8,128)S(1)}, f32[3,8,1024]{2,1,0:T(8,128)S(1)}, u32[]{:S(2)}, u32[]{:S(2)}) collective-permute-start(f32[3,8,1024]{2,1,0:T(8,128)S(1)} %get-tuple-element.62), channel_id=1, source_target_pairs={{0,56},{4,60},{8,0},{12,4},{16,8},{20,12},{24,16},{28,20},{32,24},... | collective-permute-start | bytes 294920 | tf_op jit(solution)/shard_map/ppermute | solution.py:38
  111.6 11.2 %collective-permute-start.20 = (f32[3,8,1024]{2,1,0:T(8,128)S(1)}, f32[3,8,1024]{2,1,0:T(8,128)S(1)}, u32[]{:S(2)}, u32[]{:S(2)}) collective-permute-start(f32[3,8,1024]{2,1,0:T(8,128)S(1)} %get-tuple-element.63), channel_id=1, source_target_pairs={{0,8},{4,12},{8,16},{12,20},{16,24},{20,28},{24,32},{28,36},{32,40... | collective-permute-start | bytes 294920 | tf_op jit(solution)/shard_map/ppermute | solution.py:38
  132.1 18.1 %collective-permute-start.23 = (f32[5,8,1024]{2,1,0:T(8,128)S(1)}, f32[5,8,1024]{2,1,0:T(8,128)S(1)}, u32[]{:S(2)}, u32[]{:S(2)}) collective-permute-start(f32[5,8,1024]{2,1,0:T(8,128)S(1)} %get-tuple-element.68), channel_id=1, source_target_pairs={{0,60},{4,0},{8,4},{12,8},{16,12},{20,16},{24,20},{28,24},{32,28},... | collective-permute-start | bytes 491528 | tf_op jit(solution)/shard_map/ppermute | solution.py:38
  134.1 16.1 %collective-permute-start.24 = (f32[5,8,1024]{2,1,0:T(8,128)S(1)}, f32[5,8,1024]{2,1,0:T(8,128)S(1)}, u32[]{:S(2)}, u32[]{:S(2)}) collective-permute-start(f32[5,8,1024]{2,1,0:T(8,128)S(1)} %get-tuple-element.69), channel_id=1, source_target_pairs={{0,4},{4,8},{8,12},{12,16},{16,20},{20,24},{24,28},{28,32},{32,36}... | collective-permute-start | bytes 491528 | tf_op jit(solution)/shard_map/ppermute | solution.py:38
  134.1 16.1 %collective-permute-start.25 = (f32[3,8,1024]{2,1,0:T(8,128)S(1)}, f32[3,8,1024]{2,1,0:T(8,128)S(1)}, u32[]{:S(2)}, u32[]{:S(2)}) collective-permute-start(f32[3,8,1024]{2,1,0:T(8,128)S(1)} %get-tuple-element.70), channel_id=1, source_target_pairs={{0,56},{4,60},{8,0},{12,4},{16,8},{20,12},{24,16},{28,20},{32,24},... | collective-permute-start | bytes 294920 | tf_op jit(solution)/shard_map/ppermute | solution.py:38
  159.5 18.8 %collective-permute-start.29 = (f32[5,8,1024]{2,1,0:T(8,128)S(1)}, f32[5,8,1024]{2,1,0:T(8,128)S(1)}, u32[]{:S(2)}, u32[]{:S(2)}) collective-permute-start(f32[5,8,1024]{2,1,0:T(8,128)S(1)} %get-tuple-element.76), channel_id=1, source_target_pairs={{0,60},{4,0},{8,4},{12,8},{16,12},{20,16},{24,20},{28,24},{32,28},... | collective-permute-start | bytes 491528 | tf_op jit(solution)/shard_map/ppermute | solution.py:38
  162.3 16.0 %collective-permute-start.30 = (f32[5,8,1024]{2,1,0:T(8,128)S(1)}, f32[5,8,1024]{2,1,0:T(8,128)S(1)}, u32[]{:S(2)}, u32[]{:S(2)}) collective-permute-start(f32[5,8,1024]{2,1,0:T(8,128)S(1)} %get-tuple-element.77), channel_id=1, source_target_pairs={{0,4},{4,8},{8,12},{12,16},{16,20},{20,24},{24,28},{28,32},{32,36}... | collective-permute-start | bytes 491528 | tf_op jit(solution)/shard_map/ppermute | solution.py:38
  162.3 16.0 %collective-permute-start.31 = (f32[3,8,1024]{2,1,0:T(8,128)S(1)}, f32[3,8,1024]{2,1,0:T(8,128)S(1)}, u32[]{:S(2)}, u32[]{:S(2)}) collective-permute-start(f32[3,8,1024]{2,1,0:T(8,128)S(1)} %get-tuple-element.78), channel_id=1, source_target_pairs={{0,56},{4,60},{8,0},{12,4},{16,8},{20,12},{24,16},{28,20},{32,24},... | collective-permute-start | bytes 294920 | tf_op jit(solution)/shard_map/ppermute | solution.py:38
  167.1 11.2 %collective-permute-start.32 = (f32[3,8,1024]{2,1,0:T(8,128)S(1)}, f32[3,8,1024]{2,1,0:T(8,128)S(1)}, u32[]{:S(2)}, u32[]{:S(2)}) collective-permute-start(f32[3,8,1024]{2,1,0:T(8,128)S(1)} %get-tuple-element.79), channel_id=1, source_target_pairs={{0,8},{4,12},{8,16},{12,20},{16,24},{20,28},{24,32},{28,36},{32,40... | collective-permute-start | bytes 294920 | tf_op jit(solution)/shard_map/ppermute | solution.py:38
  199.2 12.4 %collective-permute-start.40 = (f32[16,128]{1,0:T(8,128)S(1)}, f32[16,128]{1,0:T(8,128)S(1)}, u32[]{:S(2)}, u32[]{:S(2)}) collective-permute-start(f32[16,128]{1,0:T(8,128)S(1)} %add_add_fusion.2), channel_id=1, source_target_pairs={{0,12},{4,16},{8,20},{12,24},{16,28},{20,32},{24,36},{28,40},{32,4... | collective-permute-start | bytes 24584 | tf_op jit(solution)/shard_map/ppermute | solution.py:38
  (24 other events, 134.2 us)

commit v2 on v1

v2 whole, which is shorter than its diff:
```python
import jax
import jax.numpy as jnp
from jax import lax
from jax.experimental import pallas as pl
from jax.experimental.pallas import tpu as pltpu
from jax.sharding import PartitionSpec as P

S = 7
CLON = 4
CLAT = 8
LEV = 128
NT = 3
TILE = 16
ITERS = 4
SPAN = 5
ORB = 8
RAYS = 128
SLOT = ORB * RAYS
CELL = CLON * LEV
CHAN = 64
SHARD = SPAN * 2 * TILE + 8
F32 = jnp.float32
BF16 = jnp.bfloat16
highest = lax.Precision.HIGHEST
VMEM = pltpu.VMEM
LIMIT = pltpu.CompilerParams(vmem_limit_bytes=24 << 20)


def vspec():
    return pl.BlockSpec(memory_space=pltpu.VMEM)


def sspec():
    return pl.BlockSpec(memory_space=pltpu.SMEM)


def shift(block, axis, distance):
    size = lax.axis_size(axis)
    return lax.ppermute(block, axis, [(i, (i + distance) % size) for i in range(size)])


def split(values):
    high = values.astype(BF16)
    low = (values - high.astype(F32)).astype(BF16)
    return high, low


def start_kernel(*refs):
    sources, outs, places, sem = refs[:7], refs[7:11], refs[11:18], refs[18]
    copies = [pltpu.make_async_copy(src, dst, sem.at[n]) for n, (src, dst) in enumerate(zip(sources, places))]
    for copy in copies:
        copy.start()
    for copy in copies:
        copy.wait()
    prior_ref, obs_ref, start_ref, cells_ref, lengths_ref, kern_ref, noise_ref = places
    shard_ref, gram_ref, prior_out, scale_out = outs
    for slot in range(SPAN):
        lanes = slice(slot * RAYS, (slot + 1) * RAYS)
        base = slot * 2 * TILE
        shard_ref[base:base + TILE, :] = cells_ref[:, lanes].astype(F32)
        shard_ref[base + TILE:base + 2 * TILE, :] = lengths_ref[:, lanes]
    sub = lax.broadcasted_iota(jnp.int32, (8, CHAN), 0)
    kern = jnp.zeros((8, CHAN), F32)
    for s in range(S):
        kern = jnp.where(sub == s, kern_ref[s:s + 1, :], kern)
    weighted = kern * noise_ref[...]
    source = jnp.dot(weighted, obs_ref[...], precision=highest, preferred_element_type=F32)
    base = SPAN * 2 * TILE
    sub = lax.broadcasted_iota(jnp.int32, (8, RAYS), 0)
    start = jnp.broadcast_to(start_ref[...].astype(F32), (8, RAYS))
    shard_ref[base:base + 8, :] = jnp.where(sub == S, start, source)
    wide = jnp.concatenate([kern] * CLAT, axis=0)
    wide_weighted = jnp.concatenate([weighted] * CLAT, axis=0)
    gram = lax.dot_general(wide_weighted, wide, (((1,), (1,)), ((), ())), precision=highest, preferred_element_type=F32)
    row = lax.broadcasted_iota(jnp.int32, gram.shape, 0)
    col = lax.broadcasted_iota(jnp.int32, gram.shape, 1)
    trace = jnp.sum(jnp.where((row == col) & (row < 8), gram, 0.0))
    top = prior_ref[0]
    for s in range(1, S):
        top = jnp.maximum(top, prior_ref[s])
    bound = jnp.full((8, 128), trace * 128.0 + 12.0 * top, F32)
    scale = 1.0 / bound
    scale_out[...] = scale
    gram_ref[...] = jnp.where((row >> 3) == (col >> 3), gram, 0.0) * scale[0:1, 0:1]
    species = lax.broadcasted_iota(jnp.int32, (CLAT * 8, 128), 0) & 7
    prior = jnp.zeros((CLAT * 8, 128), F32)
    for s in range(S):
        prior = jnp.where(species == s, prior_ref[s], prior)
    prior_out[...] = prior * scale[0:1, 0:1]


def gather_kernel(shards, out):
    base = SPAN * 2 * TILE
    for k in range(ORB):
        out[:, k * RAYS:(k + 1) * RAYS] = shards[k, base:base + 8, :]


def build_kernel(shards, w_ref, lat_ref):
    sub = lax.broadcasted_iota(jnp.int32, (8, RAYS), 0)
    odd = (sub & 1) == 1

    def slot_body(index, carry):
        slot, k = index >> 3, index & 7
        spot = pl.multiple_of(k * RAYS, RAYS)
        base = pl.multiple_of(slot * 2 * TILE, 2 * TILE)
        cells = shards[k, pl.ds(base, TILE), :].astype(jnp.int32)
        lengths = shards[k, pl.ds(base + TILE, TILE), :]
        lat_ref[slot, :, pl.ds(spot, RAYS)] = jnp.broadcast_to((cells[0:1, :] >> 7) & 7, (8, RAYS))
        places = ((cells >> 10) << 7) | (cells & 127)
        first = jnp.broadcast_to(cells[0:1, :] & 1, (8, RAYS)) == 1
        swap = first != odd
        keys = []
        sizes = []
        for j in range(TILE // 2):
            even_key = jnp.broadcast_to(places[2 * j:2 * j + 1, :], (8, RAYS))
            odd_key = jnp.broadcast_to(places[2 * j + 1:2 * j + 2, :], (8, RAYS))
            keys.append(jnp.where(swap, odd_key, even_key) - sub)
            even_len = jnp.broadcast_to(lengths[2 * j:2 * j + 1, :], (8, RAYS))
            odd_len = jnp.broadcast_to(lengths[2 * j + 1:2 * j + 2, :], (8, RAYS))
            sizes.append(jnp.where(swap, odd_len, even_len))
        for i in range(TILE // 2):
            for j in range(i + 1, TILE // 2):
                same = keys[i] == keys[j]
                sizes[i] = sizes[i] + jnp.where(same, sizes[j], 0.0)
                keys[j] = jnp.where(same, -64, keys[j])
        for pair in range(CELL // 16):
            parts = []
            for half in range(2):
                offset = pair * 16 + half * 8
                total = jnp.zeros((8, RAYS), F32)
                for key, size in zip(keys, sizes):
                    total = jnp.where(key == offset, size, total)
                parts.append(total)
            high, low = split(jnp.concatenate(parts, axis=0))
            w_ref[slot, pl.ds(pair * 16, 16), pl.ds(spot, RAYS)] = high
            w_ref[slot, pl.ds(CELL + pair * 16, 16), pl.ds(spot, RAYS)] = low
        return carry

    lax.fori_loop(0, SPAN * ORB, slot_body, 0)


def masked_rows(values, lat):
    rows = jnp.concatenate([jnp.where(lat == l, values, 0.0) for l in range(CLAT)], axis=0)
    return jnp.concatenate(split(rows), axis=0)


def back_all(sums, lats, w_ref):
    total = None
    for slot in range(SPAN):
        part = lax.dot_general(
            masked_rows(sums[slot], lats[slot]), w_ref[slot], (((1,), (1,)), ((), ())), preferred_element_type=F32
        )
        total = part if total is None else total + part
    total = total[:, :CELL] + total[:, CELL:]
    return total[:64] + total[64:]


def project_kernel(v_ref, mask_ref, w_ref, own_ref, left_ref, right_ref, left2_ref, right2_ref):
    v = v_ref[...]
    for l in range(CLAT):
        left_ref[4, :, pl.ds(l * LEV, LEV)] = v[8 * l:8 * l + 8, 0:LEV]
        right_ref[4, :, pl.ds(l * LEV, LEV)] = v[8 * l:8 * l + 8, CELL - LEV:]
    halves = jnp.concatenate(split(v), axis=0)
    rows = jnp.concatenate([halves, halves], axis=1)
    for slot in range(SPAN):
        wide = jnp.dot(rows, w_ref[slot], preferred_element_type=F32)
        wide = wide[:64] + wide[64:]
        lat = mask_ref[slot]
        total = jnp.where(lat == 0, wide[0:8], 0.0)
        for l in range(1, CLAT):
            total = total + jnp.where(lat == l, wide[8 * l:8 * l + 8], 0.0)
        own_ref[slot] = total
        if slot >= 1:
            left_ref[slot - 1] = total
        if slot <= 3:
            right_ref[slot] = total
        if slot >= 2:
            left2_ref[slot - 2] = total
        if slot <= 2:
            right2_ref[slot] = total


def init_kernel(z2, z0, z1, z3, z4, lat_ref, w_ref, v_ref, mask_ref, middle_ref, down_ref, up_ref):
    sums, lats = [], []
    sub = lax.broadcasted_iota(jnp.int32, (8, SLOT), 0)
    for slot, z in enumerate((z0, z1, z2, z3, z4)):
        begin = jnp.broadcast_to(z[S:S + 1, :], (8, SLOT))
        present = (begin <= slot) & (begin + (NT - 1) >= slot)
        lat = jnp.where(present, lat_ref[slot], -1)
        mask_ref[slot] = lat
        middle_ref[slot] = jnp.where(begin + 1.0 == slot, 1.0, 0.0)
        lats.append(lat)
        sums.append(jnp.where(sub < S, z[...], 0.0))
    v = back_all(sums, lats, w_ref)
    v_ref[...] = v
    down_ref[...] = v[0:8]
    up_ref[...] = v[56:64]


def ray_sums(own_ref, plus1, minus1, plus2, minus2):
    sums = []
    for slot in range(SPAN):
        total = own_ref[slot]
        if slot <= 3:
            total = total + plus1[slot]
        if slot >= 1:
            total = total + minus1[slot - 1]
        if slot <= 2:
            total = total + plus2[slot]
        if slot >= 2:
            total = total + minus2[slot - 2]
        sums.append(total)
    return sums


def prior_image(v, plus1, minus1, south, north, prior_ref):
    west = jnp.concatenate([minus1[4, :, l * LEV:(l + 1) * LEV] for l in range(CLAT)], axis=0)
    east = jnp.concatenate([plus1[4, :, l * LEV:(l + 1) * LEV] for l in range(CLAT)], axis=0)
    cols = [west] + [v[:, c * LEV:(c + 1) * LEV] for c in range(CLON)] + [east]
    lane = lax.broadcasted_iota(jnp.int32, (64, LEV), 1)
    pieces = []
    for c in range(CLON):
        here = cols[c + 1]
        below = jnp.where(lane == 0, 0.0, pltpu.roll(here, 1, 1))
        above = jnp.where(lane == LEV - 1, 0.0, pltpu.roll(here, LEV - 1, 1))
        south_side = jnp.concatenate([south[:, c * LEV:(c + 1) * LEV], here[:56]], axis=0)
        north_side = jnp.concatenate([here[8:], north[:, c * LEV:(c + 1) * LEV]], axis=0)
        near = cols[c] + cols[c + 2] + below + above + south_side + north_side
        pieces.append(prior_ref[...] * (6.0 * here - near))
    return jnp.concatenate(pieces, axis=1)


def back_image(sums, mask_ref, w_ref, gram_ref):
    image = back_all(sums, [mask_ref[slot] for slot in range(SPAN)], w_ref)
    return jnp.dot(gram_ref[...], image, precision=highest, preferred_element_type=F32)


def back_kernel(v_ref, own_ref, plus1, minus1, plus2, minus2, south, north, mask_ref, w_ref, gram_ref, prior_ref, out_ref, down_ref, up_ref):
    sums = ray_sums(own_ref, plus1, minus1, plus2, minus2)
    v = back_image(sums, mask_ref, w_ref, gram_ref) + prior_image(v_ref[...], plus1, minus1, south, north, prior_ref)
    out_ref[...] = v
    down_ref[...] = v[0:8]
    up_ref[...] = v[56:64]


PAIRS = [(i, j) for i in range(ITERS) for j in range(i, ITERS)] + [(ITERS - 1, ITERS)]


def fold_rows(product):
    product = jnp.sum(product, axis=0, keepdims=True)
    fold = product[:, 0:LEV]
    for c in range(1, product.shape[1] // LEV):
        fold = fold + product[:, c * LEV:(c + 1) * LEV]
    return fold


def sums_kernel(v0, v1, v2, v3, own_ref, plus1, minus1, plus2, minus2, south, north, middle_ref, gram_ref, prior_ref, pair_ref, rays_ref, image_ref):
    sums = ray_sums(own_ref, plus1, minus1, plus2, minus2)
    vectors = [v0[...], v1[...], v2[...], v3[...]]
    image = prior_image(vectors[-1], plus1, minus1, south, north, prior_ref)
    image_ref[...] = image
    last = fold_rows(vectors[-1] * image)
    gram = gram_ref[0:8, 0:8]
    for slot in range(SPAN):
        rays_ref[slot] = sums[slot]
        mixed = jnp.dot(gram, sums[slot], precision=highest, preferred_element_type=F32)
        last = last + fold_rows(sums[slot] * mixed * middle_ref[slot])
    folds = [fold_rows(vectors[i] * vectors[j]) for i, j in PAIRS[:-1]] + [last]
    folds.append(jnp.zeros_like(last))
    folds = [fold + pltpu.roll(fold, LEV // 2, 1) for fold in folds]
    lane = lax.broadcasted_iota(jnp.int32, (1, LEV), 1)
    packed = [jnp.where(lane < LEV // 2, folds[2 * n], folds[2 * n + 1]) for n in range(len(folds) // 2)]
    sub = lax.broadcasted_iota(jnp.int32, (8, LEV), 0)
    block = jnp.zeros((8, LEV), F32)
    for n, row in enumerate(packed):
        block = jnp.where(sub == n, row, block)
    for n in range(pair_ref.shape[0] // 8):
        pair_ref[pl.ds(8 * n, 8), :] = block


def last_kernel(rays_ref, image_ref, mask_ref, w_ref, gram_ref, out_ref):
    sums = [rays_ref[slot] for slot in range(SPAN)]
    out_ref[...] = back_image(sums, mask_ref, w_ref, gram_ref) + image_ref[...]


def combine_kernel(scale_ref, *refs):
    sums_ref, vector_refs, (x_ref, r_ref, spread) = refs[0], refs[1:ITERS + 2], refs[ITERS + 2:]
    parts = [sums_ref[pl.ds(8 * n, 8), :] for n in range(sums_ref.shape[0] // 8)]
    while len(parts) > 1:
        parts = [a + b for a, b in zip(parts[::2], parts[1::2])]
    lane = lax.broadcasted_iota(jnp.int32, (8, LEV), 1)
    lower = jnp.sum(jnp.where(lane < LEV // 2, parts[0], 0.0), axis=1, keepdims=True)
    upper = jnp.sum(jnp.where(lane < LEV // 2, 0.0, parts[0]), axis=1, keepdims=True)
    table = {}
    for n, (i, j) in enumerate(PAIRS):
        half = upper if n & 1 else lower
        table[i, j] = table[j, i] = half[n >> 1:(n >> 1) + 1, :]
    for i in range(ITERS - 1):
        table[i, ITERS] = table[i + 1, ITERS - 1]
    scale = scale_ref[0:1, 0:1]
    zero, one = jnp.zeros((1, 1), F32), jnp.ones((1, 1), F32)
    x = [zero] * (ITERS + 1)
    r = [one] + [zero] * ITERS
    d = list(r)

    def form(a, b, na, nb, off):
        total = None
        for i in range(na):
            inner = None
            for j in range(nb):
                term = b[j] * table[i, j + off]
                inner = term if inner is None else inner + term
            term = a[i] * inner
            total = term if total is None else total + term
        return total

    norm = table[0, 0]
    for k in range(ITERS):
        alpha = norm / form(d, d, k + 1, k + 1, 1)
        for i in range(k + 1):
            x[i] = x[i] + alpha * d[i]
            r[i + 1] = r[i + 1] - alpha * d[i]
        if k < ITERS - 1:
            after = form(r, r, k + 2, k + 2, 0)
            ratio = after / norm
            d = [r[i] + ratio * d[i] for i in range(ITERS + 1)]
            norm = after
    x = [scale * value for value in x]
    for c in range(CLON):
        parts = [ref[:, c * LEV:(c + 1) * LEV] for ref in vector_refs]
        total = x[0] * parts[0]
        for i in range(1, ITERS):
            total = total + x[i] * parts[i]
        spread[0, c] = total
        total = r[0] * parts[0]
        for i in range(1, ITERS + 1):
            total = total + r[i] * parts[i]
        spread[1, c] = total
        for s in range(S):
            x_ref[s, c] = spread[0, c, pl.ds(s, CLAT, stride=8), :]
            r_ref[s, c] = spread[1, c, pl.ds(s, CLAT, stride=8), :]


def shape(*dims, dtype=F32):
    return jax.ShapeDtypeStruct(dims, dtype)


def call(kernel, outs, n_in, scalar=False, scratch=(), work=None):
    return pl.pallas_call(
        kernel,
        out_shape=outs,
        in_specs=([sspec()] if scalar else []) + [vspec()] * n_in,
        out_specs=[vspec()] * len(outs),
        scratch_shapes=scratch,
        compiler_params=LIMIT,
        cost_estimate=work,
    )


MATMUL = pl.CostEstimate(flops=2 * 128 * 2 * CELL * SPAN * SLOT, transcendentals=0, bytes_accessed=2 * 2 * CELL * SPAN * SLOT)
BUILD = pl.CostEstimate(flops=16 * TILE * CELL * SPAN * SLOT, transcendentals=0, bytes_accessed=4 * 2 * CELL * SPAN * SLOT)
MESSAGES = (shape(SPAN, 8, SLOT), shape(5, 8, SLOT), shape(5, 8, SLOT), shape(3, 8, SLOT), shape(3, 8, SLOT))
FACE = shape(8, CELL)
FIELD = shape(64, CELL)


def lat_faces(down, up):
    n_lat = lax.axis_size("lat")
    south = lax.ppermute(up, "lat", [(i, i + 1) for i in range(n_lat - 1)])
    north = lax.ppermute(down, "lat", [(i + 1, i) for i in range(n_lat - 1)])
    return south, north


def exchange(south, north, own, left, right, left2, right2):
    south, north, left, right, left2, right2 = lax.optimization_barrier((south, north, left, right, left2, right2))
    plus2 = shift(left2, "lon", -2)
    minus2 = shift(right2, "lon", 2)
    plus1 = shift(left, "lon", -1)
    minus1 = shift(right, "lon", 1)
    return own, plus1, minus1, plus2, minus2, south, north


def body(observed, ray_start, tile_cells, tile_lengths, channel_kernel, noise_weight, prior_weight):
    shard, gram, prior, scale = pl.pallas_call(
        start_kernel,
        out_shape=(shape(SHARD, RAYS), shape(64, 64), shape(64, LEV), shape(8, LEV)),
        in_specs=[pl.BlockSpec(memory_space=pltpu.HBM)] * 7,
        out_specs=[vspec()] * 4,
        scratch_shapes=[
            pltpu.SMEM((S,), F32),
            pltpu.VMEM((CHAN, RAYS), F32),
            pltpu.VMEM((1, RAYS), jnp.int32),
            pltpu.VMEM((TILE, SPAN * RAYS), jnp.int32),
            pltpu.VMEM((TILE, SPAN * RAYS), F32),
            pltpu.VMEM((S, CHAN), F32),
            pltpu.VMEM((1, CHAN), F32),
            pltpu.SemaphoreType.DMA((7,)),
        ],
        compiler_params=LIMIT,
    )(prior_weight, observed.T, ray_start.reshape(1, RAYS), tile_cells.T, tile_lengths.T, channel_kernel, noise_weight.reshape(1, -1))
    shards = lax.all_gather(shard, "orbit")
    (z,) = call(gather_kernel, (shape(8, SLOT),), 1)(shards)
    z1, z3 = shift(z, "lon", -1), shift(z, "lon", 1)
    z0, z4 = shift(z, "lon", -2), shift(z, "lon", 2)
    w, lat = call(build_kernel, (shape(SPAN, 2 * CELL, SLOT, dtype=BF16), shape(SPAN, 8, SLOT, dtype=jnp.int32)), 1, work=BUILD)(shards)
    mask_shape = shape(SPAN, 8, SLOT, dtype=jnp.int32)
    v, mask, middle, down, up = call(init_kernel, (FIELD, mask_shape, shape(SPAN, 8, SLOT), FACE, FACE), 7, work=MATMUL)(z, z0, z1, z3, z4, lat, w)
    south, north = lat_faces(down, up)
    vectors = [v]
    sent = call(project_kernel, MESSAGES, 3, work=MATMUL)(v, mask, w)
    for turn in range(ITERS - 1):
        received = exchange(south, north, *sent)
        v, down, up = call(back_kernel, (FIELD, FACE, FACE), 12, work=MATMUL)(v, *received, mask, w, gram, prior)
        south, north = lat_faces(down, up)
        vectors.append(v)
        sent = call(project_kernel, MESSAGES, 3, work=MATMUL)(v, mask, w)
    peers = lax.axis_size("lon") * lax.axis_size("lat")
    pairs, rays, image = call(sums_kernel, (shape(8 * peers, LEV), shape(SPAN, 8, SLOT), FIELD), 14)(
        *vectors, *exchange(south, north, *sent), middle, gram, prior
    )
    pairs = lax.all_to_all(pairs, ("lon", "lat"), 0, 0, tiled=True)
    (v,) = call(last_kernel, (FIELD,), 5, work=MATMUL)(rays, image, mask, w, gram)
    vectors.append(v)
    field = shape(S, CLON, CLAT, LEV)
    return tuple(call(combine_kernel, (field, field), ITERS + 3, False, [pltpu.VMEM((2, CLON, 64, LEV), F32)])(scale, pairs, *vectors))


def solution(mesh):
    return jax.shard_map(
        body,
        mesh=mesh,
        in_specs=(
            P(("orbit", "lon", "lat"), None),
            P(("orbit", "lon", "lat")),
            P(("orbit", "lon", "lat"), None),
            P(("orbit", "lon", "lat"), None),
            P(),
            P(),
            P(),
        ),
        out_specs=(P(None, "lon", "lat", None), P(None, "lon", "lat", None)),
        check_vma=False,
    )
```

time: 231 us -> 174 us (0.75)
  starting transfers between devices: 127 us -> 67.3 us
  blocking collectives: 0 us -> 27.5 us
  Pallas kernels: 60.9 us -> 36.6 us
  local copies, waits for them, and re-layouts: 5.38 us -> 8.93 us
  waiting for transfers between devices: 34.3 us -> 31.6 us
    ppermute x36 -> x20, starting transfers between devices: 108 us -> 46.8 us  [shift(): lax.ppermute(block, axis, [(i, (i + distance) % size) for i in range(size)])]
    all_gather x0 -> x1, blocking collectives: none -> 27.5 us  [body(): shards = lax.all_gather(shard, 'orbit')]
    pallas_call x7 -> x12, Pallas kernels: 45.8 us -> 27.2 us  [the longest x3 11.4 us: body(): call(back_kernel, (FIELD, FACE, FACE), 12, work=MATMUL)]
    ppermute x8, waiting for transfers between devices: 17.6 us -> 6.75 us  [the longest x4 6.74 us: lat_faces(): north = lax.ppermute(down, 'lat', [(i + 1, i) for i in range(n_lat - 1)])]
    pallas_call x1, Pallas kernels: 14.2 us -> 8.4 us  [body(): call(build_kernel, (shape(SPAN, 2 * CELL, SLOT, dtype=BF16), shape(SPAN,...]
    all_to_all x0 -> x1, starting transfers between devices: none -> 4.5 us  [body(): pairs = lax.all_to_all(pairs, ('lon', 'lat'), 0, 0, tiled=True)]
    all_to_all x0 -> x1, waiting for transfers between devices: none -> 4.49 us  [body(): pairs = lax.all_to_all(pairs, ('lon', 'lat'), 0, 0, tiled=True)]
    ppermute x36 -> x20, waiting for transfers between devices: 16.7 us -> 20.4 us  [shift(): lax.ppermute(block, axis, [(i, (i + distance) % size) for i in range(size)])]
  transfers between devices with their start and end apart: 44 -> 29, of which waited for: 16 -> 11; matrix products, arithmetic and copies ran while one was open for 0% -> 0% of each run, Pallas kernels for 6% -> 11%
where the time goes in v2:
time: 174 us; the launch traced here: 173 us
  starting transfers between devices  67.3 us (39%)
  Pallas kernels  36.6 us (21%)
  waiting for transfers between devices  31.6 us (18%)
  blocking collectives  27.5 us (16%)
  local copies, waits for them, and re-layouts  8.93 us (5%)
    ppermute x20, starting transfers between devices, shift(): lax.ppermute(block, axis, [(i, (i + distance) % size) for i in range(size)])  46.8 us
    all_gather x1, blocking collectives, body(): shards = lax.all_gather(shard, 'orbit')  27.5 us
    ppermute x20, waiting for transfers between devices, shift(): lax.ppermute(block, axis, [(i, (i + distance) % size) for i in range(size)])  20.4 us
    pallas_call x3, Pallas kernels, body(): call(back_kernel, (FIELD, FACE, FACE), 12, work=MATMUL)  11.4 us
    ppermute x4, starting transfers between devices, lat_faces(): south = lax.ppermute(up, 'lat', [(i, i + 1) for i in range(n_lat - 1)])  10.6 us
    unnamed x18, local copies, waits for them, and re-layouts  8.93 us
    pallas_call x1, Pallas kernels, body(): call(build_kernel, (shape(SPAN, 2 * CELL, SLOT, dtype=BF16), shape(SPAN,...  8.4 us
    ppermute x4, waiting for transfers between devices, lat_faces(): north = lax.ppermute(down, 'lat', [(i + 1, i) for i in range(n_lat - 1)])  6.74 us
  transfers between devices with their start and end apart: 29, of which 11 were waited for; matrix products, arithmetic and copies ran while one was open for 0% of the time, Pallas kernels for 11%

profile of v2, /device:TPU:1, one launch (start us, length us, event | category | flops | bytes accessed | tf_op | source)
XLA Modules:
  0.0 172.9 jit_solution(1895000729578305294)
XLA Ops:
  6.6 27.5 %all-gather = f32[1344,128]{1,0:T(8,128)S(1)} all-gather(f32[168,128]{1,0:T(8,128)S(1)} %get-tuple-element.70), channel_id=2, replica_groups=mesh['orbit'=8,'lon'=16,'lat'=4] {'orbit'}, dimensions={0}, use_global_device_ids=true | all-gather | bytes 774144 | tf_op jit(solution)/shard_map/all_gather | solution.py:401
  34.0 3.2 %collective-permute-start.3 = (f32[8,1024]{1,0:T(8,128)S(1)}, f32[8,1024]{1,0:T(8,128)S(1)}, u32[]{:S(2)}, u32[]{:S(2)}) collective-permute-start(f32[8,1024]{1,0:T(8,128)S(1)} %shard_map.87.z2), channel_id=1, source_target_pairs={{0,8},{4,12},{8,16},{12,20},{16,24},{20,28},{24,32},{28,36},{32,40... | collective-permute-start | bytes 98312 | tf_op jit(solution)/shard_map/ppermute | solution.py:39
  37.2 7.7 %collective-permute-start.2 = (f32[8,1024]{1,0:T(8,128)S(1)}, f32[8,1024]{1,0:T(8,128)S(1)}, u32[]{:S(2)}, u32[]{:S(2)}) collective-permute-start(f32[8,1024]{1,0:T(8,128)S(1)} %shard_map.87.z2), channel_id=1, source_target_pairs={{0,4},{4,8},{8,12},{12,16},{16,20},{20,24},{24,28},{28,32},{32,36}... | collective-permute-start | bytes 98312 | tf_op jit(solution)/shard_map/ppermute | solution.py:39
  44.9 3.3 %collective-permute-start = (f32[8,1024]{1,0:T(8,128)S(1)}, f32[8,1024]{1,0:T(8,128)S(1)}, u32[]{:S(2)}, u32[]{:S(2)}) collective-permute-start(f32[8,1024]{1,0:T(8,128)S(1)} %shard_map.87.z2), channel_id=1, source_target_pairs={{0,56},{4,60},{8,0},{12,4},{16,8},{20,12},{24,16},{28,20},{32,24},... | collective-permute-start | bytes 98312 | tf_op jit(solution)/shard_map/ppermute | solution.py:39
  48.2 8.4 %shard_map.88 = (bf16[5,1024,1024]{2,1,0:T(8,128)(2,1)S(1)}, s32[5,8,1024]{2,1,0:T(8,128)S(1)}) custom-call(f32[8,168,128]{2,1,0:T(8,128)S(1)} %bitcast.9), custom_call_target="tpu_custom_call" | custom-call | flops 671088640 | bytes 20971520 | tf_op jit(solution)/shard_map/pallas_call | solution.py:405
  56.7 3.5 %shard_map.89 = (f32[64,512]{1,0:T(8,128)S(1)}, s32[5,8,1024]{2,1,0:T(8,128)S(1)}, f32[5,8,1024]{2,1,0:T(8,128)S(1)}, f32[8,512]{1,0:T(8,128)S(1)}, f32[8,512]{1,0:T(8,128)S(1)}) custom-call(f32[8,1024]{1,0:T(8,128)S(1)} %shard_map.87.z2, f32[8,1024]{1,0:T(8,128)S(1)} %collective-permute-done.z0, f32[8,1024]{1,0:T(8,128)S(1)} %collective-permute-done.1.z1, ...), custom_call_target="tpu_custom_call" | custom-call | flops 1342177280 | bytes 10485760 | tf_op jit(solution)/shard_map/pallas_call | solution.py:407
  60.2 3.1 %collective-permute-start.4 = (f32[8,512]{1,0:T(8,128)S(1)}, f32[8,512]{1,0:T(8,128)S(1)}, u32[]{:S(2)}, u32[]{:S(2)}) collective-permute-start(f32[8,512]{1,0:T(8,128)S(1)} %get-tuple-element.76), channel_id=1, source_target_pairs={{0,1},{1,2},{2,3},{4,5},{5,6},{6,7},{8,9},{9,10},{10,11},{12,13},{... | collective-permute-start | bytes 49160 | tf_op jit(solution)/shard_map/ppermute | solution.py:369
  71.3 3.5 %collective-permute-start.8 = (f32[3,8,1024]{2,1,0:T(8,128)S(1)}, f32[3,8,1024]{2,1,0:T(8,128)S(1)}, u32[]{:S(2)}, u32[]{:S(2)}) collective-permute-start(f32[3,8,1024]{2,1,0:T(8,128)S(1)} %get-tuple-element.84), channel_id=1, source_target_pairs={{0,56},{4,60},{8,0},{12,4},{16,8},{20,12},{24,16},{28,20},{32,24},... | collective-permute-start | bytes 294920 | tf_op jit(solution)/shard_map/ppermute | solution.py:39
  78.0 4.4 %collective-permute-done.9.minus2 = f32[3,8,1024]{2,1,0:T(8,128)S(1)} collective-permute-done((f32[3,8,1024]{2,1,0:T(8,128)S(1)}, f32[3,8,1024]{2,1,0:T(8,128)S(1)}, u32[]{:S(2)}, u32[]{:S(2)}) %collective-permute-start.9) | collective-permute-done | bytes 98336 | tf_op jit(solution)/shard_map/ppermute | solution.py:39
  82.4 3.8 %shard_map.91 = (f32[64,512]{1,0:T(8,128)S(1)}, f32[8,512]{1,0:T(8,128)S(1)}, f32[8,512]{1,0:T(8,128)S(1)}) custom-call(f32[64,512]{1,0:T(8,128)S(1)} %get-tuple-element.73.v_ref.v0.refs_1_, f32[5,8,1024]{2,1,0:T(8,128)S(1)} %get-tuple-element.75.own_ref, f32[5,8,1024]{2,1,0:T(8,128)S(1)} %collective-permute-done.6.plus1, ...), custom_call_target="tpu_custom_call" | custom-call | flops 1342177280 | bytes 10485760 | tf_op jit(solution)/shard_map/pallas_call | solution.py:413
  86.2 3.1 %collective-permute-start.10 = (f32[8,512]{1,0:T(8,128)S(1)}, f32[8,512]{1,0:T(8,128)S(1)}, u32[]{:S(2)}, u32[]{:S(2)}) collective-permute-start(f32[8,512]{1,0:T(8,128)S(1)} %get-tuple-element.92), channel_id=1, source_target_pairs={{0,1},{1,2},{2,3},{4,5},{5,6},{6,7},{8,9},{9,10},{10,11},{12,13},{... | collective-permute-start | bytes 49160 | tf_op jit(solution)/shard_map/ppermute | solution.py:369
  96.0 4.5 %collective-permute-start.14 = (f32[3,8,1024]{2,1,0:T(8,128)S(1)}, f32[3,8,1024]{2,1,0:T(8,128)S(1)}, u32[]{:S(2)}, u32[]{:S(2)}) collective-permute-start(f32[3,8,1024]{2,1,0:T(8,128)S(1)} %get-tuple-element.100), channel_id=1, source_target_pairs={{0,56},{4,60},{8,0},{12,4},{16,8},{20,12},{24,16},{28,20},{32,24},... | collective-permute-start | bytes 294920 | tf_op jit(solution)/shard_map/ppermute | solution.py:39
  102.4 4.6 %collective-permute-done.15.minus2 = f32[3,8,1024]{2,1,0:T(8,128)S(1)} collective-permute-done((f32[3,8,1024]{2,1,0:T(8,128)S(1)}, f32[3,8,1024]{2,1,0:T(8,128)S(1)}, u32[]{:S(2)}, u32[]{:S(2)}) %collective-permute-start.15) | collective-permute-done | bytes 98336 | tf_op jit(solution)/shard_map/ppermute | solution.py:39
  107.1 3.8 %shard_map.93 = (f32[64,512]{1,0:T(8,128)S(1)}, f32[8,512]{1,0:T(8,128)S(1)}, f32[8,512]{1,0:T(8,128)S(1)}) custom-call(f32[64,512]{1,0:T(8,128)S(1)} %get-tuple-element.90.v_ref.v1.refs_2_, f32[5,8,1024]{2,1,0:T(8,128)S(1)} %get-tuple-element.91.own_ref, f32[5,8,1024]{2,1,0:T(8,128)S(1)} %collective-permute-done.12.plus1, ...), custom_call_target="tpu_custom_call" | custom-call | flops 1342177280 | bytes 10485760 | tf_op jit(solution)/shard_map/pallas_call | solution.py:413
  110.9 2.8 %collective-permute-start.16 = (f32[8,512]{1,0:T(8,128)S(1)}, f32[8,512]{1,0:T(8,128)S(1)}, u32[]{:S(2)}, u32[]{:S(2)}) collective-permute-start(f32[8,512]{1,0:T(8,128)S(1)} %get-tuple-element.106), channel_id=1, source_target_pairs={{0,1},{1,2},{2,3},{4,5},{5,6},{6,7},{8,9},{9,10},{10,11},{12,13},{... | collective-permute-start | bytes 49160 | tf_op jit(solution)/shard_map/ppermute | solution.py:369
  120.4 3.1 %collective-permute-start.20 = (f32[3,8,1024]{2,1,0:T(8,128)S(1)}, f32[3,8,1024]{2,1,0:T(8,128)S(1)}, u32[]{:S(2)}, u32[]{:S(2)}) collective-permute-start(f32[3,8,1024]{2,1,0:T(8,128)S(1)} %get-tuple-element.114), channel_id=1, source_target_pairs={{0,56},{4,60},{8,0},{12,4},{16,8},{20,12},{24,16},{28,20},{32,24},... | collective-permute-start | bytes 294920 | tf_op jit(solution)/shard_map/ppermute | solution.py:39
  126.4 4.7 %collective-permute-done.21.minus2 = f32[3,8,1024]{2,1,0:T(8,128)S(1)} collective-permute-done((f32[3,8,1024]{2,1,0:T(8,128)S(1)}, f32[3,8,1024]{2,1,0:T(8,128)S(1)}, u32[]{:S(2)}, u32[]{:S(2)}) %collective-permute-start.21) | collective-permute-done | bytes 98336 | tf_op jit(solution)/shard_map/ppermute | solution.py:39
  131.1 3.8 %shard_map.95 = (f32[64,512]{1,0:T(8,128)S(1)}, f32[8,512]{1,0:T(8,128)S(1)}, f32[8,512]{1,0:T(8,128)S(1)}) custom-call(f32[64,512]{1,0:T(8,128)S(1)} %get-tuple-element.104.v_ref.v2.refs_3_, f32[5,8,1024]{2,1,0:T(8,128)S(1)} %get-tuple-element.105.own_ref, f32[5,8,1024]{2,1,0:T(8,128)S(1)} %collective-permute-done.18.plus1, ...), custom_call_target="tpu_custom_call" | custom-call | flops 1342177280 | bytes 10485760 | tf_op jit(solution)/shard_map/pallas_call | solution.py:413
  142.8 4.5 %collective-permute-start.26 = (f32[3,8,1024]{2,1,0:T(8,128)S(1)}, f32[3,8,1024]{2,1,0:T(8,128)S(1)}, u32[]{:S(2)}, u32[]{:S(2)}) collective-permute-start(f32[3,8,1024]{2,1,0:T(8,128)S(1)} %get-tuple-element.128), channel_id=1, source_target_pairs={{0,56},{4,60},{8,0},{12,4},{16,8},{20,12},{24,16},{28,20},{32,24},... | collective-permute-start | bytes 294920 | tf_op jit(solution)/shard_map/ppermute | solution.py:39
  149.2 4.6 %collective-permute-done.27.minus2 = f32[3,8,1024]{2,1,0:T(8,128)S(1)} collective-permute-done((f32[3,8,1024]{2,1,0:T(8,128)S(1)}, f32[3,8,1024]{2,1,0:T(8,128)S(1)}, u32[]{:S(2)}, u32[]{:S(2)}) %collective-permute-start.27) | collective-permute-done | bytes 98336 | tf_op jit(solution)/shard_map/ppermute | solution.py:39
  155.1 4.5 %all-to-all-start = ((f32[64,8,128]{2,1,0:T(8,128)}), f32[64,8,128]{2,1,0:T(8,128)S(1)}, u32[]{:S(2)}, u32[]{:S(2)}) async-start(f32[64,8,128]{2,1,0:T(8,128)} %bitcast.6), calls=%async_computation | async-start | bytes 524288 | tf_op jit(solution)/shard_map/all_to_all | solution.py:421
  159.6 4.0 %copy-done.1 = bf16[5,1024,1024]{2,1,0:T(8,128)(2,1)S(1)} copy-done((bf16[5,1024,1024]{2,1,0:T(8,128)(2,1)S(1)}, bf16[5,1024,1024]{2,1,0:T(8,128)(2,1)}, u32[]{:S(2)}) %copy-start.1) | copy-done | bytes 10485784
  163.6 3.8 %shard_map.98.refs_5_ = f32[64,512]{1,0:T(8,128)S(1)} custom-call(f32[5,8,1024]{2,1,0:T(8,128)S(1)} %get-tuple-element.134.rays_ref, f32[64,512]{1,0:T(8,128)S(1)} %get-tuple-element.135.image_ref, s32[5,8,1024]{2,1,0:T(8,128)S(1)} %get-tuple-element.74.mask_ref, bf16[5,1024,1024]{2,1,0:T(8,128)(2,1)S(1)} %copy-done.1, f32[64,64]{1,0:T(8,128)S(1)} %get-tuple-element.88.gram_ref), custom_call_target="tpu_custom_call" | custom-call | flops 1342177280 | bytes 10485760 | tf_op jit(solution)/shard_map/pallas_call | solution.py:422
  167.4 4.5 %all-to-all-done = f32[64,8,128]{2,1,0:T(8,128)S(1)} async-done(((f32[64,8,128]{2,1,0:T(8,128)}), f32[64,8,128]{2,1,0:T(8,128)S(1)}, u32[]{:S(2)}, u32[]{:S(2)}) %all-to-all-start) | async-done | bytes 262176 | tf_op jit(solution)/shard_map/all_to_all | solution.py:421
  (67 shorter events, 47.1 us)
Async XLA Ops:
  34.0 22.6 %collective-permute-start.3 = (f32[8,1024]{1,0:T(8,128)S(1)}, f32[8,1024]{1,0:T(8,128)S(1)}, u32[]{:S(2)}, u32[]{:S(2)}) collective-permute-start(f32[8,1024]{1,0:T(8,128)S(1)} %shard_map.87.z2), channel_id=1, source_target_pairs={{0,8},{4,12},{8,16},{12,20},{16,24},{20,28},{24,32},{28,36},{32,40... | collective-permute-start | bytes 98312 | tf_op jit(solution)/shard_map/ppermute | solution.py:39
  37.2 19.4 %collective-permute-start.2 = (f32[8,1024]{1,0:T(8,128)S(1)}, f32[8,1024]{1,0:T(8,128)S(1)}, u32[]{:S(2)}, u32[]{:S(2)}) collective-permute-start(f32[8,1024]{1,0:T(8,128)S(1)} %shard_map.87.z2), channel_id=1, source_target_pairs={{0,4},{4,8},{8,12},{12,16},{16,20},{20,24},{24,28},{28,32},{32,36}... | collective-permute-start | bytes 98312 | tf_op jit(solution)/shard_map/ppermute | solution.py:39
  44.9 11.7 %collective-permute-start.1 = (f32[8,1024]{1,0:T(8,128)S(1)}, f32[8,1024]{1,0:T(8,128)S(1)}, u32[]{:S(2)}, u32[]{:S(2)}) collective-permute-start(f32[8,1024]{1,0:T(8,128)S(1)} %shard_map.87.z2), channel_id=1, source_target_pairs={{0,60},{4,0},{8,4},{12,8},{16,12},{20,16},{24,20},{28,24},{32,28},... | collective-permute-start | bytes 98312 | tf_op jit(solution)/shard_map/ppermute | solution.py:39
  44.9 11.7 %collective-permute-start = (f32[8,1024]{1,0:T(8,128)S(1)}, f32[8,1024]{1,0:T(8,128)S(1)}, u32[]{:S(2)}, u32[]{:S(2)}) collective-permute-start(f32[8,1024]{1,0:T(8,128)S(1)} %shard_map.87.z2), channel_id=1, source_target_pairs={{0,56},{4,60},{8,0},{12,4},{16,8},{20,12},{24,16},{28,20},{32,24},... | collective-permute-start | bytes 98312 | tf_op jit(solution)/shard_map/ppermute | solution.py:39
  60.2 6.0 %collective-permute-start.4 = (f32[8,512]{1,0:T(8,128)S(1)}, f32[8,512]{1,0:T(8,128)S(1)}, u32[]{:S(2)}, u32[]{:S(2)}) collective-permute-start(f32[8,512]{1,0:T(8,128)S(1)} %get-tuple-element.76), channel_id=1, source_target_pairs={{0,1},{1,2},{2,3},{4,5},{5,6},{6,7},{8,9},{9,10},{10,11},{12,13},{... | collective-permute-start | bytes 49160 | tf_op jit(solution)/shard_map/ppermute | solution.py:369
  67.9 14.6 %collective-permute-start.6 = (f32[5,8,1024]{2,1,0:T(8,128)S(1)}, f32[5,8,1024]{2,1,0:T(8,128)S(1)}, u32[]{:S(2)}, u32[]{:S(2)}) collective-permute-start(f32[5,8,1024]{2,1,0:T(8,128)S(1)} %get-tuple-element.82), channel_id=1, source_target_pairs={{0,60},{4,0},{8,4},{12,8},{16,12},{20,16},{24,20},{28,24},{32,28},... | collective-permute-start | bytes 491528 | tf_op jit(solution)/shard_map/ppermute | solution.py:39
  70.4 12.1 %collective-permute-start.7 = (f32[5,8,1024]{2,1,0:T(8,128)S(1)}, f32[5,8,1024]{2,1,0:T(8,128)S(1)}, u32[]{:S(2)}, u32[]{:S(2)}) collective-permute-start(f32[5,8,1024]{2,1,0:T(8,128)S(1)} %get-tuple-element.83), channel_id=1, source_target_pairs={{0,4},{4,8},{8,12},{12,16},{16,20},{20,24},{24,28},{28,32},{32,36}... | collective-permute-start | bytes 491528 | tf_op jit(solution)/shard_map/ppermute | solution.py:39
  71.3 6.7 %collective-permute-start.8 = (f32[3,8,1024]{2,1,0:T(8,128)S(1)}, f32[3,8,1024]{2,1,0:T(8,128)S(1)}, u32[]{:S(2)}, u32[]{:S(2)}) collective-permute-start(f32[3,8,1024]{2,1,0:T(8,128)S(1)} %get-tuple-element.84), channel_id=1, source_target_pairs={{0,56},{4,60},{8,0},{12,4},{16,8},{20,12},{24,16},{28,20},{32,24},... | collective-permute-start | bytes 294920 | tf_op jit(solution)/shard_map/ppermute | solution.py:39
  74.8 7.6 %collective-permute-start.9 = (f32[3,8,1024]{2,1,0:T(8,128)S(1)}, f32[3,8,1024]{2,1,0:T(8,128)S(1)}, u32[]{:S(2)}, u32[]{:S(2)}) collective-permute-start(f32[3,8,1024]{2,1,0:T(8,128)S(1)} %get-tuple-element.85), channel_id=1, source_target_pairs={{0,8},{4,12},{8,16},{12,20},{16,24},{20,28},{24,32},{28,36},{32,40... | collective-permute-start | bytes 294920 | tf_op jit(solution)/shard_map/ppermute | solution.py:39
  86.2 6.0 %collective-permute-start.10 = (f32[8,512]{1,0:T(8,128)S(1)}, f32[8,512]{1,0:T(8,128)S(1)}, u32[]{:S(2)}, u32[]{:S(2)}) collective-permute-start(f32[8,512]{1,0:T(8,128)S(1)} %get-tuple-element.92), channel_id=1, source_target_pairs={{0,1},{1,2},{2,3},{4,5},{5,6},{6,7},{8,9},{9,10},{10,11},{12,13},{... | collective-permute-start | bytes 49160 | tf_op jit(solution)/shard_map/ppermute | solution.py:369
  93.9 13.2 %collective-permute-start.12 = (f32[5,8,1024]{2,1,0:T(8,128)S(1)}, f32[5,8,1024]{2,1,0:T(8,128)S(1)}, u32[]{:S(2)}, u32[]{:S(2)}) collective-permute-start(f32[5,8,1024]{2,1,0:T(8,128)S(1)} %get-tuple-element.98), channel_id=1, source_target_pairs={{0,60},{4,0},{8,4},{12,8},{16,12},{20,16},{24,20},{28,24},{32,28},... | collective-permute-start | bytes 491528 | tf_op jit(solution)/shard_map/ppermute | solution.py:39
  96.0 11.0 %collective-permute-start.13 = (f32[5,8,1024]{2,1,0:T(8,128)S(1)}, f32[5,8,1024]{2,1,0:T(8,128)S(1)}, u32[]{:S(2)}, u32[]{:S(2)}) collective-permute-start(f32[5,8,1024]{2,1,0:T(8,128)S(1)} %get-tuple-element.99), channel_id=1, source_target_pairs={{0,4},{4,8},{8,12},{12,16},{16,20},{20,24},{24,28},{28,32},{32,36}... | collective-permute-start | bytes 491528 | tf_op jit(solution)/shard_map/ppermute | solution.py:39
  96.0 6.4 %collective-permute-start.14 = (f32[3,8,1024]{2,1,0:T(8,128)S(1)}, f32[3,8,1024]{2,1,0:T(8,128)S(1)}, u32[]{:S(2)}, u32[]{:S(2)}) collective-permute-start(f32[3,8,1024]{2,1,0:T(8,128)S(1)} %get-tuple-element.100), channel_id=1, source_target_pairs={{0,56},{4,60},{8,0},{12,4},{16,8},{20,12},{24,16},{28,20},{32,24},... | collective-permute-start | bytes 294920 | tf_op jit(solution)/shard_map/ppermute | solution.py:39
  100.5 6.6 %collective-permute-start.15 = (f32[3,8,1024]{2,1,0:T(8,128)S(1)}, f32[3,8,1024]{2,1,0:T(8,128)S(1)}, u32[]{:S(2)}, u32[]{:S(2)}) collective-permute-start(f32[3,8,1024]{2,1,0:T(8,128)S(1)} %get-tuple-element.101), channel_id=1, source_target_pairs={{0,8},{4,12},{8,16},{12,20},{16,24},{20,28},{24,32},{28,36},{32,40... | collective-permute-start | bytes 294920 | tf_op jit(solution)/shard_map/ppermute | solution.py:39
  110.9 5.9 %collective-permute-start.16 = (f32[8,512]{1,0:T(8,128)S(1)}, f32[8,512]{1,0:T(8,128)S(1)}, u32[]{:S(2)}, u32[]{:S(2)}) collective-permute-start(f32[8,512]{1,0:T(8,128)S(1)} %get-tuple-element.106), channel_id=1, source_target_pairs={{0,1},{1,2},{2,3},{4,5},{5,6},{6,7},{8,9},{9,10},{10,11},{12,13},{... | collective-permute-start | bytes 49160 | tf_op jit(solution)/shard_map/ppermute | solution.py:369
  118.6 12.5 %collective-permute-start.18 = (f32[5,8,1024]{2,1,0:T(8,128)S(1)}, f32[5,8,1024]{2,1,0:T(8,128)S(1)}, u32[]{:S(2)}, u32[]{:S(2)}) collective-permute-start(f32[5,8,1024]{2,1,0:T(8,128)S(1)} %get-tuple-element.112), channel_id=1, source_target_pairs={{0,60},{4,0},{8,4},{12,8},{16,12},{20,16},{24,20},{28,24},{32,28},... | collective-permute-start | bytes 491528 | tf_op jit(solution)/shard_map/ppermute | solution.py:39
  119.0 12.1 %collective-permute-start.19 = (f32[5,8,1024]{2,1,0:T(8,128)S(1)}, f32[5,8,1024]{2,1,0:T(8,128)S(1)}, u32[]{:S(2)}, u32[]{:S(2)}) collective-permute-start(f32[5,8,1024]{2,1,0:T(8,128)S(1)} %get-tuple-element.113), channel_id=1, source_target_pairs={{0,4},{4,8},{8,12},{12,16},{16,20},{20,24},{24,28},{28,32},{32,36}... | collective-permute-start | bytes 491528 | tf_op jit(solution)/shard_map/ppermute | solution.py:39
  120.4 6.0 %collective-permute-start.20 = (f32[3,8,1024]{2,1,0:T(8,128)S(1)}, f32[3,8,1024]{2,1,0:T(8,128)S(1)}, u32[]{:S(2)}, u32[]{:S(2)}) collective-permute-start(f32[3,8,1024]{2,1,0:T(8,128)S(1)} %get-tuple-element.114), channel_id=1, source_target_pairs={{0,56},{4,60},{8,0},{12,4},{16,8},{20,12},{24,16},{28,20},{32,24},... | collective-permute-start | bytes 294920 | tf_op jit(solution)/shard_map/ppermute | solution.py:39
  123.5 7.6 %collective-permute-start.21 = (f32[3,8,1024]{2,1,0:T(8,128)S(1)}, f32[3,8,1024]{2,1,0:T(8,128)S(1)}, u32[]{:S(2)}, u32[]{:S(2)}) collective-permute-start(f32[3,8,1024]{2,1,0:T(8,128)S(1)} %get-tuple-element.115), channel_id=1, source_target_pairs={{0,8},{4,12},{8,16},{12,20},{16,24},{20,28},{24,32},{28,36},{32,40... | collective-permute-start | bytes 294920 | tf_op jit(solution)/shard_map/ppermute | solution.py:39
  141.0 12.8 %collective-permute-start.24 = (f32[5,8,1024]{2,1,0:T(8,128)S(1)}, f32[5,8,1024]{2,1,0:T(8,128)S(1)}, u32[]{:S(2)}, u32[]{:S(2)}) collective-permute-start(f32[5,8,1024]{2,1,0:T(8,128)S(1)} %get-tuple-element.126), channel_id=1, source_target_pairs={{0,60},{4,0},{8,4},{12,8},{16,12},{20,16},{24,20},{28,24},{32,28},... | collective-permute-start | bytes 491528 | tf_op jit(solution)/shard_map/ppermute | solution.py:39
  142.8 11.0 %collective-permute-start.25 = (f32[5,8,1024]{2,1,0:T(8,128)S(1)}, f32[5,8,1024]{2,1,0:T(8,128)S(1)}, u32[]{:S(2)}, u32[]{:S(2)}) collective-permute-start(f32[5,8,1024]{2,1,0:T(8,128)S(1)} %get-tuple-element.127), channel_id=1, source_target_pairs={{0,4},{4,8},{8,12},{12,16},{16,20},{20,24},{24,28},{28,32},{32,36}... | collective-permute-start | bytes 491528 | tf_op jit(solution)/shard_map/ppermute | solution.py:39
  142.8 6.4 %collective-permute-start.26 = (f32[3,8,1024]{2,1,0:T(8,128)S(1)}, f32[3,8,1024]{2,1,0:T(8,128)S(1)}, u32[]{:S(2)}, u32[]{:S(2)}) collective-permute-start(f32[3,8,1024]{2,1,0:T(8,128)S(1)} %get-tuple-element.128), channel_id=1, source_target_pairs={{0,56},{4,60},{8,0},{12,4},{16,8},{20,12},{24,16},{28,20},{32,24},... | collective-permute-start | bytes 294920 | tf_op jit(solution)/shard_map/ppermute | solution.py:39
  147.2 6.6 %collective-permute-start.27 = (f32[3,8,1024]{2,1,0:T(8,128)S(1)}, f32[3,8,1024]{2,1,0:T(8,128)S(1)}, u32[]{:S(2)}, u32[]{:S(2)}) collective-permute-start(f32[3,8,1024]{2,1,0:T(8,128)S(1)} %get-tuple-element.129), channel_id=1, source_target_pairs={{0,8},{4,12},{8,16},{12,20},{16,24},{20,28},{24,32},{28,36},{32,40... | collective-permute-start | bytes 294920 | tf_op jit(solution)/shard_map/ppermute | solution.py:39
  155.1 16.8 %all-to-all-start = ((f32[64,8,128]{2,1,0:T(8,128)}), f32[64,8,128]{2,1,0:T(8,128)S(1)}, u32[]{:S(2)}, u32[]{:S(2)}) async-start(f32[64,8,128]{2,1,0:T(8,128)} %bitcast.6), calls=%async_computation | async-start | bytes 524288 | tf_op jit(solution)/shard_map/all_to_all | solution.py:421
  (14 other events, 112.9 us)

commit v3 on v2

--- a/solution.py
+++ b/solution.py
@@ -148,15 +148,17 @@
     total = None
     for slot in range(SPAN):
         part = lax.dot_general(
-            masked_rows(sums[slot], lats[slot]), w_ref[slot], (((1,), (1,)), ((), ())), preferred_element_type=F32
+            w_ref[slot], masked_rows(sums[slot], lats[slot]), (((1,), (1,)), ((), ())), preferred_element_type=F32
         )
         total = part if total is None else total + part
-    total = total[:, :CELL] + total[:, CELL:]
+    total = (total[:CELL] + total[CELL:]).T
     return total[:64] + total[64:]
 
 
-def project_kernel(v_ref, mask_ref, w_ref, own_ref, left_ref, right_ref, left2_ref, right2_ref):
-    v = v_ref[...]
+def project_all(v, lats, w_ref, outs):
+    own_ref, left_ref, right_ref, left2_ref, right2_ref, down_ref, up_ref = outs
+    down_ref[...] = v[0:8]
+    up_ref[...] = v[56:64]
     for l in range(CLAT):
         left_ref[4, :, pl.ds(l * LEV, LEV)] = v[8 * l:8 * l + 8, 0:LEV]
         right_ref[4, :, pl.ds(l * LEV, LEV)] = v[8 * l:8 * l + 8, CELL - LEV:]
@@ -165,7 +167,7 @@
     for slot in range(SPAN):
         wide = jnp.dot(rows, w_ref[slot], preferred_element_type=F32)
         wide = wide[:64] + wide[64:]
-        lat = mask_ref[slot]
+        lat = lats[slot]
         total = jnp.where(lat == 0, wide[0:8], 0.0)
         for l in range(1, CLAT):
             total = total + jnp.where(lat == l, wide[8 * l:8 * l + 8], 0.0)
@@ -180,7 +182,7 @@
             right2_ref[slot] = total
 
 
-def init_kernel(z2, z0, z1, z3, z4, lat_ref, w_ref, v_ref, mask_ref, middle_ref, down_ref, up_ref):
+def init_kernel(z2, z0, z1, z3, z4, lat_ref, w_ref, v_ref, mask_ref, *outs):
     sums, lats = [], []
     sub = lax.broadcasted_iota(jnp.int32, (8, SLOT), 0)
     for slot, z in enumerate((z0, z1, z2, z3, z4)):
@@ -188,13 +190,11 @@
         present = (begin <= slot) & (begin + (NT - 1) >= slot)
         lat = jnp.where(present, lat_ref[slot], -1)
         mask_ref[slot] = lat
-        middle_ref[slot] = jnp.where(begin + 1.0 == slot, 1.0, 0.0)
         lats.append(lat)
         sums.append(jnp.where(sub < S, z[...], 0.0))
     v = back_all(sums, lats, w_ref)
     v_ref[...] = v
-    down_ref[...] = v[0:8]
-    up_ref[...] = v[56:64]
+    project_all(v, lats, w_ref, outs)
 
 
 def ray_sums(own_ref, plus1, minus1, plus2, minus2):
@@ -230,71 +230,42 @@
     return jnp.concatenate(pieces, axis=1)
 
 
-def back_image(sums, mask_ref, w_ref, gram_ref):
-    image = back_all(sums, [mask_ref[slot] for slot in range(SPAN)], w_ref)
-    return jnp.dot(gram_ref[...], image, precision=highest, preferred_element_type=F32)
-
-
-def back_kernel(v_ref, own_ref, plus1, minus1, plus2, minus2, south, north, mask_ref, w_ref, gram_ref, prior_ref, out_ref, down_ref, up_ref):
-    sums = ray_sums(own_ref, plus1, minus1, plus2, minus2)
-    v = back_image(sums, mask_ref, w_ref, gram_ref) + prior_image(v_ref[...], plus1, minus1, south, north, prior_ref)
+def next_vector(v_ref, own_ref, plus1, minus1, plus2, minus2, south, north, lats, w_ref, gram_ref, prior_ref):
+    image = back_all(ray_sums(own_ref, plus1, minus1, plus2, minus2), lats, w_ref)
+    image = jnp.dot(gram_ref[...], image, precision=highest, preferred_element_type=F32)
+    return image + prior_image(v_ref[...], plus1, minus1, south, north, prior_ref)
+
+
+def step_kernel(*refs):
+    lats = [refs[8][slot] for slot in range(SPAN)]
+    v = next_vector(*refs[:8], lats, *refs[9:12])
+    refs[12][...] = v
+    project_all(v, lats, refs[9], refs[13:])
+
+
+PAIRS = [(i, j) for i in range(ITERS) for j in range(i, ITERS)] + [(ITERS - 1, ITERS)]
+
+
+def last_kernel(*refs):
+    lats = [refs[8][slot] for slot in range(SPAN)]
+    v = next_vector(*refs[:8], lats, *refs[9:12])
+    earlier, (out_ref, pair_ref) = refs[12:12 + ITERS - 1], refs[12 + ITERS - 1:]
     out_ref[...] = v
-    down_ref[...] = v[0:8]
-    up_ref[...] = v[56:64]
-
-
-PAIRS = [(i, j) for i in range(ITERS) for j in range(i, ITERS)] + [(ITERS - 1, ITERS)]
-
-
-def fold_rows(product):
-    product = jnp.sum(product, axis=0, keepdims=True)
-    fold = product[:, 0:LEV]
-    for c in range(1, product.shape[1] // LEV):
-        fold = fold + product[:, c * LEV:(c + 1) * LEV]
-    return fold
-
-
-def sums_kernel(v0, v1, v2, v3, own_ref, plus1, minus1, plus2, minus2, south, north, middle_ref, gram_ref, prior_ref, pair_ref, rays_ref, image_ref):
-    sums = ray_sums(own_ref, plus1, minus1, plus2, minus2)
-    vectors = [v0[...], v1[...], v2[...], v3[...]]
-    image = prior_image(vectors[-1], plus1, minus1, south, north, prior_ref)
-    image_ref[...] = image
-    last = fold_rows(vectors[-1] * image)
-    gram = gram_ref[0:8, 0:8]
-    for slot in range(SPAN):
-        rays_ref[slot] = sums[slot]
-        mixed = jnp.dot(gram, sums[slot], precision=highest, preferred_element_type=F32)
-        last = last + fold_rows(sums[slot] * mixed * middle_ref[slot])
-    folds = [fold_rows(vectors[i] * vectors[j]) for i, j in PAIRS[:-1]] + [last]
-    folds.append(jnp.zeros_like(last))
-    folds = [fold + pltpu.roll(fold, LEV // 2, 1) for fold in folds]
+    vectors = [ref[...] for ref in earlier] + [refs[0][...], v]
     lane = lax.broadcasted_iota(jnp.int32, (1, LEV), 1)
-    packed = [jnp.where(lane < LEV // 2, folds[2 * n], folds[2 * n + 1]) for n in range(len(folds) // 2)]
-    sub = lax.broadcasted_iota(jnp.int32, (8, LEV), 0)
-    block = jnp.zeros((8, LEV), F32)
-    for n, row in enumerate(packed):
-        block = jnp.where(sub == n, row, block)
-    for n in range(pair_ref.shape[0] // 8):
-        pair_ref[pl.ds(8 * n, 8), :] = block
-
-
-def last_kernel(rays_ref, image_ref, mask_ref, w_ref, gram_ref, out_ref):
-    sums = [rays_ref[slot] for slot in range(SPAN)]
-    out_ref[...] = back_image(sums, mask_ref, w_ref, gram_ref) + image_ref[...]
+    row = jnp.zeros((1, LEV), F32)
+    for n, (i, j) in enumerate(PAIRS):
+        product = jnp.sum(vectors[i] * vectors[j], axis=0, keepdims=True)
+        row = jnp.where(lane == n, jnp.sum(product, axis=1, keepdims=True), row)
+    pair_ref[...] = jnp.broadcast_to(row, pair_ref.shape)
 
 
 def combine_kernel(scale_ref, *refs):
     sums_ref, vector_refs, (x_ref, r_ref, spread) = refs[0], refs[1:ITERS + 2], refs[ITERS + 2:]
-    parts = [sums_ref[pl.ds(8 * n, 8), :] for n in range(sums_ref.shape[0] // 8)]
-    while len(parts) > 1:
-        parts = [a + b for a, b in zip(parts[::2], parts[1::2])]
-    lane = lax.broadcasted_iota(jnp.int32, (8, LEV), 1)
-    lower = jnp.sum(jnp.where(lane < LEV // 2, parts[0], 0.0), axis=1, keepdims=True)
-    upper = jnp.sum(jnp.where(lane < LEV // 2, 0.0, parts[0]), axis=1, keepdims=True)
+    row = jnp.sum(sums_ref[...], axis=0, keepdims=True)
     table = {}
     for n, (i, j) in enumerate(PAIRS):
-        half = upper if n & 1 else lower
-        table[i, j] = table[j, i] = half[n >> 1:(n >> 1) + 1, :]
+        table[i, j] = table[j, i] = row[:, n:n + 1]
     for i in range(ITERS - 1):
         table[i, ITERS] = table[i + 1, ITERS - 1]
     scale = scale_ref[0:1, 0:1]
@@ -362,21 +333,18 @@
 MESSAGES = (shape(SPAN, 8, SLOT), shape(5, 8, SLOT), shape(5, 8, SLOT), shape(3, 8, SLOT), shape(3, 8, SLOT))
 FACE = shape(8, CELL)
 FIELD = shape(64, CELL)
-
-
-def lat_faces(down, up):
+SENT = MESSAGES + (FACE, FACE)
+
+
+def exchange(own, left, right, left2, right2, down, up):
     n_lat = lax.axis_size("lat")
-    south = lax.ppermute(up, "lat", [(i, i + 1) for i in range(n_lat - 1)])
-    north = lax.ppermute(down, "lat", [(i + 1, i) for i in range(n_lat - 1)])
-    return south, north
-
-
-def exchange(south, north, own, left, right, left2, right2):
-    south, north, left, right, left2, right2 = lax.optimization_barrier((south, north, left, right, left2, right2))
+    plus1 = shift(left, "lon", -1)
+    minus1 = shift(right, "lon", 1)
     plus2 = shift(left2, "lon", -2)
     minus2 = shift(right2, "lon", 2)
-    plus1 = shift(left, "lon", -1)
-    minus1 = shift(right, "lon", 1)
+    south = lax.ppermute(up, "lat", [(i, i + 1) for i in range(n_lat - 1)])
+    plus1, down = lax.optimization_barrier((plus1, down))
+    north = lax.ppermute(down, "lat", [(i + 1, i) for i in range(n_lat - 1)])
     return own, plus1, minus1, plus2, minus2, south, north
 
 
@@ -397,30 +365,27 @@
             pltpu.SemaphoreType.DMA((7,)),
         ],
         compiler_params=LIMIT,
-    )(prior_weight, observed.T, ray_start.reshape(1, RAYS), tile_cells.T, tile_lengths.T, channel_kernel, noise_weight.reshape(1, -1))
+    )(*[
+        pltpu.with_memory_space_constraint(value, pltpu.HBM)
+        for value in (prior_weight, observed.T, ray_start.reshape(1, RAYS), tile_cells.T, tile_lengths.T, channel_kernel, noise_weight.reshape(1, -1))
+    ])
     shards = lax.all_gather(shard, "orbit")
     (z,) = call(gather_kernel, (shape(8, SLOT),), 1)(shards)
     z1, z3 = shift(z, "lon", -1), shift(z, "lon", 1)
     z0, z4 = shift(z, "lon", -2), shift(z, "lon", 2)
     w, lat = call(build_kernel, (shape(SPAN, 2 * CELL, SLOT, dtype=BF16), shape(SPAN, 8, SLOT, dtype=jnp.int32)), 1, work=BUILD)(shards)
     mask_shape = shape(SPAN, 8, SLOT, dtype=jnp.int32)
-    v, mask, middle, down, up = call(init_kernel, (FIELD, mask_shape, shape(SPAN, 8, SLOT), FACE, FACE), 7, work=MATMUL)(z, z0, z1, z3, z4, lat, w)
-    south, north = lat_faces(down, up)
+    v, mask, *sent = call(init_kernel, (FIELD, mask_shape) + SENT, 7, work=MATMUL)(z, z0, z1, z3, z4, lat, w)
     vectors = [v]
-    sent = call(project_kernel, MESSAGES, 3, work=MATMUL)(v, mask, w)
     for turn in range(ITERS - 1):
-        received = exchange(south, north, *sent)
-        v, down, up = call(back_kernel, (FIELD, FACE, FACE), 12, work=MATMUL)(v, *received, mask, w, gram, prior)
-        south, north = lat_faces(down, up)
+        v, *sent = call(step_kernel, (FIELD,) + SENT, 12, work=MATMUL)(v, *exchange(*sent), mask, w, gram, prior)
         vectors.append(v)
-        sent = call(project_kernel, MESSAGES, 3, work=MATMUL)(v, mask, w)
     peers = lax.axis_size("lon") * lax.axis_size("lat")
-    pairs, rays, image = call(sums_kernel, (shape(8 * peers, LEV), shape(SPAN, 8, SLOT), FIELD), 14)(
-        *vectors, *exchange(south, north, *sent), middle, gram, prior
+    v, pairs = call(last_kernel, (FIELD, shape(peers, LEV)), 12 + ITERS - 1, work=MATMUL)(
+        v, *exchange(*sent), mask, w, gram, prior, *vectors[:-1]
     )
+    vectors.append(v)
     pairs = lax.all_to_all(pairs, ("lon", "lat"), 0, 0, tiled=True)
-    (v,) = call(last_kernel, (FIELD,), 5, work=MATMUL)(rays, image, mask, w, gram)
-    vectors.append(v)
     field = shape(S, CLON, CLAT, LEV)
     return tuple(call(combine_kernel, (field, field), ITERS + 3, False, [pltpu.VMEM((2, CLON, 64, LEV), F32)])(scale, pairs, *vectors))
 

time: 174 us -> 169 us (0.971)
  waiting for transfers between devices: 31.6 us -> 12.3 us
  blocking collectives: 27.5 us -> 44.2 us
  local copies, waits for them, and re-layouts: 8.93 us -> 0 us
  Pallas kernels: 36.6 us -> 43.9 us
    all_to_all x0 -> x1, blocking collectives: none -> 16.7 us  [body(): pairs = lax.all_to_all(pairs, ('lon', 'lat'), 0, 0, tiled=True)]
    ppermute x20, waiting for transfers between devices: 20.4 us -> 4.19 us  [shift(): lax.ppermute(block, axis, [(i, (i + distance) % size) for i in range(size)])]
    unnamed x18 -> x0, local copies, waits for them, and re-layouts: 8.93 us -> none
    pallas_call x10 -> x5, Pallas kernels: 26.2 us -> 32.8 us  [the longest x3 22.3 us: body(): call(step_kernel, (FIELD,) + SENT, 12, work=MATMUL)]
    all_to_all x1 -> x0, starting transfers between devices: 4.5 us -> none  [body(): pairs = lax.all_to_all(pairs, ('lon', 'lat'), 0, 0, tiled=True)]
    all_to_all x1 -> x0, waiting for transfers between devices: 4.49 us -> none  [body(): pairs = lax.all_to_all(pairs, ('lon', 'lat'), 0, 0, tiled=True)]
    ppermute x20, starting transfers between devices: 46.8 us -> 50.4 us  [shift(): lax.ppermute(block, axis, [(i, (i + distance) % size) for i in range(size)])]
  transfers between devices with their start and end apart: 29 -> 28, of which waited for: 11 -> 8; matrix products, arithmetic and copies ran while one was open for 0% -> 0% of each run, Pallas kernels for 11% -> 5%
where the time goes in v3:
time: 169 us; the launch traced here: 168 us
  starting transfers between devices  67.1 us (40%)
  blocking collectives  44.2 us (26%)
  Pallas kernels  43.9 us (26%)
  waiting for transfers between devices  12.3 us (7%)
    ppermute x20, starting transfers between devices, shift(): lax.ppermute(block, axis, [(i, (i + distance) % size) for i in range(size)])  50.4 us
    all_gather x1, blocking collectives, body(): shards = lax.all_gather(shard, 'orbit')  27.5 us
    pallas_call x3, Pallas kernels, body(): call(step_kernel, (FIELD,) + SENT, 12, work=MATMUL)  22.3 us
    all_to_all x1, blocking collectives, body(): pairs = lax.all_to_all(pairs, ('lon', 'lat'), 0, 0, tiled=True)  16.7 us
    ppermute x4, starting transfers between devices, exchange(): south = lax.ppermute(up, 'lat', [(i, i + 1) for i in range(n_lat - 1)])  11.1 us
    pallas_call x1, Pallas kernels, body(): call(build_kernel, (shape(SPAN, 2 * CELL, SLOT, dtype=BF16), shape(SPAN,...  8.4 us
    ppermute x4, waiting for transfers between devices, exchange(): north = lax.ppermute(down, 'lat', [(i + 1, i) for i in range(n_lat - 1)])  8.12 us
    pallas_call x1, Pallas kernels, body(): call(init_kernel, (FIELD, mask_shape) + SENT, 7, work=MATMUL)  7.07 us
  transfers between devices with their start and end apart: 28, of which 8 were waited for; matrix products, arithmetic and copies ran while one was open for 0% of the time, Pallas kernels for 5%

profile of v3, /device:TPU:1, one launch (start us, length us, event | category | flops | bytes accessed | tf_op | source)
XLA Modules:
  0.0 168.4 jit_solution(8600343601435702825)
XLA Ops:
  1.9 27.5 %all-gather = f32[1344,128]{1,0:T(8,128)S(1)} all-gather(f32[168,128]{1,0:T(8,128)S(1)} %get-tuple-element.52), channel_id=2, replica_groups=mesh['orbit'=8,'lon'=16,'lat'=4] {'orbit'}, dimensions={0}, use_global_device_ids=true | all-gather | bytes 774144 | tf_op jit(solution)/shard_map/all_gather | solution.py:372
  29.3 3.2 %collective-permute-start.3 = (f32[8,1024]{1,0:T(8,128)S(1)}, f32[8,1024]{1,0:T(8,128)S(1)}, u32[]{:S(2)}, u32[]{:S(2)}) collective-permute-start(f32[8,1024]{1,0:T(8,128)S(1)} %shard_map.87.z2), channel_id=1, source_target_pairs={{0,8},{4,12},{8,16},{12,20},{16,24},{20,28},{24,32},{28,36},{32,40... | collective-permute-start | bytes 98312 | tf_op jit(solution)/shard_map/ppermute | solution.py:39
  32.5 7.7 %collective-permute-start.2 = (f32[8,1024]{1,0:T(8,128)S(1)}, f32[8,1024]{1,0:T(8,128)S(1)}, u32[]{:S(2)}, u32[]{:S(2)}) collective-permute-start(f32[8,1024]{1,0:T(8,128)S(1)} %shard_map.87.z2), channel_id=1, source_target_pairs={{0,4},{4,8},{8,12},{12,16},{16,20},{20,24},{24,28},{28,32},{32,36}... | collective-permute-start | bytes 98312 | tf_op jit(solution)/shard_map/ppermute | solution.py:39
  40.3 3.3 %collective-permute-start = (f32[8,1024]{1,0:T(8,128)S(1)}, f32[8,1024]{1,0:T(8,128)S(1)}, u32[]{:S(2)}, u32[]{:S(2)}) collective-permute-start(f32[8,1024]{1,0:T(8,128)S(1)} %shard_map.87.z2), channel_id=1, source_target_pairs={{0,56},{4,60},{8,0},{12,4},{16,8},{20,12},{24,16},{28,20},{32,24},... | collective-permute-start | bytes 98312 | tf_op jit(solution)/shard_map/ppermute | solution.py:39
  43.5 8.4 %shard_map.88 = (bf16[5,1024,1024]{2,1,0:T(8,128)(2,1)S(1)}, s32[5,8,1024]{2,1,0:T(8,128)S(1)}) custom-call(f32[8,168,128]{2,1,0:T(8,128)S(1)} %bitcast.11), custom_call_target="tpu_custom_call" | custom-call | flops 671088640 | bytes 20971520 | tf_op jit(solution)/shard_map/pallas_call | solution.py:376
  52.0 7.1 %shard_map.89 = (f32[64,512]{1,0:T(8,128)S(1)}, s32[5,8,1024]{2,1,0:T(8,128)S(1)}, f32[5,8,1024]{2,1,0:T(8,128)S(1)}, f32[5,8,1024]{2,1,0:T(8,128)S(1)}, f32[5,8...) custom-call(f32[8,1024]{1,0:T(8,128)S(1)} %shard_map.87.z2, ...), custom_call_target="tpu_custom_call" | custom-call | flops 1342177280 | bytes 10485760 | tf_op jit(solution)/shard_map/pallas_call | solution.py:378
  61.1 3.6 %collective-permute-start.6 = (f32[3,8,1024]{2,1,0:T(8,128)S(1)}, f32[3,8,1024]{2,1,0:T(8,128)S(1)}, u32[]{:S(2)}, u32[]{:S(2)}) collective-permute-start(f32[3,8,1024]{2,1,0:T(8,128)S(1)} %get-tuple-element.61), channel_id=1, source_target_pairs={{0,56},{4,60},{8,0},{12,4},{16,8},{20,12},{24,16},{28,20},{32,24},... | collective-permute-start | bytes 294920 | tf_op jit(solution)/shard_map/ppermute | solution.py:39
  64.8 1.9 %collective-permute-start.7 = (f32[3,8,1024]{2,1,0:T(8,128)S(1)}, f32[3,8,1024]{2,1,0:T(8,128)S(1)}, u32[]{:S(2)}, u32[]{:S(2)}) collective-permute-start(f32[3,8,1024]{2,1,0:T(8,128)S(1)} %get-tuple-element.62), channel_id=1, source_target_pairs={{0,8},{4,12},{8,16},{12,20},{16,24},{20,28},{24,32},{28,36},{32,40... | collective-permute-start | bytes 294920 | tf_op jit(solution)/shard_map/ppermute | solution.py:39
  66.7 3.1 %collective-permute-start.8 = (f32[8,512]{1,0:T(8,128)S(1)}, f32[8,512]{1,0:T(8,128)S(1)}, u32[]{:S(2)}, u32[]{:S(2)}) collective-permute-start(f32[8,512]{1,0:T(8,128)S(1)} %get-tuple-element.63), channel_id=1, source_target_pairs={{0,1},{1,2},{2,3},{4,5},{5,6},{6,7},{8,9},{9,10},{10,11},{12,13},{... | collective-permute-start | bytes 49160 | tf_op jit(solution)/shard_map/ppermute | solution.py:345
  72.4 2.0 %collective-permute-done.9.refs_7_ = f32[8,512]{1,0:T(8,128)S(1)} collective-permute-done((f32[8,512]{1,0:T(8,128)S(1)}, f32[8,512]{1,0:T(8,128)S(1)}, u32[]{:S(2)}, u32[]{:S(2)}) %collective-permute-start.9) | collective-permute-done | bytes 16416 | tf_op jit(solution)/shard_map/ppermute | solution.py:347
  74.3 7.5 %shard_map.90 = (f32[64,512]{1,0:T(8,128)S(1)}, f32[5,8,1024]{2,1,0:T(8,128)S(1)}, f32[5,8,1024]{2,1,0:T(8,128)S(1)}, f32[5,8,1024]{2,1,0:T(8,128)S(1)}, f32[3,8...) custom-call(f32[64,512]{1,0:T(8,128)S(1)} %get-tuple-element.55.refs_0_.refs_12_.re, ...), custom_call_target="tpu_custom_call" | custom-call | flops 1342177280 | bytes 10485760 | tf_op jit(solution)/shard_map/pallas_call | solution.py:381
  84.0 5.3 %collective-permute-start.12 = (f32[3,8,1024]{2,1,0:T(8,128)S(1)}, f32[3,8,1024]{2,1,0:T(8,128)S(1)}, u32[]{:S(2)}, u32[]{:S(2)}) collective-permute-start(f32[3,8,1024]{2,1,0:T(8,128)S(1)} %get-tuple-element.74), channel_id=1, source_target_pairs={{0,56},{4,60},{8,0},{12,4},{16,8},{20,12},{24,16},{28,20},{32,24},... | collective-permute-start | bytes 294920 | tf_op jit(solution)/shard_map/ppermute | solution.py:39
  89.3 1.9 %collective-permute-start.13 = (f32[3,8,1024]{2,1,0:T(8,128)S(1)}, f32[3,8,1024]{2,1,0:T(8,128)S(1)}, u32[]{:S(2)}, u32[]{:S(2)}) collective-permute-start(f32[3,8,1024]{2,1,0:T(8,128)S(1)} %get-tuple-element.75), channel_id=1, source_target_pairs={{0,8},{4,12},{8,16},{12,20},{16,24},{20,28},{24,32},{28,36},{32,40... | collective-permute-start | bytes 294920 | tf_op jit(solution)/shard_map/ppermute | solution.py:39
  91.3 3.1 %collective-permute-start.14 = (f32[8,512]{1,0:T(8,128)S(1)}, f32[8,512]{1,0:T(8,128)S(1)}, u32[]{:S(2)}, u32[]{:S(2)}) collective-permute-start(f32[8,512]{1,0:T(8,128)S(1)} %get-tuple-element.76), channel_id=1, source_target_pairs={{0,1},{1,2},{2,3},{4,5},{5,6},{6,7},{8,9},{9,10},{10,11},{12,13},{... | collective-permute-start | bytes 49160 | tf_op jit(solution)/shard_map/ppermute | solution.py:345
  96.9 2.0 %collective-permute-done.15.refs_7_ = f32[8,512]{1,0:T(8,128)S(1)} collective-permute-done((f32[8,512]{1,0:T(8,128)S(1)}, f32[8,512]{1,0:T(8,128)S(1)}, u32[]{:S(2)}, u32[]{:S(2)}) %collective-permute-start.15) | collective-permute-done | bytes 16416 | tf_op jit(solution)/shard_map/ppermute | solution.py:347
  98.9 7.4 %shard_map.91 = (f32[64,512]{1,0:T(8,128)S(1)}, f32[5,8,1024]{2,1,0:T(8,128)S(1)}, f32[5,8,1024]{2,1,0:T(8,128)S(1)}, f32[5,8,1024]{2,1,0:T(8,128)S(1)}, f32[3,8...) custom-call(f32[64,512]{1,0:T(8,128)S(1)} %get-tuple-element.68.refs_0_.refs_13_.re, ...), custom_call_target="tpu_custom_call" | custom-call | flops 1342177280 | bytes 10485760 | tf_op jit(solution)/shard_map/pallas_call | solution.py:381
  108.1 5.8 %collective-permute-start.18 = (f32[3,8,1024]{2,1,0:T(8,128)S(1)}, f32[3,8,1024]{2,1,0:T(8,128)S(1)}, u32[]{:S(2)}, u32[]{:S(2)}) collective-permute-start(f32[3,8,1024]{2,1,0:T(8,128)S(1)} %get-tuple-element.84), channel_id=1, source_target_pairs={{0,56},{4,60},{8,0},{12,4},{16,8},{20,12},{24,16},{28,20},{32,24},... | collective-permute-start | bytes 294920 | tf_op jit(solution)/shard_map/ppermute | solution.py:39
  115.8 2.8 %collective-permute-start.20 = (f32[8,512]{1,0:T(8,128)S(1)}, f32[8,512]{1,0:T(8,128)S(1)}, u32[]{:S(2)}, u32[]{:S(2)}) collective-permute-start(f32[8,512]{1,0:T(8,128)S(1)} %get-tuple-element.86), channel_id=1, source_target_pairs={{0,1},{1,2},{2,3},{4,5},{5,6},{6,7},{8,9},{9,10},{10,11},{12,13},{... | collective-permute-start | bytes 49160 | tf_op jit(solution)/shard_map/ppermute | solution.py:345
  120.9 2.3 %collective-permute-done.21.refs_7_ = f32[8,512]{1,0:T(8,128)S(1)} collective-permute-done((f32[8,512]{1,0:T(8,128)S(1)}, f32[8,512]{1,0:T(8,128)S(1)}, u32[]{:S(2)}, u32[]{:S(2)}) %collective-permute-start.21) | collective-permute-done | bytes 16416 | tf_op jit(solution)/shard_map/ppermute | solution.py:347
  123.1 7.4 %shard_map.92 = (f32[64,512]{1,0:T(8,128)S(1)}, f32[5,8,1024]{2,1,0:T(8,128)S(1)}, f32[5,8,1024]{2,1,0:T(8,128)S(1)}, f32[5,8,1024]{2,1,0:T(8,128)S(1)}, f32[3,8...) custom-call(f32[64,512]{1,0:T(8,128)S(1)} %get-tuple-element.78.refs_0_.refs_14_.re, ...), custom_call_target="tpu_custom_call" | custom-call | flops 1342177280 | bytes 10485760 | tf_op jit(solution)/shard_map/pallas_call | solution.py:381
  132.4 6.1 %collective-permute-start.24 = (f32[3,8,1024]{2,1,0:T(8,128)S(1)}, f32[3,8,1024]{2,1,0:T(8,128)S(1)}, u32[]{:S(2)}, u32[]{:S(2)}) collective-permute-start(f32[3,8,1024]{2,1,0:T(8,128)S(1)} %get-tuple-element.94), channel_id=1, source_target_pairs={{0,56},{4,60},{8,0},{12,4},{16,8},{20,12},{24,16},{28,20},{32,24},... | collective-permute-start | bytes 294920 | tf_op jit(solution)/shard_map/ppermute | solution.py:39
  140.4 2.0 %collective-permute-start.26 = (f32[8,512]{1,0:T(8,128)S(1)}, f32[8,512]{1,0:T(8,128)S(1)}, u32[]{:S(2)}, u32[]{:S(2)}) collective-permute-start(f32[8,512]{1,0:T(8,128)S(1)} %get-tuple-element.96), channel_id=1, source_target_pairs={{0,1},{1,2},{2,3},{4,5},{5,6},{6,7},{8,9},{9,10},{10,11},{12,13},{... | collective-permute-start | bytes 49160 | tf_op jit(solution)/shard_map/ppermute | solution.py:345
  146.9 3.4 %shard_map.93 = (f32[64,512]{1,0:T(8,128)S(1)}, f32[64,128]{1,0:T(8,128)S(1)}) custom-call(f32[64,512]{1,0:T(8,128)S(1)} %get-tuple-element.88.refs_0_.refs_4_, f32[5,8,1024]{2,1,0:T(8,128)S(1)} %get-tuple-element.89.refs_1_, f32[5,8,1024]{2,1,0:T(8,128)S(1)} %collective-permute-done.22.refs_2_, f32[5,8,1024]{2,1,0:T(8,128)S(1)} %collective-permute-done.23.refs_3_, ...), custom_call_target="tpu_custom_call" | custom-call | flops 1342177280 | bytes 10485760 | tf_op jit(solution)/shard_map/pallas_call | solution.py:384
  150.3 16.7 %all_to_all.11 = f32[64,1,128]{2,1,0:T(1,128)S(1)} all-to-all(f32[64,1,128]{2,1,0:T(1,128)S(1)} %bitcast.13), channel_id=1, replica_groups=mesh['orbit'=8,'lon'=16,'lat'=4] {'lon','lat'}, dimensions={0} | all-to-all | bytes 65536 | tf_op jit(solution)/shard_map/all_to_all | solution.py:388
  (43 shorter events, 25.9 us)
Async XLA Ops:
  29.3 22.6 %collective-permute-start.3 = (f32[8,1024]{1,0:T(8,128)S(1)}, f32[8,1024]{1,0:T(8,128)S(1)}, u32[]{:S(2)}, u32[]{:S(2)}) collective-permute-start(f32[8,1024]{1,0:T(8,128)S(1)} %shard_map.87.z2), channel_id=1, source_target_pairs={{0,8},{4,12},{8,16},{12,20},{16,24},{20,28},{24,32},{28,36},{32,40... | collective-permute-start | bytes 98312 | tf_op jit(solution)/shard_map/ppermute | solution.py:39
  32.5 19.4 %collective-permute-start.2 = (f32[8,1024]{1,0:T(8,128)S(1)}, f32[8,1024]{1,0:T(8,128)S(1)}, u32[]{:S(2)}, u32[]{:S(2)}) collective-permute-start(f32[8,1024]{1,0:T(8,128)S(1)} %shard_map.87.z2), channel_id=1, source_target_pairs={{0,4},{4,8},{8,12},{12,16},{16,20},{20,24},{24,28},{28,32},{32,36}... | collective-permute-start | bytes 98312 | tf_op jit(solution)/shard_map/ppermute | solution.py:39
  40.2 11.7 %collective-permute-start.1 = (f32[8,1024]{1,0:T(8,128)S(1)}, f32[8,1024]{1,0:T(8,128)S(1)}, u32[]{:S(2)}, u32[]{:S(2)}) collective-permute-start(f32[8,1024]{1,0:T(8,128)S(1)} %shard_map.87.z2), channel_id=1, source_target_pairs={{0,60},{4,0},{8,4},{12,8},{16,12},{20,16},{24,20},{28,24},{32,28},... | collective-permute-start | bytes 98312 | tf_op jit(solution)/shard_map/ppermute | solution.py:39
  40.3 11.7 %collective-permute-start = (f32[8,1024]{1,0:T(8,128)S(1)}, f32[8,1024]{1,0:T(8,128)S(1)}, u32[]{:S(2)}, u32[]{:S(2)}) collective-permute-start(f32[8,1024]{1,0:T(8,128)S(1)} %shard_map.87.z2), channel_id=1, source_target_pairs={{0,56},{4,60},{8,0},{12,4},{16,8},{20,12},{24,16},{28,20},{32,24},... | collective-permute-start | bytes 98312 | tf_op jit(solution)/shard_map/ppermute | solution.py:39
  59.1 10.7 %collective-permute-start.4 = (f32[5,8,1024]{2,1,0:T(8,128)S(1)}, f32[5,8,1024]{2,1,0:T(8,128)S(1)}, u32[]{:S(2)}, u32[]{:S(2)}) collective-permute-start(f32[5,8,1024]{2,1,0:T(8,128)S(1)} %get-tuple-element.57), channel_id=1, source_target_pairs={{0,60},{4,0},{8,4},{12,8},{16,12},{20,16},{24,20},{28,24},{32,28},... | collective-permute-start | bytes 491528 | tf_op jit(solution)/shard_map/ppermute | solution.py:39
  60.2 12.2 %collective-permute-start.5 = (f32[5,8,1024]{2,1,0:T(8,128)S(1)}, f32[5,8,1024]{2,1,0:T(8,128)S(1)}, u32[]{:S(2)}, u32[]{:S(2)}) collective-permute-start(f32[5,8,1024]{2,1,0:T(8,128)S(1)} %get-tuple-element.60), channel_id=1, source_target_pairs={{0,4},{4,8},{8,12},{12,16},{16,20},{20,24},{24,28},{28,32},{32,36}... | collective-permute-start | bytes 491528 | tf_op jit(solution)/shard_map/ppermute | solution.py:39
  61.1 10.0 %collective-permute-start.6 = (f32[3,8,1024]{2,1,0:T(8,128)S(1)}, f32[3,8,1024]{2,1,0:T(8,128)S(1)}, u32[]{:S(2)}, u32[]{:S(2)}) collective-permute-start(f32[3,8,1024]{2,1,0:T(8,128)S(1)} %get-tuple-element.61), channel_id=1, source_target_pairs={{0,56},{4,60},{8,0},{12,4},{16,8},{20,12},{24,16},{28,20},{32,24},... | collective-permute-start | bytes 294920 | tf_op jit(solution)/shard_map/ppermute | solution.py:39
  64.8 7.6 %collective-permute-start.7 = (f32[3,8,1024]{2,1,0:T(8,128)S(1)}, f32[3,8,1024]{2,1,0:T(8,128)S(1)}, u32[]{:S(2)}, u32[]{:S(2)}) collective-permute-start(f32[3,8,1024]{2,1,0:T(8,128)S(1)} %get-tuple-element.62), channel_id=1, source_target_pairs={{0,8},{4,12},{8,16},{12,20},{16,24},{20,28},{24,32},{28,36},{32,40... | collective-permute-start | bytes 294920 | tf_op jit(solution)/shard_map/ppermute | solution.py:39
  69.8 4.5 %collective-permute-start.9 = (f32[8,512]{1,0:T(8,128)S(1)}, f32[8,512]{1,0:T(8,128)S(1)}, u32[]{:S(2)}, u32[]{:S(2)}) collective-permute-start(f32[8,512]{1,0:T(8,128)S(1)} %get-tuple-element.64), channel_id=1, source_target_pairs={{1,0},{2,1},{3,2},{5,4},{6,5},{7,6},{9,8},{10,9},{11,10},{13,12},{... | collective-permute-start | bytes 49160 | tf_op jit(solution)/shard_map/ppermute | solution.py:347
  81.8 12.6 %collective-permute-start.10 = (f32[5,8,1024]{2,1,0:T(8,128)S(1)}, f32[5,8,1024]{2,1,0:T(8,128)S(1)}, u32[]{:S(2)}, u32[]{:S(2)}) collective-permute-start(f32[5,8,1024]{2,1,0:T(8,128)S(1)} %get-tuple-element.70), channel_id=1, source_target_pairs={{0,60},{4,0},{8,4},{12,8},{16,12},{20,16},{24,20},{28,24},{32,28},... | collective-permute-start | bytes 491528 | tf_op jit(solution)/shard_map/ppermute | solution.py:39
  83.0 13.8 %collective-permute-start.11 = (f32[5,8,1024]{2,1,0:T(8,128)S(1)}, f32[5,8,1024]{2,1,0:T(8,128)S(1)}, u32[]{:S(2)}, u32[]{:S(2)}) collective-permute-start(f32[5,8,1024]{2,1,0:T(8,128)S(1)} %get-tuple-element.73), channel_id=1, source_target_pairs={{0,4},{4,8},{8,12},{12,16},{16,20},{20,24},{24,28},{28,32},{32,36}... | collective-permute-start | bytes 491528 | tf_op jit(solution)/shard_map/ppermute | solution.py:39
  84.0 11.9 %collective-permute-start.12 = (f32[3,8,1024]{2,1,0:T(8,128)S(1)}, f32[3,8,1024]{2,1,0:T(8,128)S(1)}, u32[]{:S(2)}, u32[]{:S(2)}) collective-permute-start(f32[3,8,1024]{2,1,0:T(8,128)S(1)} %get-tuple-element.74), channel_id=1, source_target_pairs={{0,56},{4,60},{8,0},{12,4},{16,8},{20,12},{24,16},{28,20},{32,24},... | collective-permute-start | bytes 294920 | tf_op jit(solution)/shard_map/ppermute | solution.py:39
  89.3 7.5 %collective-permute-start.13 = (f32[3,8,1024]{2,1,0:T(8,128)S(1)}, f32[3,8,1024]{2,1,0:T(8,128)S(1)}, u32[]{:S(2)}, u32[]{:S(2)}) collective-permute-start(f32[3,8,1024]{2,1,0:T(8,128)S(1)} %get-tuple-element.75), channel_id=1, source_target_pairs={{0,8},{4,12},{8,16},{12,20},{16,24},{20,28},{24,32},{28,36},{32,40... | collective-permute-start | bytes 294920 | tf_op jit(solution)/shard_map/ppermute | solution.py:39
  91.3 4.6 %collective-permute-start.14 = (f32[8,512]{1,0:T(8,128)S(1)}, f32[8,512]{1,0:T(8,128)S(1)}, u32[]{:S(2)}, u32[]{:S(2)}) collective-permute-start(f32[8,512]{1,0:T(8,128)S(1)} %get-tuple-element.76), channel_id=1, source_target_pairs={{0,1},{1,2},{2,3},{4,5},{5,6},{6,7},{8,9},{9,10},{10,11},{12,13},{... | collective-permute-start | bytes 49160 | tf_op jit(solution)/shard_map/ppermute | solution.py:345
  94.4 4.5 %collective-permute-start.15 = (f32[8,512]{1,0:T(8,128)S(1)}, f32[8,512]{1,0:T(8,128)S(1)}, u32[]{:S(2)}, u32[]{:S(2)}) collective-permute-start(f32[8,512]{1,0:T(8,128)S(1)} %get-tuple-element.77), channel_id=1, source_target_pairs={{1,0},{2,1},{3,2},{5,4},{6,5},{7,6},{9,8},{10,9},{11,10},{13,12},{... | collective-permute-start | bytes 49160 | tf_op jit(solution)/shard_map/ppermute | solution.py:347
  106.3 12.3 %collective-permute-start.16 = (f32[5,8,1024]{2,1,0:T(8,128)S(1)}, f32[5,8,1024]{2,1,0:T(8,128)S(1)}, u32[]{:S(2)}, u32[]{:S(2)}) collective-permute-start(f32[5,8,1024]{2,1,0:T(8,128)S(1)} %get-tuple-element.80), channel_id=1, source_target_pairs={{0,60},{4,0},{8,4},{12,8},{16,12},{20,16},{24,20},{28,24},{32,28},... | collective-permute-start | bytes 491528 | tf_op jit(solution)/shard_map/ppermute | solution.py:39
  107.2 13.6 %collective-permute-start.17 = (f32[5,8,1024]{2,1,0:T(8,128)S(1)}, f32[5,8,1024]{2,1,0:T(8,128)S(1)}, u32[]{:S(2)}, u32[]{:S(2)}) collective-permute-start(f32[5,8,1024]{2,1,0:T(8,128)S(1)} %get-tuple-element.83), channel_id=1, source_target_pairs={{0,4},{4,8},{8,12},{12,16},{16,20},{20,24},{24,28},{28,32},{32,36}... | collective-permute-start | bytes 491528 | tf_op jit(solution)/shard_map/ppermute | solution.py:39
  108.1 11.9 %collective-permute-start.18 = (f32[3,8,1024]{2,1,0:T(8,128)S(1)}, f32[3,8,1024]{2,1,0:T(8,128)S(1)}, u32[]{:S(2)}, u32[]{:S(2)}) collective-permute-start(f32[3,8,1024]{2,1,0:T(8,128)S(1)} %get-tuple-element.84), channel_id=1, source_target_pairs={{0,56},{4,60},{8,0},{12,4},{16,8},{20,12},{24,16},{28,20},{32,24},... | collective-permute-start | bytes 294920 | tf_op jit(solution)/shard_map/ppermute | solution.py:39
  113.9 7.0 %collective-permute-start.19 = (f32[3,8,1024]{2,1,0:T(8,128)S(1)}, f32[3,8,1024]{2,1,0:T(8,128)S(1)}, u32[]{:S(2)}, u32[]{:S(2)}) collective-permute-start(f32[3,8,1024]{2,1,0:T(8,128)S(1)} %get-tuple-element.85), channel_id=1, source_target_pairs={{0,8},{4,12},{8,16},{12,20},{16,24},{20,28},{24,32},{28,36},{32,40... | collective-permute-start | bytes 294920 | tf_op jit(solution)/shard_map/ppermute | solution.py:39
  118.7 4.5 %collective-permute-start.21 = (f32[8,512]{1,0:T(8,128)S(1)}, f32[8,512]{1,0:T(8,128)S(1)}, u32[]{:S(2)}, u32[]{:S(2)}) collective-permute-start(f32[8,512]{1,0:T(8,128)S(1)} %get-tuple-element.87), channel_id=1, source_target_pairs={{1,0},{2,1},{3,2},{5,4},{6,5},{7,6},{9,8},{10,9},{11,10},{13,12},{... | collective-permute-start | bytes 49160 | tf_op jit(solution)/shard_map/ppermute | solution.py:347
  130.6 11.8 %collective-permute-start.22 = (f32[5,8,1024]{2,1,0:T(8,128)S(1)}, f32[5,8,1024]{2,1,0:T(8,128)S(1)}, u32[]{:S(2)}, u32[]{:S(2)}) collective-permute-start(f32[5,8,1024]{2,1,0:T(8,128)S(1)} %get-tuple-element.90), channel_id=1, source_target_pairs={{0,60},{4,0},{8,4},{12,8},{16,12},{20,16},{24,20},{28,24},{32,28},... | collective-permute-start | bytes 491528 | tf_op jit(solution)/shard_map/ppermute | solution.py:39
  131.5 13.5 %collective-permute-start.23 = (f32[5,8,1024]{2,1,0:T(8,128)S(1)}, f32[5,8,1024]{2,1,0:T(8,128)S(1)}, u32[]{:S(2)}, u32[]{:S(2)}) collective-permute-start(f32[5,8,1024]{2,1,0:T(8,128)S(1)} %get-tuple-element.93), channel_id=1, source_target_pairs={{0,4},{4,8},{8,12},{12,16},{16,20},{20,24},{24,28},{28,32},{32,36}... | collective-permute-start | bytes 491528 | tf_op jit(solution)/shard_map/ppermute | solution.py:39
  132.4 11.6 %collective-permute-start.24 = (f32[3,8,1024]{2,1,0:T(8,128)S(1)}, f32[3,8,1024]{2,1,0:T(8,128)S(1)}, u32[]{:S(2)}, u32[]{:S(2)}) collective-permute-start(f32[3,8,1024]{2,1,0:T(8,128)S(1)} %get-tuple-element.94), channel_id=1, source_target_pairs={{0,56},{4,60},{8,0},{12,4},{16,8},{20,12},{24,16},{28,20},{32,24},... | collective-permute-start | bytes 294920 | tf_op jit(solution)/shard_map/ppermute | solution.py:39
  138.4 6.6 %collective-permute-start.25 = (f32[3,8,1024]{2,1,0:T(8,128)S(1)}, f32[3,8,1024]{2,1,0:T(8,128)S(1)}, u32[]{:S(2)}, u32[]{:S(2)}) collective-permute-start(f32[3,8,1024]{2,1,0:T(8,128)S(1)} %get-tuple-element.95), channel_id=1, source_target_pairs={{0,8},{4,12},{8,16},{12,20},{16,24},{20,28},{24,32},{28,36},{32,40... | collective-permute-start | bytes 294920 | tf_op jit(solution)/shard_map/ppermute | solution.py:39
  (4 other events, 16.6 us)

commit v4 on v3

--- a/solution.py
+++ b/solution.py
@@ -18,7 +18,7 @@
 SLOT = ORB * RAYS
 CELL = CLON * LEV
 CHAN = 64
-SHARD = SPAN * 2 * TILE + 8
+TABLE = SPAN * 2 * TILE
 F32 = jnp.float32
 BF16 = jnp.bfloat16
 highest = lax.Precision.HIGHEST
@@ -45,30 +45,45 @@
     return high, low
 
 
-def start_kernel(*refs):
-    sources, outs, places, sem = refs[:7], refs[7:11], refs[11:18], refs[18]
+def fetch(sources, places, sem):
     copies = [pltpu.make_async_copy(src, dst, sem.at[n]) for n, (src, dst) in enumerate(zip(sources, places))]
     for copy in copies:
         copy.start()
     for copy in copies:
         copy.wait()
-    prior_ref, obs_ref, start_ref, cells_ref, lengths_ref, kern_ref, noise_ref = places
-    shard_ref, gram_ref, prior_out, scale_out = outs
-    for slot in range(SPAN):
-        lanes = slice(slot * RAYS, (slot + 1) * RAYS)
-        base = slot * 2 * TILE
-        shard_ref[base:base + TILE, :] = cells_ref[:, lanes].astype(F32)
-        shard_ref[base + TILE:base + 2 * TILE, :] = lengths_ref[:, lanes]
+
+
+def source_kernel(*refs):
+    sources, source_ref, places, sem = refs[:4], refs[4], refs[5:9], refs[9]
+    fetch(sources, places, sem)
+    obs_ref, start_ref, kern_ref, noise_ref = places
+    kern = species_rows(kern_ref)
+    source = jnp.dot(kern * noise_ref[...], obs_ref[...], precision=highest, preferred_element_type=F32)
+    sub = lax.broadcasted_iota(jnp.int32, (8, RAYS), 0)
+    start = jnp.broadcast_to(start_ref[...].astype(F32), (8, RAYS))
+    source_ref[...] = jnp.where(sub == S, start, source)
+
+
+def species_rows(kern_ref):
     sub = lax.broadcasted_iota(jnp.int32, (8, CHAN), 0)
     kern = jnp.zeros((8, CHAN), F32)
     for s in range(S):
         kern = jnp.where(sub == s, kern_ref[s:s + 1, :], kern)
+    return kern
+
+
+def table_kernel(*refs):
+    sources, outs, places, sem = refs[:5], refs[5:9], refs[9:14], refs[14]
+    fetch(sources, places, sem)
+    prior_ref, cells_ref, lengths_ref, kern_ref, noise_ref = places
+    table_ref, gram_ref, prior_out, scale_out = outs
+    for slot in range(SPAN):
+        lanes = slice(slot * RAYS, (slot + 1) * RAYS)
+        base = slot * 2 * TILE
+        table_ref[base:base + TILE, :] = cells_ref[:, lanes].astype(F32)
+        table_ref[base + TILE:base + 2 * TILE, :] = lengths_ref[:, lanes]
+    kern = species_rows(kern_ref)
     weighted = kern * noise_ref[...]
-    source = jnp.dot(weighted, obs_ref[...], precision=highest, preferred_element_type=F32)
-    base = SPAN * 2 * TILE
-    sub = lax.broadcasted_iota(jnp.int32, (8, RAYS), 0)
-    start = jnp.broadcast_to(start_ref[...].astype(F32), (8, RAYS))
-    shard_ref[base:base + 8, :] = jnp.where(sub == S, start, source)
     wide = jnp.concatenate([kern] * CLAT, axis=0)
     wide_weighted = jnp.concatenate([weighted] * CLAT, axis=0)
     gram = lax.dot_general(wide_weighted, wide, (((1,), (1,)), ((), ())), precision=highest, preferred_element_type=F32)
@@ -87,12 +102,6 @@
     for s in range(S):
         prior = jnp.where(species == s, prior_ref[s], prior)
     prior_out[...] = prior * scale[0:1, 0:1]
-
-
-def gather_kernel(shards, out):
-    base = SPAN * 2 * TILE
-    for k in range(ORB):
-        out[:, k * RAYS:(k + 1) * RAYS] = shards[k, base:base + 8, :]
 
 
 def build_kernel(shards, w_ref, lat_ref):
@@ -155,8 +164,8 @@
     return total[:64] + total[64:]
 
 
-def project_all(v, lats, w_ref, outs):
-    own_ref, left_ref, right_ref, left2_ref, right2_ref, down_ref, up_ref = outs
+def project_kernel(v_ref, mask_ref, w_ref, own_ref, left_ref, right_ref, left2_ref, right2_ref, down_ref, up_ref):
+    v = v_ref[...]
     down_ref[...] = v[0:8]
     up_ref[...] = v[56:64]
     for l in range(CLAT):
@@ -167,7 +176,7 @@
     for slot in range(SPAN):
         wide = jnp.dot(rows, w_ref[slot], preferred_element_type=F32)
         wide = wide[:64] + wide[64:]
-        lat = lats[slot]
+        lat = mask_ref[slot]
         total = jnp.where(lat == 0, wide[0:8], 0.0)
         for l in range(1, CLAT):
             total = total + jnp.where(lat == l, wide[8 * l:8 * l + 8], 0.0)
@@ -182,19 +191,19 @@
             right2_ref[slot] = total
 
 
-def init_kernel(z2, z0, z1, z3, z4, lat_ref, w_ref, v_ref, mask_ref, *outs):
+def init_kernel(shards, lat_ref, w_ref, v_ref, mask_ref):
     sums, lats = [], []
     sub = lax.broadcasted_iota(jnp.int32, (8, SLOT), 0)
-    for slot, z in enumerate((z0, z1, z2, z3, z4)):
+    for slot in range(SPAN):
+        base = TABLE + 8 * slot
+        z = jnp.concatenate([shards[k, base:base + 8, :] for k in range(ORB)], axis=1)
         begin = jnp.broadcast_to(z[S:S + 1, :], (8, SLOT))
         present = (begin <= slot) & (begin + (NT - 1) >= slot)
         lat = jnp.where(present, lat_ref[slot], -1)
         mask_ref[slot] = lat
         lats.append(lat)
-        sums.append(jnp.where(sub < S, z[...], 0.0))
-    v = back_all(sums, lats, w_ref)
-    v_ref[...] = v
-    project_all(v, lats, w_ref, outs)
+        sums.append(jnp.where(sub < S, z, 0.0))
+    v_ref[...] = back_all(sums, lats, w_ref)
 
 
 def ray_sums(own_ref, plus1, minus1, plus2, minus2):
@@ -238,9 +247,7 @@
 
 def step_kernel(*refs):
     lats = [refs[8][slot] for slot in range(SPAN)]
-    v = next_vector(*refs[:8], lats, *refs[9:12])
-    refs[12][...] = v
-    project_all(v, lats, refs[9], refs[13:])
+    refs[12][...] = next_vector(*refs[:8], lats, *refs[9:12])
 
 
 PAIRS = [(i, j) for i in range(ITERS) for j in range(i, ITERS)] + [(ITERS - 1, ITERS)]
@@ -348,38 +355,49 @@
     return own, plus1, minus1, plus2, minus2, south, north
 
 
+def fetching(kernel, outs, scratch, values):
+    return pl.pallas_call(
+        kernel,
+        out_shape=outs,
+        in_specs=[pl.BlockSpec(memory_space=pltpu.HBM)] * len(values),
+        out_specs=[vspec()] * len(outs),
+        scratch_shapes=list(scratch) + [pltpu.SemaphoreType.DMA((len(values),))],
+        compiler_params=LIMIT,
+    )(*[pltpu.with_memory_space_constraint(value, pltpu.HBM) for value in values])
+
+
 def body(observed, ray_start, tile_cells, tile_lengths, channel_kernel, noise_weight, prior_weight):
-    shard, gram, prior, scale = pl.pallas_call(
-        start_kernel,
-        out_shape=(shape(SHARD, RAYS), shape(64, 64), shape(64, LEV), shape(8, LEV)),
-        in_specs=[pl.BlockSpec(memory_space=pltpu.HBM)] * 7,
-        out_specs=[vspec()] * 4,
-        scratch_shapes=[
+    noise = noise_weight.reshape(1, CHAN)
+    kern_space, noise_space = pltpu.VMEM((S, CHAN), F32), pltpu.VMEM((1, CHAN), F32)
+    (z,) = fetching(
+        source_kernel,
+        (shape(8, RAYS),),
+        (pltpu.VMEM((CHAN, RAYS), F32), pltpu.VMEM((1, RAYS), jnp.int32), kern_space, noise_space),
+        (observed.T, ray_start.reshape(1, RAYS), channel_kernel, noise),
+    )
+    z1, z3 = shift(z, "lon", -1), shift(z, "lon", 1)
+    z0, z4 = shift(z, "lon", -2), shift(z, "lon", 2)
+    table, gram, prior, scale = fetching(
+        table_kernel,
+        (shape(TABLE, RAYS), shape(64, 64), shape(64, LEV), shape(8, LEV)),
+        (
             pltpu.SMEM((S,), F32),
-            pltpu.VMEM((CHAN, RAYS), F32),
-            pltpu.VMEM((1, RAYS), jnp.int32),
             pltpu.VMEM((TILE, SPAN * RAYS), jnp.int32),
             pltpu.VMEM((TILE, SPAN * RAYS), F32),
-            pltpu.VMEM((S, CHAN), F32),
-            pltpu.VMEM((1, CHAN), F32),
-            pltpu.SemaphoreType.DMA((7,)),
-        ],
-        compiler_params=LIMIT,
-    )(*[
-        pltpu.with_memory_space_constraint(value, pltpu.HBM)
-        for value in (prior_weight, observed.T, ray_start.reshape(1, RAYS), tile_cells.T, tile_lengths.T, channel_kernel, noise_weight.reshape(1, -1))
-    ])
-    shards = lax.all_gather(shard, "orbit")
-    (z,) = call(gather_kernel, (shape(8, SLOT),), 1)(shards)
-    z1, z3 = shift(z, "lon", -1), shift(z, "lon", 1)
-    z0, z4 = shift(z, "lon", -2), shift(z, "lon", 2)
+            kern_space,
+            noise_space,
+        ),
+        (prior_weight, tile_cells.T, tile_lengths.T, channel_kernel, noise),
+    )
+    shards = lax.all_gather(jnp.concatenate([table, z0, z1, z, z3, z4], axis=0), "orbit")
     w, lat = call(build_kernel, (shape(SPAN, 2 * CELL, SLOT, dtype=BF16), shape(SPAN, 8, SLOT, dtype=jnp.int32)), 1, work=BUILD)(shards)
-    mask_shape = shape(SPAN, 8, SLOT, dtype=jnp.int32)
-    v, mask, *sent = call(init_kernel, (FIELD, mask_shape) + SENT, 7, work=MATMUL)(z, z0, z1, z3, z4, lat, w)
+    v, mask = call(init_kernel, (FIELD, shape(SPAN, 8, SLOT, dtype=jnp.int32)), 3, work=MATMUL)(shards, lat, w)
     vectors = [v]
+    sent = call(project_kernel, SENT, 3, work=MATMUL)(v, mask, w)
     for turn in range(ITERS - 1):
-        v, *sent = call(step_kernel, (FIELD,) + SENT, 12, work=MATMUL)(v, *exchange(*sent), mask, w, gram, prior)
+        (v,) = call(step_kernel, (FIELD,), 12, work=MATMUL)(v, *exchange(*sent), mask, w, gram, prior)
         vectors.append(v)
+        sent = call(project_kernel, SENT, 3, work=MATMUL)(v, mask, w)
     peers = lax.axis_size("lon") * lax.axis_size("lat")
     v, pairs = call(last_kernel, (FIELD, shape(peers, LEV)), 12 + ITERS - 1, work=MATMUL)(
         v, *exchange(*sent), mask, w, gram, prior, *vectors[:-1]

time: 169 us -> 161 us (0.953)
  Pallas kernels: 43.9 us -> 34.3 us
  starting transfers between devices: 67.1 us -> 72.6 us
  blocking collectives: 44.2 us -> 40.1 us
    pallas_call x6 -> x10, Pallas kernels: 30.7 us -> 21.1 us  [the longest x3 9.91 us: body(): call(step_kernel, (FIELD,), 12, work=MATMUL)]
    ppermute x20, starting transfers between devices: 50.4 us -> 56.7 us  [shift(): lax.ppermute(block, axis, [(i, (i + distance) % size) for i in range(size)])]
    all_gather x1, blocking collectives: 27.5 us -> 23.3 us  [body(): lax.all_gather(jnp.concatenate([table, z0, z1, z, z3, z4], axis=0), 'orbit')]
  transfers between devices with their start and end apart: 28 -> 28, of which waited for: 8 -> 8; matrix products, arithmetic and copies ran while one was open for 0% -> 0% of each run, Pallas kernels for 5% -> 1%
where the time goes in v4:
time: 161 us
  starting transfers between devices  72.6 us (45%)
  blocking collectives  40.1 us (25%)
  Pallas kernels  34.3 us (21%)
  waiting for transfers between devices  12.5 us (8%)
    ppermute x20, starting transfers between devices, shift(): lax.ppermute(block, axis, [(i, (i + distance) % size) for i in range(size)])  56.7 us
    all_gather x1, blocking collectives, body(): lax.all_gather(jnp.concatenate([table, z0, z1, z, z3, z4], axis=0), 'orbit')  23.3 us
    all_to_all x1, blocking collectives, body(): pairs = lax.all_to_all(pairs, ('lon', 'lat'), 0, 0, tiled=True)  16.8 us
    ppermute x4, starting transfers between devices, exchange(): south = lax.ppermute(up, 'lat', [(i, i + 1) for i in range(n_lat - 1)])  10.5 us
    pallas_call x3, Pallas kernels, body(): call(step_kernel, (FIELD,), 12, work=MATMUL)  9.91 us
    pallas_call x1, Pallas kernels, body(): call(build_kernel, (shape(SPAN, 2 * CELL, SLOT, dtype=BF16), shape(SPAN,...  8.4 us
    ppermute x4, waiting for transfers between devices, exchange(): north = lax.ppermute(down, 'lat', [(i + 1, i) for i in range(n_lat - 1)])  7.25 us
    pallas_call x4, Pallas kernels, body(): sent = call(project_kernel, SENT, 3, work=MATMUL)(v, mask, w)  6.18 us
  transfers between devices with their start and end apart: 28, of which 8 were waited for; matrix products, arithmetic and copies ran while one was open for 0% of the time, Pallas kernels for 1%

profile of v4, /device:TPU:1, one launch (start us, length us, event | category | flops | bytes accessed | tf_op | source)
XLA Modules:
  0.0 160.6 jit_solution(15079939252056602485)
XLA Ops:
  1.6 4.0 %collective-permute-start.3 = (f32[8,128]{1,0:T(8,128)S(1)}, f32[8,128]{1,0:T(8,128)S(1)}, u32[]{:S(2)}, u32[]{:S(2)}) collective-permute-start(f32[8,128]{1,0:T(8,128)S(1)} %shard_map.87), channel_id=1, source_target_pairs={{0,8},{4,12},{8,16},{12,20},{16,24},{20,28},{24,32},{28,36},{32,40... | collective-permute-start | bytes 12296 | tf_op jit(solution)/shard_map/ppermute | solution.py:39
  5.6 2.1 %collective-permute-start.2 = (f32[8,128]{1,0:T(8,128)S(1)}, f32[8,128]{1,0:T(8,128)S(1)}, u32[]{:S(2)}, u32[]{:S(2)}) collective-permute-start(f32[8,128]{1,0:T(8,128)S(1)} %shard_map.87), channel_id=1, source_target_pairs={{0,4},{4,8},{8,12},{12,16},{16,20},{20,24},{24,28},{28,32},{32,36}... | collective-permute-start | bytes 12296 | tf_op jit(solution)/shard_map/ppermute | solution.py:39
  7.8 2.7 %collective-permute-start.1 = (f32[8,128]{1,0:T(8,128)S(1)}, f32[8,128]{1,0:T(8,128)S(1)}, u32[]{:S(2)}, u32[]{:S(2)}) collective-permute-start(f32[8,128]{1,0:T(8,128)S(1)} %shard_map.87), channel_id=1, source_target_pairs={{0,60},{4,0},{8,4},{12,8},{16,12},{20,16},{24,20},{28,24},{32,28},... | collective-permute-start | bytes 12296 | tf_op jit(solution)/shard_map/ppermute | solution.py:39
  10.4 4.8 %collective-permute-start = (f32[8,128]{1,0:T(8,128)S(1)}, f32[8,128]{1,0:T(8,128)S(1)}, u32[]{:S(2)}, u32[]{:S(2)}) collective-permute-start(f32[8,128]{1,0:T(8,128)S(1)} %shard_map.87), channel_id=1, source_target_pairs={{0,56},{4,60},{8,0},{12,4},{16,8},{20,12},{24,16},{28,20},{32,24},... | collective-permute-start | bytes 12296 | tf_op jit(solution)/shard_map/ppermute | solution.py:39
  16.6 23.3 %all-gather = f32[1600,128]{1,0:T(8,128)S(1)} all-gather(f32[200,128]{1,0:T(8,128)S(1)} %constant_dynamic-update-slice_fusion), channel_id=2, replica_groups=mesh['orbit'=8,'lon'=16,'lat'=4] {'orbit'}, dimensions={0}, use_global_device_ids=true | all-gather | bytes 921600 | tf_op jit(solution)/shard_map/all_gather | solution.py:392
  39.9 8.4 %shard_map.88 = (bf16[5,1024,1024]{2,1,0:T(8,128)(2,1)S(1)}, s32[5,8,1024]{2,1,0:T(8,128)S(1)}) custom-call(f32[8,200,128]{2,1,0:T(8,128)S(1)} %bitcast.10), custom_call_target="tpu_custom_call" | custom-call | flops 671088640 | bytes 20971520 | tf_op jit(solution)/shard_map/pallas_call | solution.py:393
  48.3 2.9 %shard_map.89 = (f32[64,512]{1,0:T(8,128)S(1)}, s32[5,8,1024]{2,1,0:T(8,128)S(1)}) custom-call(f32[8,200,128]{2,1,0:T(8,128)S(1)} %bitcast.11, s32[5,8,1024]{2,1,0:T(8,128)S(1)} %get-tuple-element.50.lat_ref, bf16[5,1024,1024]{2,1,0:T(8,128)(2,1)S(1)} %get-tuple-element.51.w_ref.refs_9_), custom_call_target="tpu_custom_call" | custom-call | flops 1342177280 | bytes 10485760 | tf_op jit(solution)/shard_map/pallas_call | solution.py:394
  52.8 7.9 %collective-permute-start.4 = (f32[5,8,1024]{2,1,0:T(8,128)S(1)}, f32[5,8,1024]{2,1,0:T(8,128)S(1)}, u32[]{:S(2)}, u32[]{:S(2)}) collective-permute-start(f32[5,8,1024]{2,1,0:T(8,128)S(1)} %get-tuple-element.55), channel_id=1, source_target_pairs={{0,60},{4,0},{8,4},{12,8},{16,12},{20,16},{24,20},{28,24},{32,28},... | collective-permute-start | bytes 491528 | tf_op jit(solution)/shard_map/ppermute | solution.py:39
  60.6 4.5 %collective-permute-start.6 = (f32[3,8,1024]{2,1,0:T(8,128)S(1)}, f32[3,8,1024]{2,1,0:T(8,128)S(1)}, u32[]{:S(2)}, u32[]{:S(2)}) collective-permute-start(f32[3,8,1024]{2,1,0:T(8,128)S(1)} %get-tuple-element.59), channel_id=1, source_target_pairs={{0,56},{4,60},{8,0},{12,4},{16,8},{20,12},{24,16},{28,20},{32,24},... | collective-permute-start | bytes 294920 | tf_op jit(solution)/shard_map/ppermute | solution.py:39
  65.1 1.9 %collective-permute-start.7 = (f32[3,8,1024]{2,1,0:T(8,128)S(1)}, f32[3,8,1024]{2,1,0:T(8,128)S(1)}, u32[]{:S(2)}, u32[]{:S(2)}) collective-permute-start(f32[3,8,1024]{2,1,0:T(8,128)S(1)} %get-tuple-element.60), channel_id=1, source_target_pairs={{0,8},{4,12},{8,16},{12,20},{16,24},{20,28},{24,32},{28,36},{32,40... | collective-permute-start | bytes 294920 | tf_op jit(solution)/shard_map/ppermute | solution.py:39
  67.1 3.1 %collective-permute-start.8 = (f32[8,512]{1,0:T(8,128)S(1)}, f32[8,512]{1,0:T(8,128)S(1)}, u32[]{:S(2)}, u32[]{:S(2)}) collective-permute-start(f32[8,512]{1,0:T(8,128)S(1)} %get-tuple-element.61), channel_id=1, source_target_pairs={{0,1},{1,2},{2,3},{4,5},{5,6},{6,7},{8,9},{9,10},{10,11},{12,13},{... | collective-permute-start | bytes 49160 | tf_op jit(solution)/shard_map/ppermute | solution.py:352
  74.7 3.3 %shard_map.91.v_ref.refs_0_.refs_13_.refs_2_ = f32[64,512]{1,0:T(8,128)S(1)} custom-call(f32[64,512]{1,0:T(8,128)S(1)} %get-tuple-element.52.v_ref.refs_0_.refs_12_.refs_1_, f32[5,8,1024]{2,1,0:T(8,128)S(1)} %get-tuple-element.54.refs_1_, f32[5,8,1024]{2,1,0:T(8,128)S(1)} %collective-permute-done.4.refs_2_, ...), custom_call_target="tpu_custom_call" | custom-call | flops 1342177280 | bytes 10485760 | tf_op jit(solution)/shard_map/pallas_call | solution.py:398
  81.5 5.6 %collective-permute-start.12 = (f32[3,8,1024]{2,1,0:T(8,128)S(1)}, f32[3,8,1024]{2,1,0:T(8,128)S(1)}, u32[]{:S(2)}, u32[]{:S(2)}) collective-permute-start(f32[3,8,1024]{2,1,0:T(8,128)S(1)} %get-tuple-element.70), channel_id=1, source_target_pairs={{0,56},{4,60},{8,0},{12,4},{16,8},{20,12},{24,16},{28,20},{32,24},... | collective-permute-start | bytes 294920 | tf_op jit(solution)/shard_map/ppermute | solution.py:39
  87.1 1.9 %collective-permute-start.13 = (f32[3,8,1024]{2,1,0:T(8,128)S(1)}, f32[3,8,1024]{2,1,0:T(8,128)S(1)}, u32[]{:S(2)}, u32[]{:S(2)}) collective-permute-start(f32[3,8,1024]{2,1,0:T(8,128)S(1)} %get-tuple-element.71), channel_id=1, source_target_pairs={{0,8},{4,12},{8,16},{12,20},{16,24},{20,28},{24,32},{28,36},{32,40... | collective-permute-start | bytes 294920 | tf_op jit(solution)/shard_map/ppermute | solution.py:39
  89.0 3.1 %collective-permute-start.14 = (f32[8,512]{1,0:T(8,128)S(1)}, f32[8,512]{1,0:T(8,128)S(1)}, u32[]{:S(2)}, u32[]{:S(2)}) collective-permute-start(f32[8,512]{1,0:T(8,128)S(1)} %get-tuple-element.72), channel_id=1, source_target_pairs={{0,1},{1,2},{2,3},{4,5},{5,6},{6,7},{8,9},{9,10},{10,11},{12,13},{... | collective-permute-start | bytes 49160 | tf_op jit(solution)/shard_map/ppermute | solution.py:352
  96.6 3.3 %shard_map.93.v_ref.refs_0_.refs_14_.refs_3_ = f32[64,512]{1,0:T(8,128)S(1)} custom-call(f32[64,512]{1,0:T(8,128)S(1)} %shard_map.91.v_ref.refs_0_.refs_13_.refs_2_, f32[5,8,1024]{2,1,0:T(8,128)S(1)} %get-tuple-element.65.refs_1_, f32[5,8,1024]{2,1,0:T(8,128)S(1)} %collective-permute-done.10.refs_2_, f32[5,8,1024]{2,1,0:T(8,128)S(1)} %collective-permute-done.11.refs_3_, ...), custom_call_target="tpu_custom_call" | custom-call | flops 1342177280 | bytes 10485760 | tf_op jit(solution)/shard_map/pallas_call | solution.py:398
  103.3 5.8 %collective-permute-start.18 = (f32[3,8,1024]{2,1,0:T(8,128)S(1)}, f32[3,8,1024]{2,1,0:T(8,128)S(1)}, u32[]{:S(2)}, u32[]{:S(2)}) collective-permute-start(f32[3,8,1024]{2,1,0:T(8,128)S(1)} %get-tuple-element.79), channel_id=1, source_target_pairs={{0,56},{4,60},{8,0},{12,4},{16,8},{20,12},{24,16},{28,20},{32,24},... | collective-permute-start | bytes 294920 | tf_op jit(solution)/shard_map/ppermute | solution.py:39
  109.0 1.9 %collective-permute-start.19 = (f32[3,8,1024]{2,1,0:T(8,128)S(1)}, f32[3,8,1024]{2,1,0:T(8,128)S(1)}, u32[]{:S(2)}, u32[]{:S(2)}) collective-permute-start(f32[3,8,1024]{2,1,0:T(8,128)S(1)} %get-tuple-element.80), channel_id=1, source_target_pairs={{0,8},{4,12},{8,16},{12,20},{16,24},{20,28},{24,32},{28,36},{32,40... | collective-permute-start | bytes 294920 | tf_op jit(solution)/shard_map/ppermute | solution.py:39
  111.0 2.8 %collective-permute-start.20 = (f32[8,512]{1,0:T(8,128)S(1)}, f32[8,512]{1,0:T(8,128)S(1)}, u32[]{:S(2)}, u32[]{:S(2)}) collective-permute-start(f32[8,512]{1,0:T(8,128)S(1)} %get-tuple-element.81), channel_id=1, source_target_pairs={{0,1},{1,2},{2,3},{4,5},{5,6},{6,7},{8,9},{9,10},{10,11},{12,13},{... | collective-permute-start | bytes 49160 | tf_op jit(solution)/shard_map/ppermute | solution.py:352
  116.1 2.2 %collective-permute-done.21.refs_7_ = f32[8,512]{1,0:T(8,128)S(1)} collective-permute-done((f32[8,512]{1,0:T(8,128)S(1)}, f32[8,512]{1,0:T(8,128)S(1)}, u32[]{:S(2)}, u32[]{:S(2)}) %collective-permute-start.21) | collective-permute-done | bytes 16416 | tf_op jit(solution)/shard_map/ppermute | solution.py:354
  118.3 3.3 %shard_map.95.v_ref.refs_0_.refs_4_ = f32[64,512]{1,0:T(8,128)S(1)} custom-call(f32[64,512]{1,0:T(8,128)S(1)} %shard_map.93.v_ref.refs_0_.refs_14_.refs_3_, f32[5,8,1024]{2,1,0:T(8,128)S(1)} %get-tuple-element.74.refs_1_, f32[5,8,1024]{2,1,0:T(8,128)S(1)} %collective-permute-done.16.refs_2_, f32[5,8,1024]{2,1,0:T(8,128)S(1)} %collective-permute-done.17.refs_3_, ...), custom_call_target="tpu_custom_call" | custom-call | flops 1342177280 | bytes 10485760 | tf_op jit(solution)/shard_map/pallas_call | solution.py:398
  124.9 6.2 %collective-permute-start.24 = (f32[3,8,1024]{2,1,0:T(8,128)S(1)}, f32[3,8,1024]{2,1,0:T(8,128)S(1)}, u32[]{:S(2)}, u32[]{:S(2)}) collective-permute-start(f32[3,8,1024]{2,1,0:T(8,128)S(1)} %get-tuple-element.88), channel_id=1, source_target_pairs={{0,56},{4,60},{8,0},{12,4},{16,8},{20,12},{24,16},{28,20},{32,24},... | collective-permute-start | bytes 294920 | tf_op jit(solution)/shard_map/ppermute | solution.py:39
  139.0 3.4 %shard_map.97 = (f32[64,512]{1,0:T(8,128)S(1)}, f32[64,128]{1,0:T(8,128)S(1)}) custom-call(f32[64,512]{1,0:T(8,128)S(1)} %shard_map.95.v_ref.refs_0_.refs_4_, f32[5,8,1024]{2,1,0:T(8,128)S(1)} %get-tuple-element.83.refs_1_, f32[5,8,1024]{2,1,0:T(8,128)S(1)} %collective-permute-done.22.refs_2_, f32[5,8,1024]{2,1,0:T(8,128)S(1)} %collective-permute-done.23.refs_3_, ...), custom_call_target="tpu_custom_call" | custom-call | flops 1342177280 | bytes 10485760 | tf_op jit(solution)/shard_map/pallas_call | solution.py:402
  142.4 16.8 %all_to_all.11 = f32[64,1,128]{2,1,0:T(1,128)S(1)} all-to-all(f32[64,1,128]{2,1,0:T(1,128)S(1)} %bitcast.13), channel_id=1, replica_groups=mesh['orbit'=8,'lon'=16,'lat'=4] {'lon','lat'}, dimensions={0} | all-to-all | bytes 65536 | tf_op jit(solution)/shard_map/all_to_all | solution.py:406
  (53 shorter events, 34.2 us)
Async XLA Ops:
  1.6 15.0 %collective-permute-start.3 = (f32[8,128]{1,0:T(8,128)S(1)}, f32[8,128]{1,0:T(8,128)S(1)}, u32[]{:S(2)}, u32[]{:S(2)}) collective-permute-start(f32[8,128]{1,0:T(8,128)S(1)} %shard_map.87), channel_id=1, source_target_pairs={{0,8},{4,12},{8,16},{12,20},{16,24},{20,28},{24,32},{28,36},{32,40... | collective-permute-start | bytes 12296 | tf_op jit(solution)/shard_map/ppermute | solution.py:39
  5.6 10.9 %collective-permute-start.2 = (f32[8,128]{1,0:T(8,128)S(1)}, f32[8,128]{1,0:T(8,128)S(1)}, u32[]{:S(2)}, u32[]{:S(2)}) collective-permute-start(f32[8,128]{1,0:T(8,128)S(1)} %shard_map.87), channel_id=1, source_target_pairs={{0,4},{4,8},{8,12},{12,16},{16,20},{20,24},{24,28},{28,32},{32,36}... | collective-permute-start | bytes 12296 | tf_op jit(solution)/shard_map/ppermute | solution.py:39
  7.8 8.7 %collective-permute-start.1 = (f32[8,128]{1,0:T(8,128)S(1)}, f32[8,128]{1,0:T(8,128)S(1)}, u32[]{:S(2)}, u32[]{:S(2)}) collective-permute-start(f32[8,128]{1,0:T(8,128)S(1)} %shard_map.87), channel_id=1, source_target_pairs={{0,60},{4,0},{8,4},{12,8},{16,12},{20,16},{24,20},{28,24},{32,28},... | collective-permute-start | bytes 12296 | tf_op jit(solution)/shard_map/ppermute | solution.py:39
  10.4 6.0 %collective-permute-start = (f32[8,128]{1,0:T(8,128)S(1)}, f32[8,128]{1,0:T(8,128)S(1)}, u32[]{:S(2)}, u32[]{:S(2)}) collective-permute-start(f32[8,128]{1,0:T(8,128)S(1)} %shard_map.87), channel_id=1, source_target_pairs={{0,56},{4,60},{8,0},{12,4},{16,8},{20,12},{24,16},{28,20},{32,24},... | collective-permute-start | bytes 12296 | tf_op jit(solution)/shard_map/ppermute | solution.py:39
  52.8 17.4 %collective-permute-start.4 = (f32[5,8,1024]{2,1,0:T(8,128)S(1)}, f32[5,8,1024]{2,1,0:T(8,128)S(1)}, u32[]{:S(2)}, u32[]{:S(2)}) collective-permute-start(f32[5,8,1024]{2,1,0:T(8,128)S(1)} %get-tuple-element.55), channel_id=1, source_target_pairs={{0,60},{4,0},{8,4},{12,8},{16,12},{20,16},{24,20},{28,24},{32,28},... | collective-permute-start | bytes 491528 | tf_op jit(solution)/shard_map/ppermute | solution.py:39
  60.6 12.2 %collective-permute-start.5 = (f32[5,8,1024]{2,1,0:T(8,128)S(1)}, f32[5,8,1024]{2,1,0:T(8,128)S(1)}, u32[]{:S(2)}, u32[]{:S(2)}) collective-permute-start(f32[5,8,1024]{2,1,0:T(8,128)S(1)} %get-tuple-element.58), channel_id=1, source_target_pairs={{0,4},{4,8},{8,12},{12,16},{16,20},{20,24},{24,28},{28,32},{32,36}... | collective-permute-start | bytes 491528 | tf_op jit(solution)/shard_map/ppermute | solution.py:39
  60.6 10.9 %collective-permute-start.6 = (f32[3,8,1024]{2,1,0:T(8,128)S(1)}, f32[3,8,1024]{2,1,0:T(8,128)S(1)}, u32[]{:S(2)}, u32[]{:S(2)}) collective-permute-start(f32[3,8,1024]{2,1,0:T(8,128)S(1)} %get-tuple-element.59), channel_id=1, source_target_pairs={{0,56},{4,60},{8,0},{12,4},{16,8},{20,12},{24,16},{28,20},{32,24},... | collective-permute-start | bytes 294920 | tf_op jit(solution)/shard_map/ppermute | solution.py:39
  65.1 7.7 %collective-permute-start.7 = (f32[3,8,1024]{2,1,0:T(8,128)S(1)}, f32[3,8,1024]{2,1,0:T(8,128)S(1)}, u32[]{:S(2)}, u32[]{:S(2)}) collective-permute-start(f32[3,8,1024]{2,1,0:T(8,128)S(1)} %get-tuple-element.60), channel_id=1, source_target_pairs={{0,8},{4,12},{8,16},{12,20},{16,24},{20,28},{24,32},{28,36},{32,40... | collective-permute-start | bytes 294920 | tf_op jit(solution)/shard_map/ppermute | solution.py:39
  70.2 4.5 %collective-permute-start.9 = (f32[8,512]{1,0:T(8,128)S(1)}, f32[8,512]{1,0:T(8,128)S(1)}, u32[]{:S(2)}, u32[]{:S(2)}) collective-permute-start(f32[8,512]{1,0:T(8,128)S(1)} %get-tuple-element.62), channel_id=1, source_target_pairs={{1,0},{2,1},{3,2},{5,4},{6,5},{7,6},{9,8},{10,9},{11,10},{13,12},{... | collective-permute-start | bytes 49160 | tf_op jit(solution)/shard_map/ppermute | solution.py:354
  79.5 12.6 %collective-permute-start.10 = (f32[5,8,1024]{2,1,0:T(8,128)S(1)}, f32[5,8,1024]{2,1,0:T(8,128)S(1)}, u32[]{:S(2)}, u32[]{:S(2)}) collective-permute-start(f32[5,8,1024]{2,1,0:T(8,128)S(1)} %get-tuple-element.66), channel_id=1, source_target_pairs={{0,60},{4,0},{8,4},{12,8},{16,12},{20,16},{24,20},{28,24},{32,28},... | collective-permute-start | bytes 491528 | tf_op jit(solution)/shard_map/ppermute | solution.py:39
  80.9 13.9 %collective-permute-start.11 = (f32[5,8,1024]{2,1,0:T(8,128)S(1)}, f32[5,8,1024]{2,1,0:T(8,128)S(1)}, u32[]{:S(2)}, u32[]{:S(2)}) collective-permute-start(f32[5,8,1024]{2,1,0:T(8,128)S(1)} %get-tuple-element.69), channel_id=1, source_target_pairs={{0,4},{4,8},{8,12},{12,16},{16,20},{20,24},{24,28},{28,32},{32,36}... | collective-permute-start | bytes 491528 | tf_op jit(solution)/shard_map/ppermute | solution.py:39
  81.5 12.2 %collective-permute-start.12 = (f32[3,8,1024]{2,1,0:T(8,128)S(1)}, f32[3,8,1024]{2,1,0:T(8,128)S(1)}, u32[]{:S(2)}, u32[]{:S(2)}) collective-permute-start(f32[3,8,1024]{2,1,0:T(8,128)S(1)} %get-tuple-element.70), channel_id=1, source_target_pairs={{0,56},{4,60},{8,0},{12,4},{16,8},{20,12},{24,16},{28,20},{32,24},... | collective-permute-start | bytes 294920 | tf_op jit(solution)/shard_map/ppermute | solution.py:39
  87.1 7.7 %collective-permute-start.13 = (f32[3,8,1024]{2,1,0:T(8,128)S(1)}, f32[3,8,1024]{2,1,0:T(8,128)S(1)}, u32[]{:S(2)}, u32[]{:S(2)}) collective-permute-start(f32[3,8,1024]{2,1,0:T(8,128)S(1)} %get-tuple-element.71), channel_id=1, source_target_pairs={{0,8},{4,12},{8,16},{12,20},{16,24},{20,28},{24,32},{28,36},{32,40... | collective-permute-start | bytes 294920 | tf_op jit(solution)/shard_map/ppermute | solution.py:39
  89.0 4.6 %collective-permute-start.14 = (f32[8,512]{1,0:T(8,128)S(1)}, f32[8,512]{1,0:T(8,128)S(1)}, u32[]{:S(2)}, u32[]{:S(2)}) collective-permute-start(f32[8,512]{1,0:T(8,128)S(1)} %get-tuple-element.72), channel_id=1, source_target_pairs={{0,1},{1,2},{2,3},{4,5},{5,6},{6,7},{8,9},{9,10},{10,11},{12,13},{... | collective-permute-start | bytes 49160 | tf_op jit(solution)/shard_map/ppermute | solution.py:352
  92.1 4.5 %collective-permute-start.15 = (f32[8,512]{1,0:T(8,128)S(1)}, f32[8,512]{1,0:T(8,128)S(1)}, u32[]{:S(2)}, u32[]{:S(2)}) collective-permute-start(f32[8,512]{1,0:T(8,128)S(1)} %get-tuple-element.73), channel_id=1, source_target_pairs={{1,0},{2,1},{3,2},{5,4},{6,5},{7,6},{9,8},{10,9},{11,10},{13,12},{... | collective-permute-start | bytes 49160 | tf_op jit(solution)/shard_map/ppermute | solution.py:354
  101.5 12.3 %collective-permute-start.16 = (f32[5,8,1024]{2,1,0:T(8,128)S(1)}, f32[5,8,1024]{2,1,0:T(8,128)S(1)}, u32[]{:S(2)}, u32[]{:S(2)}) collective-permute-start(f32[5,8,1024]{2,1,0:T(8,128)S(1)} %get-tuple-element.75), channel_id=1, source_target_pairs={{0,60},{4,0},{8,4},{12,8},{16,12},{20,16},{24,20},{28,24},{32,28},... | collective-permute-start | bytes 491528 | tf_op jit(solution)/shard_map/ppermute | solution.py:39
  102.4 13.7 %collective-permute-start.17 = (f32[5,8,1024]{2,1,0:T(8,128)S(1)}, f32[5,8,1024]{2,1,0:T(8,128)S(1)}, u32[]{:S(2)}, u32[]{:S(2)}) collective-permute-start(f32[5,8,1024]{2,1,0:T(8,128)S(1)} %get-tuple-element.78), channel_id=1, source_target_pairs={{0,4},{4,8},{8,12},{12,16},{16,20},{20,24},{24,28},{28,32},{32,36}... | collective-permute-start | bytes 491528 | tf_op jit(solution)/shard_map/ppermute | solution.py:39
  103.3 11.9 %collective-permute-start.18 = (f32[3,8,1024]{2,1,0:T(8,128)S(1)}, f32[3,8,1024]{2,1,0:T(8,128)S(1)}, u32[]{:S(2)}, u32[]{:S(2)}) collective-permute-start(f32[3,8,1024]{2,1,0:T(8,128)S(1)} %get-tuple-element.79), channel_id=1, source_target_pairs={{0,56},{4,60},{8,0},{12,4},{16,8},{20,12},{24,16},{28,20},{32,24},... | collective-permute-start | bytes 294920 | tf_op jit(solution)/shard_map/ppermute | solution.py:39
  109.0 7.1 %collective-permute-start.19 = (f32[3,8,1024]{2,1,0:T(8,128)S(1)}, f32[3,8,1024]{2,1,0:T(8,128)S(1)}, u32[]{:S(2)}, u32[]{:S(2)}) collective-permute-start(f32[3,8,1024]{2,1,0:T(8,128)S(1)} %get-tuple-element.80), channel_id=1, source_target_pairs={{0,8},{4,12},{8,16},{12,20},{16,24},{20,28},{24,32},{28,36},{32,40... | collective-permute-start | bytes 294920 | tf_op jit(solution)/shard_map/ppermute | solution.py:39
  113.8 4.5 %collective-permute-start.21 = (f32[8,512]{1,0:T(8,128)S(1)}, f32[8,512]{1,0:T(8,128)S(1)}, u32[]{:S(2)}, u32[]{:S(2)}) collective-permute-start(f32[8,512]{1,0:T(8,128)S(1)} %get-tuple-element.82), channel_id=1, source_target_pairs={{1,0},{2,1},{3,2},{5,4},{6,5},{7,6},{9,8},{10,9},{11,10},{13,12},{... | collective-permute-start | bytes 49160 | tf_op jit(solution)/shard_map/ppermute | solution.py:354
  123.1 11.4 %collective-permute-start.22 = (f32[5,8,1024]{2,1,0:T(8,128)S(1)}, f32[5,8,1024]{2,1,0:T(8,128)S(1)}, u32[]{:S(2)}, u32[]{:S(2)}) collective-permute-start(f32[5,8,1024]{2,1,0:T(8,128)S(1)} %get-tuple-element.84), channel_id=1, source_target_pairs={{0,60},{4,0},{8,4},{12,8},{16,12},{20,16},{24,20},{28,24},{32,28},... | collective-permute-start | bytes 491528 | tf_op jit(solution)/shard_map/ppermute | solution.py:39
  124.0 13.7 %collective-permute-start.23 = (f32[5,8,1024]{2,1,0:T(8,128)S(1)}, f32[5,8,1024]{2,1,0:T(8,128)S(1)}, u32[]{:S(2)}, u32[]{:S(2)}) collective-permute-start(f32[5,8,1024]{2,1,0:T(8,128)S(1)} %get-tuple-element.87), channel_id=1, source_target_pairs={{0,4},{4,8},{8,12},{12,16},{16,20},{20,24},{24,28},{28,32},{32,36}... | collective-permute-start | bytes 491528 | tf_op jit(solution)/shard_map/ppermute | solution.py:39
  124.9 11.0 %collective-permute-start.24 = (f32[3,8,1024]{2,1,0:T(8,128)S(1)}, f32[3,8,1024]{2,1,0:T(8,128)S(1)}, u32[]{:S(2)}, u32[]{:S(2)}) collective-permute-start(f32[3,8,1024]{2,1,0:T(8,128)S(1)} %get-tuple-element.88), channel_id=1, source_target_pairs={{0,56},{4,60},{8,0},{12,4},{16,8},{20,12},{24,16},{28,20},{32,24},... | collective-permute-start | bytes 294920 | tf_op jit(solution)/shard_map/ppermute | solution.py:39
  131.1 6.6 %collective-permute-start.25 = (f32[3,8,1024]{2,1,0:T(8,128)S(1)}, f32[3,8,1024]{2,1,0:T(8,128)S(1)}, u32[]{:S(2)}, u32[]{:S(2)}) collective-permute-start(f32[3,8,1024]{2,1,0:T(8,128)S(1)} %get-tuple-element.89), channel_id=1, source_target_pairs={{0,8},{4,12},{8,16},{12,20},{16,24},{20,28},{24,32},{28,36},{32,40... | collective-permute-start | bytes 294920 | tf_op jit(solution)/shard_map/ppermute | solution.py:39
  (4 other events, 15.9 us)

commit v5 on v4

--- a/solution.py
+++ b/solution.py
@@ -164,8 +164,22 @@
     return total[:64] + total[64:]
 
 
-def project_kernel(v_ref, mask_ref, w_ref, own_ref, left_ref, right_ref, left2_ref, right2_ref, down_ref, up_ref):
-    v = v_ref[...]
+def project_first_kernel(v_ref, mask_ref, w_ref, *outs):
+    project_all(v_ref[...], mask_ref, w_ref, *outs)
+
+
+def project_kernel(part_ref, south, north, prior_ref, mask_ref, w_ref, v_ref, *outs):
+    v = with_faces(part_ref[...], south[...], north[...], prior_ref)
+    v_ref[...] = v
+    project_all(v, mask_ref, w_ref, *outs)
+
+
+def with_faces(part, south, north, prior_ref):
+    weight = jnp.concatenate([prior_ref[0:8, :]] * CLON, axis=1)
+    return jnp.concatenate([part[0:8] - weight * south, part[8:56], part[56:64] - weight * north], axis=0)
+
+
+def project_all(v, mask_ref, w_ref, own_ref, left_ref, right_ref, left2_ref, right2_ref, down_ref, up_ref):
     down_ref[...] = v[0:8]
     up_ref[...] = v[56:64]
     for l in range(CLAT):
@@ -222,7 +236,7 @@
     return sums
 
 
-def prior_image(v, plus1, minus1, south, north, prior_ref):
+def prior_image(v, plus1, minus1, prior_ref):
     west = jnp.concatenate([minus1[4, :, l * LEV:(l + 1) * LEV] for l in range(CLAT)], axis=0)
     east = jnp.concatenate([plus1[4, :, l * LEV:(l + 1) * LEV] for l in range(CLAT)], axis=0)
     cols = [west] + [v[:, c * LEV:(c + 1) * LEV] for c in range(CLON)] + [east]
@@ -232,33 +246,29 @@
         here = cols[c + 1]
         below = jnp.where(lane == 0, 0.0, pltpu.roll(here, 1, 1))
         above = jnp.where(lane == LEV - 1, 0.0, pltpu.roll(here, LEV - 1, 1))
-        south_side = jnp.concatenate([south[:, c * LEV:(c + 1) * LEV], here[:56]], axis=0)
-        north_side = jnp.concatenate([here[8:], north[:, c * LEV:(c + 1) * LEV]], axis=0)
+        edge = jnp.zeros((8, LEV), F32)
+        south_side = jnp.concatenate([edge, here[:56]], axis=0)
+        north_side = jnp.concatenate([here[8:], edge], axis=0)
         near = cols[c] + cols[c + 2] + below + above + south_side + north_side
         pieces.append(prior_ref[...] * (6.0 * here - near))
     return jnp.concatenate(pieces, axis=1)
 
 
-def next_vector(v_ref, own_ref, plus1, minus1, plus2, minus2, south, north, lats, w_ref, gram_ref, prior_ref):
+def step_kernel(v_ref, own_ref, plus1, minus1, plus2, minus2, mask_ref, w_ref, gram_ref, prior_ref, out_ref):
+    lats = [mask_ref[slot] for slot in range(SPAN)]
     image = back_all(ray_sums(own_ref, plus1, minus1, plus2, minus2), lats, w_ref)
     image = jnp.dot(gram_ref[...], image, precision=highest, preferred_element_type=F32)
-    return image + prior_image(v_ref[...], plus1, minus1, south, north, prior_ref)
-
-
-def step_kernel(*refs):
-    lats = [refs[8][slot] for slot in range(SPAN)]
-    refs[12][...] = next_vector(*refs[:8], lats, *refs[9:12])
+    out_ref[...] = image + prior_image(v_ref[...], plus1, minus1, prior_ref)
 
 
 PAIRS = [(i, j) for i in range(ITERS) for j in range(i, ITERS)] + [(ITERS - 1, ITERS)]
 
 
-def last_kernel(*refs):
-    lats = [refs[8][slot] for slot in range(SPAN)]
-    v = next_vector(*refs[:8], lats, *refs[9:12])
-    earlier, (out_ref, pair_ref) = refs[12:12 + ITERS - 1], refs[12 + ITERS - 1:]
+def last_kernel(part_ref, south, north, prior_ref, *refs):
+    earlier, (out_ref, pair_ref) = refs[:ITERS], refs[ITERS:]
+    v = with_faces(part_ref[...], south[...], north[...], prior_ref)
     out_ref[...] = v
-    vectors = [ref[...] for ref in earlier] + [refs[0][...], v]
+    vectors = [ref[...] for ref in earlier] + [v]
     lane = lax.broadcasted_iota(jnp.int32, (1, LEV), 1)
     row = jnp.zeros((1, LEV), F32)
     for n, (i, j) in enumerate(PAIRS):
@@ -393,15 +403,15 @@
     w, lat = call(build_kernel, (shape(SPAN, 2 * CELL, SLOT, dtype=BF16), shape(SPAN, 8, SLOT, dtype=jnp.int32)), 1, work=BUILD)(shards)
     v, mask = call(init_kernel, (FIELD, shape(SPAN, 8, SLOT, dtype=jnp.int32)), 3, work=MATMUL)(shards, lat, w)
     vectors = [v]
-    sent = call(project_kernel, SENT, 3, work=MATMUL)(v, mask, w)
-    for turn in range(ITERS - 1):
-        (v,) = call(step_kernel, (FIELD,), 12, work=MATMUL)(v, *exchange(*sent), mask, w, gram, prior)
-        vectors.append(v)
-        sent = call(project_kernel, SENT, 3, work=MATMUL)(v, mask, w)
+    sent = call(project_first_kernel, SENT, 3, work=MATMUL)(v, mask, w)
+    for turn in range(ITERS):
+        *sums, south, north = exchange(*sent)
+        (part,) = call(step_kernel, (FIELD,), 10, work=MATMUL)(v, *sums, mask, w, gram, prior)
+        if turn < ITERS - 1:
+            v, *sent = call(project_kernel, (FIELD,) + SENT, 6, work=MATMUL)(part, south, north, prior, mask, w)
+            vectors.append(v)
     peers = lax.axis_size("lon") * lax.axis_size("lat")
-    v, pairs = call(last_kernel, (FIELD, shape(peers, LEV)), 12 + ITERS - 1, work=MATMUL)(
-        v, *exchange(*sent), mask, w, gram, prior, *vectors[:-1]
-    )
+    v, pairs = call(last_kernel, (FIELD, shape(peers, LEV)), 4 + ITERS)(part, south, north, prior, *vectors)
     vectors.append(v)
     pairs = lax.all_to_all(pairs, ("lon", "lat"), 0, 0, tiled=True)
     field = shape(S, CLON, CLAT, LEV)

time: 161 us -> 156 us (0.969)
  waiting for transfers between devices: 12.5 us -> 1.37 us
  starting transfers between devices: 72.6 us -> 75.4 us
  blocking collectives: 40.1 us -> 42.8 us
    ppermute x4, waiting for transfers between devices: 7.25 us -> 0.01 us  [exchange(): north = lax.ppermute(down, 'lat', [(i + 1, i) for i in range(n_lat - 1)])]
    ppermute x4, starting transfers between devices: 10.5 us -> 15.1 us  [exchange(): south = lax.ppermute(up, 'lat', [(i, i + 1) for i in range(n_lat - 1)])]
    ppermute x20, waiting for transfers between devices: 5.24 us -> 1.34 us  [shift(): lax.ppermute(block, axis, [(i, (i + distance) % size) for i in range(size)])]
    all_to_all x1, blocking collectives: 16.8 us -> 19.4 us  [body(): pairs = lax.all_to_all(pairs, ('lon', 'lat'), 0, 0, tiled=True)]
    ppermute x20, starting transfers between devices: 56.7 us -> 55 us  [shift(): lax.ppermute(block, axis, [(i, (i + distance) % size) for i in range(size)])]
    pallas_call x8 -> x9, Pallas kernels: 19.5 us -> 19.6 us  [the longest x4 13.2 us: body(): call(step_kernel, (FIELD,), 10, work=MATMUL)(v, *sums, mask, w, gram, prior)]
  transfers between devices with their start and end apart: 28 -> 28, of which waited for: 8 -> 1; matrix products, arithmetic and copies ran while one was open for 0% -> 0% of each run, Pallas kernels for 1% -> 9%
where the time goes in v5:
time: 156 us; the launch traced here: 155 us
  starting transfers between devices  75.4 us (48%)
  blocking collectives  42.8 us (27%)
  Pallas kernels  34.4 us (22%)
    ppermute x20, starting transfers between devices, shift(): lax.ppermute(block, axis, [(i, (i + distance) % size) for i in range(size)])  55 us
    all_gather x1, blocking collectives, body(): lax.all_gather(jnp.concatenate([table, z0, z1, z, z3, z4], axis=0), 'orbit')  23.3 us
    all_to_all x1, blocking collectives, body(): pairs = lax.all_to_all(pairs, ('lon', 'lat'), 0, 0, tiled=True)  19.4 us
    ppermute x4, starting transfers between devices, exchange(): south = lax.ppermute(up, 'lat', [(i, i + 1) for i in range(n_lat - 1)])  15.1 us
    pallas_call x4, Pallas kernels, body(): call(step_kernel, (FIELD,), 10, work=MATMUL)(v, *sums, mask, w, gram, prior)  13.2 us
    pallas_call x1, Pallas kernels, body(): call(build_kernel, (shape(SPAN, 2 * CELL, SLOT, dtype=BF16), shape(SPAN,...  8.4 us
    ppermute x4, starting transfers between devices, exchange(): north = lax.ppermute(down, 'lat', [(i + 1, i) for i in range(n_lat - 1)])  5.35 us
    pallas_call x3, Pallas kernels, body(): call(project_kernel, (FIELD,) + SENT, 6, work=MATMUL)  4.61 us
  transfers between devices with their start and end apart: 28, of which 1 were waited for; matrix products, arithmetic and copies ran while one was open for 0% of the time, Pallas kernels for 9%

profile of v5, /device:TPU:1, one launch (start us, length us, event | category | flops | bytes accessed | tf_op | source)
XLA Modules:
  0.0 155.1 jit_solution(3591085206956978178)
XLA Ops:
  1.6 4.0 %collective-permute-start.3 = (f32[8,128]{1,0:T(8,128)S(1)}, f32[8,128]{1,0:T(8,128)S(1)}, u32[]{:S(2)}, u32[]{:S(2)}) collective-permute-start(f32[8,128]{1,0:T(8,128)S(1)} %shard_map.87), channel_id=1, source_target_pairs={{0,8},{4,12},{8,16},{12,20},{16,24},{20,28},{24,32},{28,36},{32,40... | collective-permute-start | bytes 12296 | tf_op jit(solution)/shard_map/ppermute | solution.py:39
  5.6 2.1 %collective-permute-start.2 = (f32[8,128]{1,0:T(8,128)S(1)}, f32[8,128]{1,0:T(8,128)S(1)}, u32[]{:S(2)}, u32[]{:S(2)}) collective-permute-start(f32[8,128]{1,0:T(8,128)S(1)} %shard_map.87), channel_id=1, source_target_pairs={{0,4},{4,8},{8,12},{12,16},{16,20},{20,24},{24,28},{28,32},{32,36}... | collective-permute-start | bytes 12296 | tf_op jit(solution)/shard_map/ppermute | solution.py:39
  7.8 2.7 %collective-permute-start.1 = (f32[8,128]{1,0:T(8,128)S(1)}, f32[8,128]{1,0:T(8,128)S(1)}, u32[]{:S(2)}, u32[]{:S(2)}) collective-permute-start(f32[8,128]{1,0:T(8,128)S(1)} %shard_map.87), channel_id=1, source_target_pairs={{0,60},{4,0},{8,4},{12,8},{16,12},{20,16},{24,20},{28,24},{32,28},... | collective-permute-start | bytes 12296 | tf_op jit(solution)/shard_map/ppermute | solution.py:39
  10.4 4.8 %collective-permute-start = (f32[8,128]{1,0:T(8,128)S(1)}, f32[8,128]{1,0:T(8,128)S(1)}, u32[]{:S(2)}, u32[]{:S(2)}) collective-permute-start(f32[8,128]{1,0:T(8,128)S(1)} %shard_map.87), channel_id=1, source_target_pairs={{0,56},{4,60},{8,0},{12,4},{16,8},{20,12},{24,16},{28,20},{32,24},... | collective-permute-start | bytes 12296 | tf_op jit(solution)/shard_map/ppermute | solution.py:39
  16.6 23.3 %all-gather = f32[1600,128]{1,0:T(8,128)S(1)} all-gather(f32[200,128]{1,0:T(8,128)S(1)} %constant_dynamic-update-slice_fusion), channel_id=2, replica_groups=mesh['orbit'=8,'lon'=16,'lat'=4] {'orbit'}, dimensions={0}, use_global_device_ids=true | all-gather | bytes 921600 | tf_op jit(solution)/shard_map/all_gather | solution.py:402
  39.9 8.4 %shard_map.88 = (bf16[5,1024,1024]{2,1,0:T(8,128)(2,1)S(1)}, s32[5,8,1024]{2,1,0:T(8,128)S(1)}) custom-call(f32[8,200,128]{2,1,0:T(8,128)S(1)} %bitcast.10), custom_call_target="tpu_custom_call" | custom-call | flops 671088640 | bytes 20971520 | tf_op jit(solution)/shard_map/pallas_call | solution.py:403
  48.3 2.9 %shard_map.89 = (f32[64,512]{1,0:T(8,128)S(1)}, s32[5,8,1024]{2,1,0:T(8,128)S(1)}) custom-call(f32[8,200,128]{2,1,0:T(8,128)S(1)} %bitcast.11, s32[5,8,1024]{2,1,0:T(8,128)S(1)} %get-tuple-element.53.lat_ref, bf16[5,1024,1024]{2,1,0:T(8,128)(2,1)S(1)} %get-tuple-element.54.w_ref), custom_call_target="tpu_custom_call" | custom-call | flops 1342177280 | bytes 10485760 | tf_op jit(solution)/shard_map/pallas_call | solution.py:404
  52.8 7.9 %collective-permute-start.4 = (f32[5,8,1024]{2,1,0:T(8,128)S(1)}, f32[5,8,1024]{2,1,0:T(8,128)S(1)}, u32[]{:S(2)}, u32[]{:S(2)}) collective-permute-start(f32[5,8,1024]{2,1,0:T(8,128)S(1)} %get-tuple-element.58), channel_id=1, source_target_pairs={{0,60},{4,0},{8,4},{12,8},{16,12},{20,16},{24,20},{28,24},{32,28},... | collective-permute-start | bytes 491528 | tf_op jit(solution)/shard_map/ppermute | solution.py:39
  60.6 4.5 %collective-permute-start.6 = (f32[3,8,1024]{2,1,0:T(8,128)S(1)}, f32[3,8,1024]{2,1,0:T(8,128)S(1)}, u32[]{:S(2)}, u32[]{:S(2)}) collective-permute-start(f32[3,8,1024]{2,1,0:T(8,128)S(1)} %get-tuple-element.62), channel_id=1, source_target_pairs={{0,56},{4,60},{8,0},{12,4},{16,8},{20,12},{24,16},{28,20},{32,24},... | collective-permute-start | bytes 294920 | tf_op jit(solution)/shard_map/ppermute | solution.py:39
  65.1 1.9 %collective-permute-start.7 = (f32[3,8,1024]{2,1,0:T(8,128)S(1)}, f32[3,8,1024]{2,1,0:T(8,128)S(1)}, u32[]{:S(2)}, u32[]{:S(2)}) collective-permute-start(f32[3,8,1024]{2,1,0:T(8,128)S(1)} %get-tuple-element.63), channel_id=1, source_target_pairs={{0,8},{4,12},{8,16},{12,20},{16,24},{20,28},{24,32},{28,36},{32,40... | collective-permute-start | bytes 294920 | tf_op jit(solution)/shard_map/ppermute | solution.py:39
  67.1 3.1 %collective-permute-start.8 = (f32[8,512]{1,0:T(8,128)S(1)}, f32[8,512]{1,0:T(8,128)S(1)}, u32[]{:S(2)}, u32[]{:S(2)}) collective-permute-start(f32[8,512]{1,0:T(8,128)S(1)} %get-tuple-element.66), channel_id=1, source_target_pairs={{0,1},{1,2},{2,3},{4,5},{5,6},{6,7},{8,9},{9,10},{10,11},{12,13},{... | collective-permute-start | bytes 49160 | tf_op jit(solution)/shard_map/ppermute | solution.py:362
  72.8 3.3 %shard_map.91.part_ref = f32[64,512]{1,0:T(8,128)S(1)} custom-call(f32[64,512]{1,0:T(8,128)S(1)} %get-tuple-element.55.v_ref.refs_0_.refs_1_, f32[5,8,1024]{2,1,0:T(8,128)S(1)} %get-tuple-element.57.own_ref, f32[5,8,1024]{2,1,0:T(8,128)S(1)} %collective-permute-done.4.plus1, f32[5,8,1024]{2,1,0:T(8,128)S(1)} %collective-permute-done.5.minus1, ...), custom_call_target="tpu_custom_call" | custom-call | flops 1342177280 | bytes 10485760 | tf_op jit(solution)/shard_map/pallas_call | solution.py:409
  79.4 4.5 %collective-permute-start.12 = (f32[3,8,1024]{2,1,0:T(8,128)S(1)}, f32[3,8,1024]{2,1,0:T(8,128)S(1)}, u32[]{:S(2)}, u32[]{:S(2)}) collective-permute-start(f32[3,8,1024]{2,1,0:T(8,128)S(1)} %get-tuple-element.74), channel_id=1, source_target_pairs={{0,56},{4,60},{8,0},{12,4},{16,8},{20,12},{24,16},{28,20},{32,24},... | collective-permute-start | bytes 294920 | tf_op jit(solution)/shard_map/ppermute | solution.py:39
  83.9 1.9 %collective-permute-start.13 = (f32[3,8,1024]{2,1,0:T(8,128)S(1)}, f32[3,8,1024]{2,1,0:T(8,128)S(1)}, u32[]{:S(2)}, u32[]{:S(2)}) collective-permute-start(f32[3,8,1024]{2,1,0:T(8,128)S(1)} %get-tuple-element.75), channel_id=1, source_target_pairs={{0,8},{4,12},{8,16},{12,20},{16,24},{20,28},{24,32},{28,36},{32,40... | collective-permute-start | bytes 294920 | tf_op jit(solution)/shard_map/ppermute | solution.py:39
  85.9 4.0 %collective-permute-start.14 = (f32[8,512]{1,0:T(8,128)S(1)}, f32[8,512]{1,0:T(8,128)S(1)}, u32[]{:S(2)}, u32[]{:S(2)}) collective-permute-start(f32[8,512]{1,0:T(8,128)S(1)} %get-tuple-element.76), channel_id=1, source_target_pairs={{0,1},{1,2},{2,3},{4,5},{5,6},{6,7},{8,9},{9,10},{10,11},{12,13},{... | collective-permute-start | bytes 49160 | tf_op jit(solution)/shard_map/ppermute | solution.py:362
  91.4 3.3 %shard_map.93.part_ref = f32[64,512]{1,0:T(8,128)S(1)} custom-call(f32[64,512]{1,0:T(8,128)S(1)} %get-tuple-element.68.v_ref.refs_1_.refs_2_, f32[5,8,1024]{2,1,0:T(8,128)S(1)} %get-tuple-element.69.own_ref, f32[5,8,1024]{2,1,0:T(8,128)S(1)} %collective-permute-done.10.plus1, f32[5,8,1024]{2,1,0:T(8,128)S(1)} %collective-permute-done.11.minus1, ...), custom_call_target="tpu_custom_call" | custom-call | flops 1342177280 | bytes 10485760 | tf_op jit(solution)/shard_map/pallas_call | solution.py:409
  98.0 5.8 %collective-permute-start.18 = (f32[3,8,1024]{2,1,0:T(8,128)S(1)}, f32[3,8,1024]{2,1,0:T(8,128)S(1)}, u32[]{:S(2)}, u32[]{:S(2)}) collective-permute-start(f32[3,8,1024]{2,1,0:T(8,128)S(1)} %get-tuple-element.84), channel_id=1, source_target_pairs={{0,56},{4,60},{8,0},{12,4},{16,8},{20,12},{24,16},{28,20},{32,24},... | collective-permute-start | bytes 294920 | tf_op jit(solution)/shard_map/ppermute | solution.py:39
  103.8 1.9 %collective-permute-start.19 = (f32[3,8,1024]{2,1,0:T(8,128)S(1)}, f32[3,8,1024]{2,1,0:T(8,128)S(1)}, u32[]{:S(2)}, u32[]{:S(2)}) collective-permute-start(f32[3,8,1024]{2,1,0:T(8,128)S(1)} %get-tuple-element.85), channel_id=1, source_target_pairs={{0,8},{4,12},{8,16},{12,20},{16,24},{20,28},{24,32},{28,36},{32,40... | collective-permute-start | bytes 294920 | tf_op jit(solution)/shard_map/ppermute | solution.py:39
  105.7 4.0 %collective-permute-start.20 = (f32[8,512]{1,0:T(8,128)S(1)}, f32[8,512]{1,0:T(8,128)S(1)}, u32[]{:S(2)}, u32[]{:S(2)}) collective-permute-start(f32[8,512]{1,0:T(8,128)S(1)} %get-tuple-element.86), channel_id=1, source_target_pairs={{0,1},{1,2},{2,3},{4,5},{5,6},{6,7},{8,9},{9,10},{10,11},{12,13},{... | collective-permute-start | bytes 49160 | tf_op jit(solution)/shard_map/ppermute | solution.py:362
  111.0 3.3 %shard_map.95.part_ref = f32[64,512]{1,0:T(8,128)S(1)} custom-call(f32[64,512]{1,0:T(8,128)S(1)} %get-tuple-element.78.v_ref.refs_2_.refs_3_, f32[5,8,1024]{2,1,0:T(8,128)S(1)} %get-tuple-element.79.own_ref, f32[5,8,1024]{2,1,0:T(8,128)S(1)} %collective-permute-done.16.plus1, f32[5,8,1024]{2,1,0:T(8,128)S(1)} %collective-permute-done.17.minus1, ...), custom_call_target="tpu_custom_call" | custom-call | flops 1342177280 | bytes 10485760 | tf_op jit(solution)/shard_map/pallas_call | solution.py:409
  117.7 5.8 %collective-permute-start.24 = (f32[3,8,1024]{2,1,0:T(8,128)S(1)}, f32[3,8,1024]{2,1,0:T(8,128)S(1)}, u32[]{:S(2)}, u32[]{:S(2)}) collective-permute-start(f32[3,8,1024]{2,1,0:T(8,128)S(1)} %get-tuple-element.94), channel_id=1, source_target_pairs={{0,56},{4,60},{8,0},{12,4},{16,8},{20,12},{24,16},{28,20},{32,24},... | collective-permute-start | bytes 294920 | tf_op jit(solution)/shard_map/ppermute | solution.py:39
  125.4 4.0 %collective-permute-start.26 = (f32[8,512]{1,0:T(8,128)S(1)}, f32[8,512]{1,0:T(8,128)S(1)}, u32[]{:S(2)}, u32[]{:S(2)}) collective-permute-start(f32[8,512]{1,0:T(8,128)S(1)} %get-tuple-element.96), channel_id=1, source_target_pairs={{0,1},{1,2},{2,3},{4,5},{5,6},{6,7},{8,9},{9,10},{10,11},{12,13},{... | collective-permute-start | bytes 49160 | tf_op jit(solution)/shard_map/ppermute | solution.py:362
  130.7 3.3 %shard_map.97.part_ref = f32[64,512]{1,0:T(8,128)S(1)} custom-call(f32[64,512]{1,0:T(8,128)S(1)} %get-tuple-element.88.v_ref.refs_3_.refs_4_, f32[5,8,1024]{2,1,0:T(8,128)S(1)} %get-tuple-element.89.own_ref, f32[5,8,1024]{2,1,0:T(8,128)S(1)} %collective-permute-done.22.plus1, f32[5,8,1024]{2,1,0:T(8,128)S(1)} %collective-permute-done.23.minus1, ...), custom_call_target="tpu_custom_call" | custom-call | flops 1342177280 | bytes 10485760 | tf_op jit(solution)/shard_map/pallas_call | solution.py:409
  134.3 19.4 %all_to_all.11 = f32[64,1,128]{2,1,0:T(1,128)S(1)} all-to-all(f32[64,1,128]{2,1,0:T(1,128)S(1)} %bitcast.13), channel_id=1, replica_groups=mesh['orbit'=8,'lon'=16,'lat'=4] {'lon','lat'}, dimensions={0} | all-to-all | bytes 65536 | tf_op jit(solution)/shard_map/all_to_all | solution.py:416
  (54 shorter events, 23.8 us)
Async XLA Ops:
  1.6 15.0 %collective-permute-start.3 = (f32[8,128]{1,0:T(8,128)S(1)}, f32[8,128]{1,0:T(8,128)S(1)}, u32[]{:S(2)}, u32[]{:S(2)}) collective-permute-start(f32[8,128]{1,0:T(8,128)S(1)} %shard_map.87), channel_id=1, source_target_pairs={{0,8},{4,12},{8,16},{12,20},{16,24},{20,28},{24,32},{28,36},{32,40... | collective-permute-start | bytes 12296 | tf_op jit(solution)/shard_map/ppermute | solution.py:39
  5.6 10.9 %collective-permute-start.2 = (f32[8,128]{1,0:T(8,128)S(1)}, f32[8,128]{1,0:T(8,128)S(1)}, u32[]{:S(2)}, u32[]{:S(2)}) collective-permute-start(f32[8,128]{1,0:T(8,128)S(1)} %shard_map.87), channel_id=1, source_target_pairs={{0,4},{4,8},{8,12},{12,16},{16,20},{20,24},{24,28},{28,32},{32,36}... | collective-permute-start | bytes 12296 | tf_op jit(solution)/shard_map/ppermute | solution.py:39
  7.8 8.7 %collective-permute-start.1 = (f32[8,128]{1,0:T(8,128)S(1)}, f32[8,128]{1,0:T(8,128)S(1)}, u32[]{:S(2)}, u32[]{:S(2)}) collective-permute-start(f32[8,128]{1,0:T(8,128)S(1)} %shard_map.87), channel_id=1, source_target_pairs={{0,60},{4,0},{8,4},{12,8},{16,12},{20,16},{24,20},{28,24},{32,28},... | collective-permute-start | bytes 12296 | tf_op jit(solution)/shard_map/ppermute | solution.py:39
  10.4 6.0 %collective-permute-start = (f32[8,128]{1,0:T(8,128)S(1)}, f32[8,128]{1,0:T(8,128)S(1)}, u32[]{:S(2)}, u32[]{:S(2)}) collective-permute-start(f32[8,128]{1,0:T(8,128)S(1)} %shard_map.87), channel_id=1, source_target_pairs={{0,56},{4,60},{8,0},{12,4},{16,8},{20,12},{24,16},{28,20},{32,24},... | collective-permute-start | bytes 12296 | tf_op jit(solution)/shard_map/ppermute | solution.py:39
  52.8 17.4 %collective-permute-start.4 = (f32[5,8,1024]{2,1,0:T(8,128)S(1)}, f32[5,8,1024]{2,1,0:T(8,128)S(1)}, u32[]{:S(2)}, u32[]{:S(2)}) collective-permute-start(f32[5,8,1024]{2,1,0:T(8,128)S(1)} %get-tuple-element.58), channel_id=1, source_target_pairs={{0,60},{4,0},{8,4},{12,8},{16,12},{20,16},{24,20},{28,24},{32,28},... | collective-permute-start | bytes 491528 | tf_op jit(solution)/shard_map/ppermute | solution.py:39
  60.6 12.2 %collective-permute-start.5 = (f32[5,8,1024]{2,1,0:T(8,128)S(1)}, f32[5,8,1024]{2,1,0:T(8,128)S(1)}, u32[]{:S(2)}, u32[]{:S(2)}) collective-permute-start(f32[5,8,1024]{2,1,0:T(8,128)S(1)} %get-tuple-element.61), channel_id=1, source_target_pairs={{0,4},{4,8},{8,12},{12,16},{16,20},{20,24},{24,28},{28,32},{32,36}... | collective-permute-start | bytes 491528 | tf_op jit(solution)/shard_map/ppermute | solution.py:39
  60.6 10.8 %collective-permute-start.6 = (f32[3,8,1024]{2,1,0:T(8,128)S(1)}, f32[3,8,1024]{2,1,0:T(8,128)S(1)}, u32[]{:S(2)}, u32[]{:S(2)}) collective-permute-start(f32[3,8,1024]{2,1,0:T(8,128)S(1)} %get-tuple-element.62), channel_id=1, source_target_pairs={{0,56},{4,60},{8,0},{12,4},{16,8},{20,12},{24,16},{28,20},{32,24},... | collective-permute-start | bytes 294920 | tf_op jit(solution)/shard_map/ppermute | solution.py:39
  65.1 7.7 %collective-permute-start.7 = (f32[3,8,1024]{2,1,0:T(8,128)S(1)}, f32[3,8,1024]{2,1,0:T(8,128)S(1)}, u32[]{:S(2)}, u32[]{:S(2)}) collective-permute-start(f32[3,8,1024]{2,1,0:T(8,128)S(1)} %get-tuple-element.63), channel_id=1, source_target_pairs={{0,8},{4,12},{8,16},{12,20},{16,24},{20,28},{24,32},{28,36},{32,40... | collective-permute-start | bytes 294920 | tf_op jit(solution)/shard_map/ppermute | solution.py:39
  67.1 9.0 %collective-permute-start.8 = (f32[8,512]{1,0:T(8,128)S(1)}, f32[8,512]{1,0:T(8,128)S(1)}, u32[]{:S(2)}, u32[]{:S(2)}) collective-permute-start(f32[8,512]{1,0:T(8,128)S(1)} %get-tuple-element.66), channel_id=1, source_target_pairs={{0,1},{1,2},{2,3},{4,5},{5,6},{6,7},{8,9},{9,10},{10,11},{12,13},{... | collective-permute-start | bytes 49160 | tf_op jit(solution)/shard_map/ppermute | solution.py:362
  77.7 12.2 %collective-permute-start.10 = (f32[5,8,1024]{2,1,0:T(8,128)S(1)}, f32[5,8,1024]{2,1,0:T(8,128)S(1)}, u32[]{:S(2)}, u32[]{:S(2)}) collective-permute-start(f32[5,8,1024]{2,1,0:T(8,128)S(1)} %get-tuple-element.70), channel_id=1, source_target_pairs={{0,60},{4,0},{8,4},{12,8},{16,12},{20,16},{24,20},{28,24},{32,28},... | collective-permute-start | bytes 491528 | tf_op jit(solution)/shard_map/ppermute | solution.py:39
  78.3 13.0 %collective-permute-start.11 = (f32[5,8,1024]{2,1,0:T(8,128)S(1)}, f32[5,8,1024]{2,1,0:T(8,128)S(1)}, u32[]{:S(2)}, u32[]{:S(2)}) collective-permute-start(f32[5,8,1024]{2,1,0:T(8,128)S(1)} %get-tuple-element.73), channel_id=1, source_target_pairs={{0,4},{4,8},{8,12},{12,16},{16,20},{20,24},{24,28},{28,32},{32,36}... | collective-permute-start | bytes 491528 | tf_op jit(solution)/shard_map/ppermute | solution.py:39
  79.4 11.9 %collective-permute-start.12 = (f32[3,8,1024]{2,1,0:T(8,128)S(1)}, f32[3,8,1024]{2,1,0:T(8,128)S(1)}, u32[]{:S(2)}, u32[]{:S(2)}) collective-permute-start(f32[3,8,1024]{2,1,0:T(8,128)S(1)} %get-tuple-element.74), channel_id=1, source_target_pairs={{0,56},{4,60},{8,0},{12,4},{16,8},{20,12},{24,16},{28,20},{32,24},... | collective-permute-start | bytes 294920 | tf_op jit(solution)/shard_map/ppermute | solution.py:39
  83.9 7.4 %collective-permute-start.13 = (f32[3,8,1024]{2,1,0:T(8,128)S(1)}, f32[3,8,1024]{2,1,0:T(8,128)S(1)}, u32[]{:S(2)}, u32[]{:S(2)}) collective-permute-start(f32[3,8,1024]{2,1,0:T(8,128)S(1)} %get-tuple-element.75), channel_id=1, source_target_pairs={{0,8},{4,12},{8,16},{12,20},{16,24},{20,28},{24,32},{28,36},{32,40... | collective-permute-start | bytes 294920 | tf_op jit(solution)/shard_map/ppermute | solution.py:39
  85.9 8.8 %collective-permute-start.14 = (f32[8,512]{1,0:T(8,128)S(1)}, f32[8,512]{1,0:T(8,128)S(1)}, u32[]{:S(2)}, u32[]{:S(2)}) collective-permute-start(f32[8,512]{1,0:T(8,128)S(1)} %get-tuple-element.76), channel_id=1, source_target_pairs={{0,1},{1,2},{2,3},{4,5},{5,6},{6,7},{8,9},{9,10},{10,11},{12,13},{... | collective-permute-start | bytes 49160 | tf_op jit(solution)/shard_map/ppermute | solution.py:362
  96.2 13.5 %collective-permute-start.16 = (f32[5,8,1024]{2,1,0:T(8,128)S(1)}, f32[5,8,1024]{2,1,0:T(8,128)S(1)}, u32[]{:S(2)}, u32[]{:S(2)}) collective-permute-start(f32[5,8,1024]{2,1,0:T(8,128)S(1)} %get-tuple-element.80), channel_id=1, source_target_pairs={{0,60},{4,0},{8,4},{12,8},{16,12},{20,16},{24,20},{28,24},{32,28},... | collective-permute-start | bytes 491528 | tf_op jit(solution)/shard_map/ppermute | solution.py:39
  96.8 14.3 %collective-permute-start.17 = (f32[5,8,1024]{2,1,0:T(8,128)S(1)}, f32[5,8,1024]{2,1,0:T(8,128)S(1)}, u32[]{:S(2)}, u32[]{:S(2)}) collective-permute-start(f32[5,8,1024]{2,1,0:T(8,128)S(1)} %get-tuple-element.83), channel_id=1, source_target_pairs={{0,4},{4,8},{8,12},{12,16},{16,20},{20,24},{24,28},{28,32},{32,36}... | collective-permute-start | bytes 491528 | tf_op jit(solution)/shard_map/ppermute | solution.py:39
  98.0 13.0 %collective-permute-start.18 = (f32[3,8,1024]{2,1,0:T(8,128)S(1)}, f32[3,8,1024]{2,1,0:T(8,128)S(1)}, u32[]{:S(2)}, u32[]{:S(2)}) collective-permute-start(f32[3,8,1024]{2,1,0:T(8,128)S(1)} %get-tuple-element.84), channel_id=1, source_target_pairs={{0,56},{4,60},{8,0},{12,4},{16,8},{20,12},{24,16},{28,20},{32,24},... | collective-permute-start | bytes 294920 | tf_op jit(solution)/shard_map/ppermute | solution.py:39
  103.8 7.2 %collective-permute-start.19 = (f32[3,8,1024]{2,1,0:T(8,128)S(1)}, f32[3,8,1024]{2,1,0:T(8,128)S(1)}, u32[]{:S(2)}, u32[]{:S(2)}) collective-permute-start(f32[3,8,1024]{2,1,0:T(8,128)S(1)} %get-tuple-element.85), channel_id=1, source_target_pairs={{0,8},{4,12},{8,16},{12,20},{16,24},{20,28},{24,32},{28,36},{32,40... | collective-permute-start | bytes 294920 | tf_op jit(solution)/shard_map/ppermute | solution.py:39
  105.7 8.6 %collective-permute-start.20 = (f32[8,512]{1,0:T(8,128)S(1)}, f32[8,512]{1,0:T(8,128)S(1)}, u32[]{:S(2)}, u32[]{:S(2)}) collective-permute-start(f32[8,512]{1,0:T(8,128)S(1)} %get-tuple-element.86), channel_id=1, source_target_pairs={{0,1},{1,2},{2,3},{4,5},{5,6},{6,7},{8,9},{9,10},{10,11},{12,13},{... | collective-permute-start | bytes 49160 | tf_op jit(solution)/shard_map/ppermute | solution.py:362
  115.9 13.5 %collective-permute-start.22 = (f32[5,8,1024]{2,1,0:T(8,128)S(1)}, f32[5,8,1024]{2,1,0:T(8,128)S(1)}, u32[]{:S(2)}, u32[]{:S(2)}) collective-permute-start(f32[5,8,1024]{2,1,0:T(8,128)S(1)} %get-tuple-element.90), channel_id=1, source_target_pairs={{0,60},{4,0},{8,4},{12,8},{16,12},{20,16},{24,20},{28,24},{32,28},... | collective-permute-start | bytes 491528 | tf_op jit(solution)/shard_map/ppermute | solution.py:39
  116.6 14.1 %collective-permute-start.23 = (f32[5,8,1024]{2,1,0:T(8,128)S(1)}, f32[5,8,1024]{2,1,0:T(8,128)S(1)}, u32[]{:S(2)}, u32[]{:S(2)}) collective-permute-start(f32[5,8,1024]{2,1,0:T(8,128)S(1)} %get-tuple-element.93), channel_id=1, source_target_pairs={{0,4},{4,8},{8,12},{12,16},{16,20},{20,24},{24,28},{28,32},{32,36}... | collective-permute-start | bytes 491528 | tf_op jit(solution)/shard_map/ppermute | solution.py:39
  117.7 13.0 %collective-permute-start.24 = (f32[3,8,1024]{2,1,0:T(8,128)S(1)}, f32[3,8,1024]{2,1,0:T(8,128)S(1)}, u32[]{:S(2)}, u32[]{:S(2)}) collective-permute-start(f32[3,8,1024]{2,1,0:T(8,128)S(1)} %get-tuple-element.94), channel_id=1, source_target_pairs={{0,56},{4,60},{8,0},{12,4},{16,8},{20,12},{24,16},{28,20},{32,24},... | collective-permute-start | bytes 294920 | tf_op jit(solution)/shard_map/ppermute | solution.py:39
  123.5 7.3 %collective-permute-start.25 = (f32[3,8,1024]{2,1,0:T(8,128)S(1)}, f32[3,8,1024]{2,1,0:T(8,128)S(1)}, u32[]{:S(2)}, u32[]{:S(2)}) collective-permute-start(f32[3,8,1024]{2,1,0:T(8,128)S(1)} %get-tuple-element.95), channel_id=1, source_target_pairs={{0,8},{4,12},{8,16},{12,20},{16,24},{20,28},{24,32},{28,36},{32,40... | collective-permute-start | bytes 294920 | tf_op jit(solution)/shard_map/ppermute | solution.py:39
  125.4 8.7 %collective-permute-start.26 = (f32[8,512]{1,0:T(8,128)S(1)}, f32[8,512]{1,0:T(8,128)S(1)}, u32[]{:S(2)}, u32[]{:S(2)}) collective-permute-start(f32[8,512]{1,0:T(8,128)S(1)} %get-tuple-element.96), channel_id=1, source_target_pairs={{0,1},{1,2},{2,3},{4,5},{5,6},{6,7},{8,9},{9,10},{10,11},{12,13},{... | collective-permute-start | bytes 49160 | tf_op jit(solution)/shard_map/ppermute | solution.py:362
  (4 other events, 20.1 us)

commit v6 on v5

--- a/solution.py
+++ b/solution.py
@@ -53,17 +53,6 @@
         copy.wait()
 
 
-def source_kernel(*refs):
-    sources, source_ref, places, sem = refs[:4], refs[4], refs[5:9], refs[9]
-    fetch(sources, places, sem)
-    obs_ref, start_ref, kern_ref, noise_ref = places
-    kern = species_rows(kern_ref)
-    source = jnp.dot(kern * noise_ref[...], obs_ref[...], precision=highest, preferred_element_type=F32)
-    sub = lax.broadcasted_iota(jnp.int32, (8, RAYS), 0)
-    start = jnp.broadcast_to(start_ref[...].astype(F32), (8, RAYS))
-    source_ref[...] = jnp.where(sub == S, start, source)
-
-
 def species_rows(kern_ref):
     sub = lax.broadcasted_iota(jnp.int32, (8, CHAN), 0)
     kern = jnp.zeros((8, CHAN), F32)
@@ -73,9 +62,9 @@
 
 
 def table_kernel(*refs):
-    sources, outs, places, sem = refs[:5], refs[5:9], refs[9:14], refs[14]
+    sources, outs, places, sem = refs[:7], refs[7:11], refs[11:18], refs[18]
     fetch(sources, places, sem)
-    prior_ref, cells_ref, lengths_ref, kern_ref, noise_ref = places
+    prior_ref, cells_ref, lengths_ref, kern_ref, noise_ref, obs_ref, start_ref = places
     table_ref, gram_ref, prior_out, scale_out = outs
     for slot in range(SPAN):
         lanes = slice(slot * RAYS, (slot + 1) * RAYS)
@@ -84,6 +73,10 @@
         table_ref[base + TILE:base + 2 * TILE, :] = lengths_ref[:, lanes]
     kern = species_rows(kern_ref)
     weighted = kern * noise_ref[...]
+    source = jnp.dot(weighted, obs_ref[...], precision=highest, preferred_element_type=F32)
+    sub = lax.broadcasted_iota(jnp.int32, (8, RAYS), 0)
+    start = jnp.broadcast_to(start_ref[...].astype(F32), (8, RAYS))
+    table_ref[TABLE:TABLE + 8, :] = jnp.where(sub == S, start, source)
     wide = jnp.concatenate([kern] * CLAT, axis=0)
     wide_weighted = jnp.concatenate([weighted] * CLAT, axis=0)
     gram = lax.dot_general(wide_weighted, wide, (((1,), (1,)), ((), ())), precision=highest, preferred_element_type=F32)
@@ -104,9 +97,14 @@
     prior_out[...] = prior * scale[0:1, 0:1]
 
 
+def gather_kernel(shards, out):
+    for k in range(ORB):
+        out[:, k * RAYS:(k + 1) * RAYS] = shards[k, TABLE:TABLE + 8, :]
+
+
 def build_kernel(shards, w_ref, lat_ref):
-    sub = lax.broadcasted_iota(jnp.int32, (8, RAYS), 0)
-    odd = (sub & 1) == 1
+    sub = lax.broadcasted_iota(jnp.int32, (16, RAYS), 0)
+    odd = (sub[:8] & 1) == 1
 
     def slot_body(index, carry):
         slot, k = index >> 3, index & 7
@@ -123,7 +121,7 @@
         for j in range(TILE // 2):
             even_key = jnp.broadcast_to(places[2 * j:2 * j + 1, :], (8, RAYS))
             odd_key = jnp.broadcast_to(places[2 * j + 1:2 * j + 2, :], (8, RAYS))
-            keys.append(jnp.where(swap, odd_key, even_key) - sub)
+            keys.append(jnp.where(swap, odd_key, even_key))
             even_len = jnp.broadcast_to(lengths[2 * j:2 * j + 1, :], (8, RAYS))
             odd_len = jnp.broadcast_to(lengths[2 * j + 1:2 * j + 2, :], (8, RAYS))
             sizes.append(jnp.where(swap, odd_len, even_len))
@@ -131,18 +129,22 @@
             for j in range(i + 1, TILE // 2):
                 same = keys[i] == keys[j]
                 sizes[i] = sizes[i] + jnp.where(same, sizes[j], 0.0)
-                keys[j] = jnp.where(same, -64, keys[j])
-        for pair in range(CELL // 16):
-            parts = []
-            for half in range(2):
-                offset = pair * 16 + half * 8
-                total = jnp.zeros((8, RAYS), F32)
-                for key, size in zip(keys, sizes):
-                    total = jnp.where(key == offset, size, total)
-                parts.append(total)
-            high, low = split(jnp.concatenate(parts, axis=0))
-            w_ref[slot, pl.ds(pair * 16, 16), pl.ds(spot, RAYS)] = high
-            w_ref[slot, pl.ds(CELL + pair * 16, 16), pl.ds(spot, RAYS)] = low
+                keys[j] = jnp.where(same, -1024, keys[j])
+        highs, lows = zip(*[split(jnp.concatenate([size, size], axis=0)) for size in sizes])
+        keys = [jnp.concatenate([key, key], axis=0) for key in keys]
+        zero = jnp.zeros((16, RAYS), BF16)
+        for c in range(CLON):
+            levels = [jnp.where((key >> 7) == c, (key & 127) - sub, -64).astype(F32).astype(BF16) for key in keys]
+            for part in range(LEV // 16):
+                high, low = zero, zero
+                target = jnp.full((16, RAYS), part * 16, BF16)
+                for j in range(TILE // 2):
+                    hit = levels[j] == target
+                    high = jnp.where(hit, highs[j], high)
+                    low = jnp.where(hit, lows[j], low)
+                row = c * LEV + part * 16
+                w_ref[slot, pl.ds(row, 16), pl.ds(spot, RAYS)] = high
+                w_ref[slot, pl.ds(CELL + row, 16), pl.ds(spot, RAYS)] = low
         return carry
 
     lax.fori_loop(0, SPAN * ORB, slot_body, 0)
@@ -164,24 +166,26 @@
     return total[:64] + total[64:]
 
 
-def project_first_kernel(v_ref, mask_ref, w_ref, *outs):
-    project_all(v_ref[...], mask_ref, w_ref, *outs)
-
-
-def project_kernel(part_ref, south, north, prior_ref, mask_ref, w_ref, v_ref, *outs):
-    v = with_faces(part_ref[...], south[...], north[...], prior_ref)
+def project_first_kernel(side_ref, v_ref, mask_ref, w_ref, *outs):
+    project_all(side_ref[0] == 1, v_ref[...], mask_ref, w_ref, *outs)
+
+
+def project_kernel(side_ref, part_ref, first, second, prior_ref, mask_ref, w_ref, v_ref, *outs):
+    odd = side_ref[0] == 1
+    v = with_faces(odd, part_ref[...], first[...], second[...], prior_ref)
     v_ref[...] = v
-    project_all(v, mask_ref, w_ref, *outs)
-
-
-def with_faces(part, south, north, prior_ref):
+    project_all(odd, v, mask_ref, w_ref, *outs)
+
+
+def with_faces(odd, part, first, second, prior_ref):
+    south, north = jnp.where(odd, first, second), jnp.where(odd, second, first)
     weight = jnp.concatenate([prior_ref[0:8, :]] * CLON, axis=1)
     return jnp.concatenate([part[0:8] - weight * south, part[8:56], part[56:64] - weight * north], axis=0)
 
 
-def project_all(v, mask_ref, w_ref, own_ref, left_ref, right_ref, left2_ref, right2_ref, down_ref, up_ref):
-    down_ref[...] = v[0:8]
-    up_ref[...] = v[56:64]
+def project_all(odd, v, mask_ref, w_ref, own_ref, left_ref, right_ref, left2_ref, right2_ref, first_ref, second_ref):
+    first_ref[...] = jnp.where(odd, v[0:8], v[56:64])
+    second_ref[...] = jnp.where(odd, v[56:64], v[0:8])
     for l in range(CLAT):
         left_ref[4, :, pl.ds(l * LEV, LEV)] = v[8 * l:8 * l + 8, 0:LEV]
         right_ref[4, :, pl.ds(l * LEV, LEV)] = v[8 * l:8 * l + 8, CELL - LEV:]
@@ -205,12 +209,11 @@
             right2_ref[slot] = total
 
 
-def init_kernel(shards, lat_ref, w_ref, v_ref, mask_ref):
+def init_kernel(z2, z0, z1, z3, z4, lat_ref, w_ref, v_ref, mask_ref):
     sums, lats = [], []
     sub = lax.broadcasted_iota(jnp.int32, (8, SLOT), 0)
-    for slot in range(SPAN):
-        base = TABLE + 8 * slot
-        z = jnp.concatenate([shards[k, base:base + 8, :] for k in range(ORB)], axis=1)
+    for slot, z_ref in enumerate((z0, z1, z2, z3, z4)):
+        z = z_ref[...]
         begin = jnp.broadcast_to(z[S:S + 1, :], (8, SLOT))
         present = (begin <= slot) & (begin + (NT - 1) >= slot)
         lat = jnp.where(present, lat_ref[slot], -1)
@@ -264,9 +267,9 @@
 PAIRS = [(i, j) for i in range(ITERS) for j in range(i, ITERS)] + [(ITERS - 1, ITERS)]
 
 
-def last_kernel(part_ref, south, north, prior_ref, *refs):
+def last_kernel(side_ref, part_ref, first, second, prior_ref, *refs):
     earlier, (out_ref, pair_ref) = refs[:ITERS], refs[ITERS:]
-    v = with_faces(part_ref[...], south[...], north[...], prior_ref)
+    v = with_faces(side_ref[0] == 1, part_ref[...], first[...], second[...], prior_ref)
     out_ref[...] = v
     vectors = [ref[...] for ref in earlier] + [v]
     lane = lax.broadcasted_iota(jnp.int32, (1, LEV), 1)
@@ -353,16 +356,21 @@
 SENT = MESSAGES + (FACE, FACE)
 
 
-def exchange(own, left, right, left2, right2, down, up):
+def pairs_from(start, size):
+    route = [(i, i + 1) for i in range(start, size - 1, 2)]
+    return route + [(j, i) for i, j in route]
+
+
+def exchange(own, left, right, left2, right2, first, second):
     n_lat = lax.axis_size("lat")
     plus1 = shift(left, "lon", -1)
     minus1 = shift(right, "lon", 1)
     plus2 = shift(left2, "lon", -2)
     minus2 = shift(right2, "lon", 2)
-    south = lax.ppermute(up, "lat", [(i, i + 1) for i in range(n_lat - 1)])
-    plus1, down = lax.optimization_barrier((plus1, down))
-    north = lax.ppermute(down, "lat", [(i + 1, i) for i in range(n_lat - 1)])
-    return own, plus1, minus1, plus2, minus2, south, north
+    first = lax.ppermute(first, "lat", pairs_from(0, n_lat))
+    plus1, second = lax.optimization_barrier((plus1, second))
+    second = lax.ppermute(second, "lat", pairs_from(1, n_lat))
+    return own, plus1, minus1, plus2, minus2, first, second
 
 
 def fetching(kernel, outs, scratch, values):
@@ -377,41 +385,37 @@
 
 
 def body(observed, ray_start, tile_cells, tile_lengths, channel_kernel, noise_weight, prior_weight):
-    noise = noise_weight.reshape(1, CHAN)
-    kern_space, noise_space = pltpu.VMEM((S, CHAN), F32), pltpu.VMEM((1, CHAN), F32)
-    (z,) = fetching(
-        source_kernel,
-        (shape(8, RAYS),),
-        (pltpu.VMEM((CHAN, RAYS), F32), pltpu.VMEM((1, RAYS), jnp.int32), kern_space, noise_space),
-        (observed.T, ray_start.reshape(1, RAYS), channel_kernel, noise),
-    )
-    z1, z3 = shift(z, "lon", -1), shift(z, "lon", 1)
-    z0, z4 = shift(z, "lon", -2), shift(z, "lon", 2)
+    side = (lax.axis_index("lat") & 1).astype(jnp.int32).reshape(1)
     table, gram, prior, scale = fetching(
         table_kernel,
-        (shape(TABLE, RAYS), shape(64, 64), shape(64, LEV), shape(8, LEV)),
+        (shape(TABLE + 8, RAYS), shape(64, 64), shape(64, LEV), shape(8, LEV)),
         (
             pltpu.SMEM((S,), F32),
             pltpu.VMEM((TILE, SPAN * RAYS), jnp.int32),
             pltpu.VMEM((TILE, SPAN * RAYS), F32),
-            kern_space,
-            noise_space,
+            pltpu.VMEM((S, CHAN), F32),
+            pltpu.VMEM((1, CHAN), F32),
+            pltpu.VMEM((CHAN, RAYS), F32),
+            pltpu.VMEM((1, RAYS), jnp.int32),
         ),
-        (prior_weight, tile_cells.T, tile_lengths.T, channel_kernel, noise),
+        (prior_weight, tile_cells.T, tile_lengths.T, channel_kernel, noise_weight.reshape(1, CHAN), observed.T, ray_start.reshape(1, RAYS)),
     )
-    shards = lax.all_gather(jnp.concatenate([table, z0, z1, z, z3, z4], axis=0), "orbit")
+    shards = lax.all_gather(table, "orbit")
+    (z,) = call(gather_kernel, (shape(8, SLOT),), 1)(shards)
+    z1, z3 = shift(z, "lon", -1), shift(z, "lon", 1)
+    z0, z4 = shift(z, "lon", -2), shift(z, "lon", 2)
     w, lat = call(build_kernel, (shape(SPAN, 2 * CELL, SLOT, dtype=BF16), shape(SPAN, 8, SLOT, dtype=jnp.int32)), 1, work=BUILD)(shards)
-    v, mask = call(init_kernel, (FIELD, shape(SPAN, 8, SLOT, dtype=jnp.int32)), 3, work=MATMUL)(shards, lat, w)
+    v, mask = call(init_kernel, (FIELD, shape(SPAN, 8, SLOT, dtype=jnp.int32)), 7, work=MATMUL)(z, z0, z1, z3, z4, lat, w)
     vectors = [v]
-    sent = call(project_first_kernel, SENT, 3, work=MATMUL)(v, mask, w)
+    sent = call(project_first_kernel, SENT, 3, True, work=MATMUL)(side, v, mask, w)
     for turn in range(ITERS):
-        *sums, south, north = exchange(*sent)
+        *sums, first, second = exchange(*sent)
         (part,) = call(step_kernel, (FIELD,), 10, work=MATMUL)(v, *sums, mask, w, gram, prior)
         if turn < ITERS - 1:
-            v, *sent = call(project_kernel, (FIELD,) + SENT, 6, work=MATMUL)(part, south, north, prior, mask, w)
+            v, *sent = call(project_kernel, (FIELD,) + SENT, 6, True, work=MATMUL)(side, part, first, second, prior, mask, w)
             vectors.append(v)
     peers = lax.axis_size("lon") * lax.axis_size("lat")
-    v, pairs = call(last_kernel, (FIELD, shape(peers, LEV)), 4 + ITERS)(part, south, north, prior, *vectors)
+    v, pairs = call(last_kernel, (FIELD, shape(peers, LEV)), 4 + ITERS, True)(side, part, first, second, prior, *vectors)
     vectors.append(v)
     pairs = lax.all_to_all(pairs, ("lon", "lat"), 0, 0, tiled=True)
     field = shape(S, CLON, CLAT, LEV)

time: 156 us -> 151 us (0.968)
  starting transfers between devices: 75.4 us -> 66.6 us
  blocking collectives: 42.8 us -> 46.8 us
  Pallas kernels: 34.4 us -> 32.7 us
    ppermute x20, starting transfers between devices: 55 us -> 47.6 us  [shift(): lax.ppermute(block, axis, [(i, (i + distance) % size) for i in range(size)])]
    all_gather x1, blocking collectives: 23.3 us -> 27.5 us  [body(): shards = lax.all_gather(table, 'orbit')]
    pallas_call x6 -> x7, Pallas kernels: 9.32 us -> 9.34 us  [the longest x3 4.63 us: body(): call(project_kernel, (FIELD,) + SENT, 6, True, work=MATMUL)]
  transfers between devices with their start and end apart: 28 -> 28, of which waited for: 1 -> 2; matrix products, arithmetic and copies ran while one was open for 0% -> 0% of each run, Pallas kernels for 9% -> 14%
where the time goes in v6:
time: 151 us; the launch traced here: 150 us
  starting transfers between devices  66.6 us (44%)
  blocking collectives  46.8 us (31%)
  Pallas kernels  32.7 us (22%)
  waiting for transfers between devices  2.69 us (2%)
    ppermute x20, starting transfers between devices, shift(): lax.ppermute(block, axis, [(i, (i + distance) % size) for i in range(size)])  47.6 us
    all_gather x1, blocking collectives, body(): shards = lax.all_gather(table, 'orbit')  27.5 us
    all_to_all x1, blocking collectives, body(): pairs = lax.all_to_all(pairs, ('lon', 'lat'), 0, 0, tiled=True)  19.4 us
    ppermute x4, starting transfers between devices, exchange(): first = lax.ppermute(first, 'lat', pairs_from(0, n_lat))  16.2 us
    pallas_call x4, Pallas kernels, body(): call(step_kernel, (FIELD,), 10, work=MATMUL)(v, *sums, mask, w, gram, prior)  13.2 us
    pallas_call x1, Pallas kernels, body(): call(build_kernel, (shape(SPAN, 2 * CELL, SLOT, dtype=BF16), shape(SPAN,...  7.54 us
    pallas_call x3, Pallas kernels, body(): call(project_kernel, (FIELD,) + SENT, 6, True, work=MATMUL)  4.63 us
  transfers between devices with their start and end apart: 28, of which 2 were waited for; matrix products, arithmetic and copies ran while one was open for 0% of the time, Pallas kernels for 14%

profile of v6, /device:TPU:1, one launch (start us, length us, event | category | flops | bytes accessed | tf_op | source)
XLA Modules:
  0.0 149.9 jit_solution(3773451797304475046)
XLA Ops:
  1.9 27.5 %all-gather = f32[1344,128]{1,0:T(8,128)S(1)} all-gather(f32[168,128]{1,0:T(8,128)S(1)} %get-tuple-element.52), channel_id=2, replica_groups=mesh['orbit'=8,'lon'=16,'lat'=4] {'orbit'}, dimensions={0}, use_global_device_ids=true | all-gather | bytes 774144 | tf_op jit(solution)/shard_map/all_gather | solution.py:403
  29.3 3.2 %collective-permute-start.3 = (f32[8,1024]{1,0:T(8,128)S(1)}, f32[8,1024]{1,0:T(8,128)S(1)}, u32[]{:S(2)}, u32[]{:S(2)}) collective-permute-start(f32[8,1024]{1,0:T(8,128)S(1)} %shard_map.87.z2), channel_id=1, source_target_pairs={{0,8},{4,12},{8,16},{12,20},{16,24},{20,28},{24,32},{28,36},{32,40... | collective-permute-start | bytes 98312 | tf_op jit(solution)/shard_map/ppermute | solution.py:39
  32.5 7.7 %collective-permute-start.2 = (f32[8,1024]{1,0:T(8,128)S(1)}, f32[8,1024]{1,0:T(8,128)S(1)}, u32[]{:S(2)}, u32[]{:S(2)}) collective-permute-start(f32[8,1024]{1,0:T(8,128)S(1)} %shard_map.87.z2), channel_id=1, source_target_pairs={{0,4},{4,8},{8,12},{12,16},{16,20},{20,24},{24,28},{28,32},{32,36}... | collective-permute-start | bytes 98312 | tf_op jit(solution)/shard_map/ppermute | solution.py:39
  40.2 3.3 %collective-permute-start = (f32[8,1024]{1,0:T(8,128)S(1)}, f32[8,1024]{1,0:T(8,128)S(1)}, u32[]{:S(2)}, u32[]{:S(2)}) collective-permute-start(f32[8,1024]{1,0:T(8,128)S(1)} %shard_map.87.z2), channel_id=1, source_target_pairs={{0,56},{4,60},{8,0},{12,4},{16,8},{20,12},{24,16},{28,20},{32,24},... | collective-permute-start | bytes 98312 | tf_op jit(solution)/shard_map/ppermute | solution.py:39
  43.5 7.5 %shard_map.88 = (bf16[5,1024,1024]{2,1,0:T(8,128)(2,1)S(1)}, s32[5,8,1024]{2,1,0:T(8,128)S(1)}) custom-call(f32[8,168,128]{2,1,0:T(8,128)S(1)} %bitcast.12), custom_call_target="tpu_custom_call" | custom-call | flops 671088640 | bytes 20971520 | tf_op jit(solution)/shard_map/pallas_call | solution.py:407
  51.1 2.9 %shard_map.89 = (f32[64,512]{1,0:T(8,128)S(1)}, s32[5,8,1024]{2,1,0:T(8,128)S(1)}) custom-call(f32[8,1024]{1,0:T(8,128)S(1)} %shard_map.87.z2, f32[8,1024]{1,0:T(8,128)S(1)} %collective-permute-done.z0, f32[8,1024]{1,0:T(8,128)S(1)} %collective-permute-done.1.z1, f32[8,1024]{1,0:T(8,128)S(1)} %collective-permute-done.2.z3, ...), custom_call_target="tpu_custom_call" | custom-call | flops 1342177280 | bytes 10485760 | tf_op jit(solution)/shard_map/pallas_call | solution.py:408
  57.7 3.6 %collective-permute-start.6 = (f32[3,8,1024]{2,1,0:T(8,128)S(1)}, f32[3,8,1024]{2,1,0:T(8,128)S(1)}, u32[]{:S(2)}, u32[]{:S(2)}) collective-permute-start(f32[3,8,1024]{2,1,0:T(8,128)S(1)} %get-tuple-element.62), channel_id=1, source_target_pairs={{0,56},{4,60},{8,0},{12,4},{16,8},{20,12},{24,16},{28,20},{32,24},... | collective-permute-start | bytes 294920 | tf_op jit(solution)/shard_map/ppermute | solution.py:39
  61.3 1.9 %collective-permute-start.7 = (f32[3,8,1024]{2,1,0:T(8,128)S(1)}, f32[3,8,1024]{2,1,0:T(8,128)S(1)}, u32[]{:S(2)}, u32[]{:S(2)}) collective-permute-start(f32[3,8,1024]{2,1,0:T(8,128)S(1)} %get-tuple-element.63), channel_id=1, source_target_pairs={{0,8},{4,12},{8,16},{12,20},{16,24},{20,28},{24,32},{28,36},{32,40... | collective-permute-start | bytes 294920 | tf_op jit(solution)/shard_map/ppermute | solution.py:39
  63.2 3.1 %collective-permute-start.8 = (f32[8,512]{1,0:T(8,128)S(1)}, f32[8,512]{1,0:T(8,128)S(1)}, u32[]{:S(2)}, u32[]{:S(2)}) collective-permute-start(f32[8,512]{1,0:T(8,128)S(1)} %get-tuple-element.66), channel_id=1, source_target_pairs={{0,1},{2,3},{1,0},{3,2},{4,5},{6,7},{5,4},{7,6},{8,9},{10,11},{9,8... | collective-permute-start | bytes 49160 | tf_op jit(solution)/shard_map/ppermute | solution.py:370
  67.1 1.9 %collective-permute-done.7.minus2 = f32[3,8,1024]{2,1,0:T(8,128)S(1)} collective-permute-done((f32[3,8,1024]{2,1,0:T(8,128)S(1)}, f32[3,8,1024]{2,1,0:T(8,128)S(1)}, u32[]{:S(2)}, u32[]{:S(2)}) %collective-permute-start.7) | collective-permute-done | bytes 98336 | tf_op jit(solution)/shard_map/ppermute | solution.py:39
  68.9 3.3 %shard_map.91.part_ref = f32[64,512]{1,0:T(8,128)S(1)} custom-call(f32[64,512]{1,0:T(8,128)S(1)} %get-tuple-element.55.v_ref.refs_0_.refs_1_, f32[5,8,1024]{2,1,0:T(8,128)S(1)} %get-tuple-element.57.own_ref, f32[5,8,1024]{2,1,0:T(8,128)S(1)} %collective-permute-done.4.plus1, f32[5,8,1024]{2,1,0:T(8,128)S(1)} %collective-permute-done.5.minus1, ...), custom_call_target="tpu_custom_call" | custom-call | flops 1342177280 | bytes 10485760 | tf_op jit(solution)/shard_map/pallas_call | solution.py:413
  75.6 4.0 %collective-permute-start.12 = (f32[3,8,1024]{2,1,0:T(8,128)S(1)}, f32[3,8,1024]{2,1,0:T(8,128)S(1)}, u32[]{:S(2)}, u32[]{:S(2)}) collective-permute-start(f32[3,8,1024]{2,1,0:T(8,128)S(1)} %get-tuple-element.74), channel_id=1, source_target_pairs={{0,56},{4,60},{8,0},{12,4},{16,8},{20,12},{24,16},{28,20},{32,24},... | collective-permute-start | bytes 294920 | tf_op jit(solution)/shard_map/ppermute | solution.py:39
  79.5 1.9 %collective-permute-start.13 = (f32[3,8,1024]{2,1,0:T(8,128)S(1)}, f32[3,8,1024]{2,1,0:T(8,128)S(1)}, u32[]{:S(2)}, u32[]{:S(2)}) collective-permute-start(f32[3,8,1024]{2,1,0:T(8,128)S(1)} %get-tuple-element.75), channel_id=1, source_target_pairs={{0,8},{4,12},{8,16},{12,20},{16,24},{20,28},{24,32},{28,36},{32,40... | collective-permute-start | bytes 294920 | tf_op jit(solution)/shard_map/ppermute | solution.py:39
  81.5 5.3 %collective-permute-start.14 = (f32[8,512]{1,0:T(8,128)S(1)}, f32[8,512]{1,0:T(8,128)S(1)}, u32[]{:S(2)}, u32[]{:S(2)}) collective-permute-start(f32[8,512]{1,0:T(8,128)S(1)} %get-tuple-element.76), channel_id=1, source_target_pairs={{0,1},{2,3},{1,0},{3,2},{4,5},{6,7},{5,4},{7,6},{8,9},{10,11},{9,8... | collective-permute-start | bytes 49160 | tf_op jit(solution)/shard_map/ppermute | solution.py:370
  87.7 3.3 %shard_map.93.part_ref = f32[64,512]{1,0:T(8,128)S(1)} custom-call(f32[64,512]{1,0:T(8,128)S(1)} %get-tuple-element.68.v_ref.refs_1_.refs_2_, f32[5,8,1024]{2,1,0:T(8,128)S(1)} %get-tuple-element.69.own_ref, f32[5,8,1024]{2,1,0:T(8,128)S(1)} %collective-permute-done.10.plus1, f32[5,8,1024]{2,1,0:T(8,128)S(1)} %collective-permute-done.11.minus1, ...), custom_call_target="tpu_custom_call" | custom-call | flops 1342177280 | bytes 10485760 | tf_op jit(solution)/shard_map/pallas_call | solution.py:413
  94.3 5.8 %collective-permute-start.18 = (f32[3,8,1024]{2,1,0:T(8,128)S(1)}, f32[3,8,1024]{2,1,0:T(8,128)S(1)}, u32[]{:S(2)}, u32[]{:S(2)}) collective-permute-start(f32[3,8,1024]{2,1,0:T(8,128)S(1)} %get-tuple-element.84), channel_id=1, source_target_pairs={{0,56},{4,60},{8,0},{12,4},{16,8},{20,12},{24,16},{28,20},{32,24},... | collective-permute-start | bytes 294920 | tf_op jit(solution)/shard_map/ppermute | solution.py:39
  100.1 1.9 %collective-permute-start.19 = (f32[3,8,1024]{2,1,0:T(8,128)S(1)}, f32[3,8,1024]{2,1,0:T(8,128)S(1)}, u32[]{:S(2)}, u32[]{:S(2)}) collective-permute-start(f32[3,8,1024]{2,1,0:T(8,128)S(1)} %get-tuple-element.85), channel_id=1, source_target_pairs={{0,8},{4,12},{8,16},{12,20},{16,24},{20,28},{24,32},{28,36},{32,40... | collective-permute-start | bytes 294920 | tf_op jit(solution)/shard_map/ppermute | solution.py:39
  102.0 3.2 %collective-permute-start.20 = (f32[8,512]{1,0:T(8,128)S(1)}, f32[8,512]{1,0:T(8,128)S(1)}, u32[]{:S(2)}, u32[]{:S(2)}) collective-permute-start(f32[8,512]{1,0:T(8,128)S(1)} %get-tuple-element.86), channel_id=1, source_target_pairs={{0,1},{2,3},{1,0},{3,2},{4,5},{6,7},{5,4},{7,6},{8,9},{10,11},{9,8... | collective-permute-start | bytes 49160 | tf_op jit(solution)/shard_map/ppermute | solution.py:370
  106.7 3.3 %shard_map.95.part_ref = f32[64,512]{1,0:T(8,128)S(1)} custom-call(f32[64,512]{1,0:T(8,128)S(1)} %get-tuple-element.78.v_ref.refs_2_.refs_3_, f32[5,8,1024]{2,1,0:T(8,128)S(1)} %get-tuple-element.79.own_ref, f32[5,8,1024]{2,1,0:T(8,128)S(1)} %collective-permute-done.16.plus1, f32[5,8,1024]{2,1,0:T(8,128)S(1)} %collective-permute-done.17.minus1, ...), custom_call_target="tpu_custom_call" | custom-call | flops 1342177280 | bytes 10485760 | tf_op jit(solution)/shard_map/pallas_call | solution.py:413
  113.3 5.1 %collective-permute-start.24 = (f32[3,8,1024]{2,1,0:T(8,128)S(1)}, f32[3,8,1024]{2,1,0:T(8,128)S(1)}, u32[]{:S(2)}, u32[]{:S(2)}) collective-permute-start(f32[3,8,1024]{2,1,0:T(8,128)S(1)} %get-tuple-element.94), channel_id=1, source_target_pairs={{0,56},{4,60},{8,0},{12,4},{16,8},{20,12},{24,16},{28,20},{32,24},... | collective-permute-start | bytes 294920 | tf_op jit(solution)/shard_map/ppermute | solution.py:39
  118.4 1.9 %collective-permute-start.25 = (f32[3,8,1024]{2,1,0:T(8,128)S(1)}, f32[3,8,1024]{2,1,0:T(8,128)S(1)}, u32[]{:S(2)}, u32[]{:S(2)}) collective-permute-start(f32[3,8,1024]{2,1,0:T(8,128)S(1)} %get-tuple-element.95), channel_id=1, source_target_pairs={{0,8},{4,12},{8,16},{12,20},{16,24},{20,28},{24,32},{28,36},{32,40... | collective-permute-start | bytes 294920 | tf_op jit(solution)/shard_map/ppermute | solution.py:39
  120.3 4.6 %collective-permute-start.26 = (f32[8,512]{1,0:T(8,128)S(1)}, f32[8,512]{1,0:T(8,128)S(1)}, u32[]{:S(2)}, u32[]{:S(2)}) collective-permute-start(f32[8,512]{1,0:T(8,128)S(1)} %get-tuple-element.96), channel_id=1, source_target_pairs={{0,1},{2,3},{1,0},{3,2},{4,5},{6,7},{5,4},{7,6},{8,9},{10,11},{9,8... | collective-permute-start | bytes 49160 | tf_op jit(solution)/shard_map/ppermute | solution.py:370
  125.6 3.3 %shard_map.97.part_ref = f32[64,512]{1,0:T(8,128)S(1)} custom-call(f32[64,512]{1,0:T(8,128)S(1)} %get-tuple-element.88.v_ref.refs_3_.refs_4_, f32[5,8,1024]{2,1,0:T(8,128)S(1)} %get-tuple-element.89.own_ref, f32[5,8,1024]{2,1,0:T(8,128)S(1)} %collective-permute-done.22.plus1, f32[5,8,1024]{2,1,0:T(8,128)S(1)} %collective-permute-done.23.minus1, ...), custom_call_target="tpu_custom_call" | custom-call | flops 1342177280 | bytes 10485760 | tf_op jit(solution)/shard_map/pallas_call | solution.py:413
  129.2 19.4 %all_to_all.11 = f32[64,1,128]{2,1,0:T(1,128)S(1)} all-to-all(f32[64,1,128]{2,1,0:T(1,128)S(1)} %bitcast.14), channel_id=1, replica_groups=mesh['orbit'=8,'lon'=16,'lat'=4] {'lon','lat'}, dimensions={0} | all-to-all | bytes 65536 | tf_op jit(solution)/shard_map/all_to_all | solution.py:420
  (48 shorter events, 20.0 us)
Async XLA Ops:
  29.3 21.8 %collective-permute-start.3 = (f32[8,1024]{1,0:T(8,128)S(1)}, f32[8,1024]{1,0:T(8,128)S(1)}, u32[]{:S(2)}, u32[]{:S(2)}) collective-permute-start(f32[8,1024]{1,0:T(8,128)S(1)} %shard_map.87.z2), channel_id=1, source_target_pairs={{0,8},{4,12},{8,16},{12,20},{16,24},{20,28},{24,32},{28,36},{32,40... | collective-permute-start | bytes 98312 | tf_op jit(solution)/shard_map/ppermute | solution.py:39
  32.5 18.6 %collective-permute-start.2 = (f32[8,1024]{1,0:T(8,128)S(1)}, f32[8,1024]{1,0:T(8,128)S(1)}, u32[]{:S(2)}, u32[]{:S(2)}) collective-permute-start(f32[8,1024]{1,0:T(8,128)S(1)} %shard_map.87.z2), channel_id=1, source_target_pairs={{0,4},{4,8},{8,12},{12,16},{16,20},{20,24},{24,28},{28,32},{32,36}... | collective-permute-start | bytes 98312 | tf_op jit(solution)/shard_map/ppermute | solution.py:39
  40.2 10.9 %collective-permute-start.1 = (f32[8,1024]{1,0:T(8,128)S(1)}, f32[8,1024]{1,0:T(8,128)S(1)}, u32[]{:S(2)}, u32[]{:S(2)}) collective-permute-start(f32[8,1024]{1,0:T(8,128)S(1)} %shard_map.87.z2), channel_id=1, source_target_pairs={{0,60},{4,0},{8,4},{12,8},{16,12},{20,16},{24,20},{28,24},{32,28},... | collective-permute-start | bytes 98312 | tf_op jit(solution)/shard_map/ppermute | solution.py:39
  40.2 10.9 %collective-permute-start = (f32[8,1024]{1,0:T(8,128)S(1)}, f32[8,1024]{1,0:T(8,128)S(1)}, u32[]{:S(2)}, u32[]{:S(2)}) collective-permute-start(f32[8,1024]{1,0:T(8,128)S(1)} %shard_map.87.z2), channel_id=1, source_target_pairs={{0,56},{4,60},{8,0},{12,4},{16,8},{20,12},{24,16},{28,20},{32,24},... | collective-permute-start | bytes 98312 | tf_op jit(solution)/shard_map/ppermute | solution.py:39
  55.6 10.8 %collective-permute-start.4 = (f32[5,8,1024]{2,1,0:T(8,128)S(1)}, f32[5,8,1024]{2,1,0:T(8,128)S(1)}, u32[]{:S(2)}, u32[]{:S(2)}) collective-permute-start(f32[5,8,1024]{2,1,0:T(8,128)S(1)} %get-tuple-element.58), channel_id=1, source_target_pairs={{0,60},{4,0},{8,4},{12,8},{16,12},{20,16},{24,20},{28,24},{32,28},... | collective-permute-start | bytes 491528 | tf_op jit(solution)/shard_map/ppermute | solution.py:39
  56.7 12.2 %collective-permute-start.5 = (f32[5,8,1024]{2,1,0:T(8,128)S(1)}, f32[5,8,1024]{2,1,0:T(8,128)S(1)}, u32[]{:S(2)}, u32[]{:S(2)}) collective-permute-start(f32[5,8,1024]{2,1,0:T(8,128)S(1)} %get-tuple-element.61), channel_id=1, source_target_pairs={{0,4},{4,8},{8,12},{12,16},{16,20},{20,24},{24,28},{28,32},{32,36}... | collective-permute-start | bytes 491528 | tf_op jit(solution)/shard_map/ppermute | solution.py:39
  57.7 9.4 %collective-permute-start.6 = (f32[3,8,1024]{2,1,0:T(8,128)S(1)}, f32[3,8,1024]{2,1,0:T(8,128)S(1)}, u32[]{:S(2)}, u32[]{:S(2)}) collective-permute-start(f32[3,8,1024]{2,1,0:T(8,128)S(1)} %get-tuple-element.62), channel_id=1, source_target_pairs={{0,56},{4,60},{8,0},{12,4},{16,8},{20,12},{24,16},{28,20},{32,24},... | collective-permute-start | bytes 294920 | tf_op jit(solution)/shard_map/ppermute | solution.py:39
  61.3 7.6 %collective-permute-start.7 = (f32[3,8,1024]{2,1,0:T(8,128)S(1)}, f32[3,8,1024]{2,1,0:T(8,128)S(1)}, u32[]{:S(2)}, u32[]{:S(2)}) collective-permute-start(f32[3,8,1024]{2,1,0:T(8,128)S(1)} %get-tuple-element.63), channel_id=1, source_target_pairs={{0,8},{4,12},{8,16},{12,20},{16,24},{20,28},{24,32},{28,36},{32,40... | collective-permute-start | bytes 294920 | tf_op jit(solution)/shard_map/ppermute | solution.py:39
  63.2 9.0 %collective-permute-start.8 = (f32[8,512]{1,0:T(8,128)S(1)}, f32[8,512]{1,0:T(8,128)S(1)}, u32[]{:S(2)}, u32[]{:S(2)}) collective-permute-start(f32[8,512]{1,0:T(8,128)S(1)} %get-tuple-element.66), channel_id=1, source_target_pairs={{0,1},{2,3},{1,0},{3,2},{4,5},{6,7},{5,4},{7,6},{8,9},{10,11},{9,8... | collective-permute-start | bytes 49160 | tf_op jit(solution)/shard_map/ppermute | solution.py:370
  73.8 12.9 %collective-permute-start.10 = (f32[5,8,1024]{2,1,0:T(8,128)S(1)}, f32[5,8,1024]{2,1,0:T(8,128)S(1)}, u32[]{:S(2)}, u32[]{:S(2)}) collective-permute-start(f32[5,8,1024]{2,1,0:T(8,128)S(1)} %get-tuple-element.70), channel_id=1, source_target_pairs={{0,60},{4,0},{8,4},{12,8},{16,12},{20,16},{24,20},{28,24},{32,28},... | collective-permute-start | bytes 491528 | tf_op jit(solution)/shard_map/ppermute | solution.py:39
  74.5 13.1 %collective-permute-start.11 = (f32[5,8,1024]{2,1,0:T(8,128)S(1)}, f32[5,8,1024]{2,1,0:T(8,128)S(1)}, u32[]{:S(2)}, u32[]{:S(2)}) collective-permute-start(f32[5,8,1024]{2,1,0:T(8,128)S(1)} %get-tuple-element.73), channel_id=1, source_target_pairs={{0,4},{4,8},{8,12},{12,16},{16,20},{20,24},{24,28},{28,32},{32,36}... | collective-permute-start | bytes 491528 | tf_op jit(solution)/shard_map/ppermute | solution.py:39
  75.6 12.1 %collective-permute-start.12 = (f32[3,8,1024]{2,1,0:T(8,128)S(1)}, f32[3,8,1024]{2,1,0:T(8,128)S(1)}, u32[]{:S(2)}, u32[]{:S(2)}) collective-permute-start(f32[3,8,1024]{2,1,0:T(8,128)S(1)} %get-tuple-element.74), channel_id=1, source_target_pairs={{0,56},{4,60},{8,0},{12,4},{16,8},{20,12},{24,16},{28,20},{32,24},... | collective-permute-start | bytes 294920 | tf_op jit(solution)/shard_map/ppermute | solution.py:39
  79.5 8.1 %collective-permute-start.13 = (f32[3,8,1024]{2,1,0:T(8,128)S(1)}, f32[3,8,1024]{2,1,0:T(8,128)S(1)}, u32[]{:S(2)}, u32[]{:S(2)}) collective-permute-start(f32[3,8,1024]{2,1,0:T(8,128)S(1)} %get-tuple-element.75), channel_id=1, source_target_pairs={{0,8},{4,12},{8,16},{12,20},{16,24},{20,28},{24,32},{28,36},{32,40... | collective-permute-start | bytes 294920 | tf_op jit(solution)/shard_map/ppermute | solution.py:39
  81.5 9.5 %collective-permute-start.14 = (f32[8,512]{1,0:T(8,128)S(1)}, f32[8,512]{1,0:T(8,128)S(1)}, u32[]{:S(2)}, u32[]{:S(2)}) collective-permute-start(f32[8,512]{1,0:T(8,128)S(1)} %get-tuple-element.76), channel_id=1, source_target_pairs={{0,1},{2,3},{1,0},{3,2},{4,5},{6,7},{5,4},{7,6},{8,9},{10,11},{9,8... | collective-permute-start | bytes 49160 | tf_op jit(solution)/shard_map/ppermute | solution.py:370
  92.5 12.7 %collective-permute-start.16 = (f32[5,8,1024]{2,1,0:T(8,128)S(1)}, f32[5,8,1024]{2,1,0:T(8,128)S(1)}, u32[]{:S(2)}, u32[]{:S(2)}) collective-permute-start(f32[5,8,1024]{2,1,0:T(8,128)S(1)} %get-tuple-element.80), channel_id=1, source_target_pairs={{0,60},{4,0},{8,4},{12,8},{16,12},{20,16},{24,20},{28,24},{32,28},... | collective-permute-start | bytes 491528 | tf_op jit(solution)/shard_map/ppermute | solution.py:39
  92.6 14.1 %collective-permute-start.17 = (f32[5,8,1024]{2,1,0:T(8,128)S(1)}, f32[5,8,1024]{2,1,0:T(8,128)S(1)}, u32[]{:S(2)}, u32[]{:S(2)}) collective-permute-start(f32[5,8,1024]{2,1,0:T(8,128)S(1)} %get-tuple-element.83), channel_id=1, source_target_pairs={{0,4},{4,8},{8,12},{12,16},{16,20},{20,24},{24,28},{28,32},{32,36}... | collective-permute-start | bytes 491528 | tf_op jit(solution)/shard_map/ppermute | solution.py:39
  94.3 11.6 %collective-permute-start.18 = (f32[3,8,1024]{2,1,0:T(8,128)S(1)}, f32[3,8,1024]{2,1,0:T(8,128)S(1)}, u32[]{:S(2)}, u32[]{:S(2)}) collective-permute-start(f32[3,8,1024]{2,1,0:T(8,128)S(1)} %get-tuple-element.84), channel_id=1, source_target_pairs={{0,56},{4,60},{8,0},{12,4},{16,8},{20,12},{24,16},{28,20},{32,24},... | collective-permute-start | bytes 294920 | tf_op jit(solution)/shard_map/ppermute | solution.py:39
  100.1 6.6 %collective-permute-start.19 = (f32[3,8,1024]{2,1,0:T(8,128)S(1)}, f32[3,8,1024]{2,1,0:T(8,128)S(1)}, u32[]{:S(2)}, u32[]{:S(2)}) collective-permute-start(f32[3,8,1024]{2,1,0:T(8,128)S(1)} %get-tuple-element.85), channel_id=1, source_target_pairs={{0,8},{4,12},{8,16},{12,20},{16,24},{20,28},{24,32},{28,36},{32,40... | collective-permute-start | bytes 294920 | tf_op jit(solution)/shard_map/ppermute | solution.py:39
  102.0 8.0 %collective-permute-start.20 = (f32[8,512]{1,0:T(8,128)S(1)}, f32[8,512]{1,0:T(8,128)S(1)}, u32[]{:S(2)}, u32[]{:S(2)}) collective-permute-start(f32[8,512]{1,0:T(8,128)S(1)} %get-tuple-element.86), channel_id=1, source_target_pairs={{0,1},{2,3},{1,0},{3,2},{4,5},{6,7},{5,4},{7,6},{8,9},{10,11},{9,8... | collective-permute-start | bytes 49160 | tf_op jit(solution)/shard_map/ppermute | solution.py:370
  111.5 13.4 %collective-permute-start.22 = (f32[5,8,1024]{2,1,0:T(8,128)S(1)}, f32[5,8,1024]{2,1,0:T(8,128)S(1)}, u32[]{:S(2)}, u32[]{:S(2)}) collective-permute-start(f32[5,8,1024]{2,1,0:T(8,128)S(1)} %get-tuple-element.90), channel_id=1, source_target_pairs={{0,60},{4,0},{8,4},{12,8},{16,12},{20,16},{24,20},{28,24},{32,28},... | collective-permute-start | bytes 491528 | tf_op jit(solution)/shard_map/ppermute | solution.py:39
  111.6 14.0 %collective-permute-start.23 = (f32[5,8,1024]{2,1,0:T(8,128)S(1)}, f32[5,8,1024]{2,1,0:T(8,128)S(1)}, u32[]{:S(2)}, u32[]{:S(2)}) collective-permute-start(f32[5,8,1024]{2,1,0:T(8,128)S(1)} %get-tuple-element.93), channel_id=1, source_target_pairs={{0,4},{4,8},{8,12},{12,16},{16,20},{20,24},{24,28},{28,32},{32,36}... | collective-permute-start | bytes 491528 | tf_op jit(solution)/shard_map/ppermute | solution.py:39
  113.3 12.3 %collective-permute-start.24 = (f32[3,8,1024]{2,1,0:T(8,128)S(1)}, f32[3,8,1024]{2,1,0:T(8,128)S(1)}, u32[]{:S(2)}, u32[]{:S(2)}) collective-permute-start(f32[3,8,1024]{2,1,0:T(8,128)S(1)} %get-tuple-element.94), channel_id=1, source_target_pairs={{0,56},{4,60},{8,0},{12,4},{16,8},{20,12},{24,16},{28,20},{32,24},... | collective-permute-start | bytes 294920 | tf_op jit(solution)/shard_map/ppermute | solution.py:39
  118.4 7.2 %collective-permute-start.25 = (f32[3,8,1024]{2,1,0:T(8,128)S(1)}, f32[3,8,1024]{2,1,0:T(8,128)S(1)}, u32[]{:S(2)}, u32[]{:S(2)}) collective-permute-start(f32[3,8,1024]{2,1,0:T(8,128)S(1)} %get-tuple-element.95), channel_id=1, source_target_pairs={{0,8},{4,12},{8,16},{12,20},{16,24},{20,28},{24,32},{28,36},{32,40... | collective-permute-start | bytes 294920 | tf_op jit(solution)/shard_map/ppermute | solution.py:39
  120.3 8.6 %collective-permute-start.26 = (f32[8,512]{1,0:T(8,128)S(1)}, f32[8,512]{1,0:T(8,128)S(1)}, u32[]{:S(2)}, u32[]{:S(2)}) collective-permute-start(f32[8,512]{1,0:T(8,128)S(1)} %get-tuple-element.96), channel_id=1, source_target_pairs={{0,1},{2,3},{1,0},{3,2},{4,5},{6,7},{5,4},{7,6},{8,9},{10,11},{9,8... | collective-permute-start | bytes 49160 | tf_op jit(solution)/shard_map/ppermute | solution.py:370
  (4 other events, 18.9 us)

commit v7 on v6

--- a/solution.py
+++ b/solution.py
@@ -23,7 +23,7 @@
 BF16 = jnp.bfloat16
 highest = lax.Precision.HIGHEST
 VMEM = pltpu.VMEM
-LIMIT = pltpu.CompilerParams(vmem_limit_bytes=24 << 20)
+LIMIT = pltpu.CompilerParams(vmem_limit_bytes=16 << 20)
 
 
 def vspec():
@@ -102,7 +102,7 @@
         out[:, k * RAYS:(k + 1) * RAYS] = shards[k, TABLE:TABLE + 8, :]
 
 
-def build_kernel(shards, w_ref, lat_ref):
+def build_kernel(shards, w_ref, wt_ref, lat_ref):
     sub = lax.broadcasted_iota(jnp.int32, (16, RAYS), 0)
     odd = (sub[:8] & 1) == 1
 
@@ -135,6 +135,7 @@
         zero = jnp.zeros((16, RAYS), BF16)
         for c in range(CLON):
             levels = [jnp.where((key >> 7) == c, (key & 127) - sub, -64).astype(F32).astype(BF16) for key in keys]
+            high_parts, low_parts = [], []
             for part in range(LEV // 16):
                 high, low = zero, zero
                 target = jnp.full((16, RAYS), part * 16, BF16)
@@ -145,6 +146,10 @@
                 row = c * LEV + part * 16
                 w_ref[slot, pl.ds(row, 16), pl.ds(spot, RAYS)] = high
                 w_ref[slot, pl.ds(CELL + row, 16), pl.ds(spot, RAYS)] = low
+                high_parts.append(high)
+                low_parts.append(low)
+            wt_ref[slot, pl.ds(spot, RAYS), c * LEV:(c + 1) * LEV] = jnp.concatenate(high_parts, axis=0).T
+            wt_ref[slot, pl.ds(spot, RAYS), CELL + c * LEV:CELL + (c + 1) * LEV] = jnp.concatenate(low_parts, axis=0).T
         return carry
 
     lax.fori_loop(0, SPAN * ORB, slot_body, 0)
@@ -155,14 +160,12 @@
     return jnp.concatenate(split(rows), axis=0)
 
 
-def back_all(sums, lats, w_ref):
+def back_all(sums, lats, wt_ref):
     total = None
     for slot in range(SPAN):
-        part = lax.dot_general(
-            w_ref[slot], masked_rows(sums[slot], lats[slot]), (((1,), (1,)), ((), ())), preferred_element_type=F32
-        )
+        part = jnp.dot(masked_rows(sums[slot], lats[slot]), wt_ref[slot], preferred_element_type=F32)
         total = part if total is None else total + part
-    total = (total[:CELL] + total[CELL:]).T
+    total = total[:, :CELL] + total[:, CELL:]
     return total[:64] + total[64:]
 
 
@@ -404,13 +407,13 @@
     (z,) = call(gather_kernel, (shape(8, SLOT),), 1)(shards)
     z1, z3 = shift(z, "lon", -1), shift(z, "lon", 1)
     z0, z4 = shift(z, "lon", -2), shift(z, "lon", 2)
-    w, lat = call(build_kernel, (shape(SPAN, 2 * CELL, SLOT, dtype=BF16), shape(SPAN, 8, SLOT, dtype=jnp.int32)), 1, work=BUILD)(shards)
-    v, mask = call(init_kernel, (FIELD, shape(SPAN, 8, SLOT, dtype=jnp.int32)), 7, work=MATMUL)(z, z0, z1, z3, z4, lat, w)
+    w, wt, lat = call(build_kernel, (shape(SPAN, 2 * CELL, SLOT, dtype=BF16), shape(SPAN, SLOT, 2 * CELL, dtype=BF16), shape(SPAN, 8, SLOT, dtype=jnp.int32)), 1, work=BUILD)(shards)
+    v, mask = call(init_kernel, (FIELD, shape(SPAN, 8, SLOT, dtype=jnp.int32)), 7, work=MATMUL)(z, z0, z1, z3, z4, lat, wt)
     vectors = [v]
     sent = call(project_first_kernel, SENT, 3, True, work=MATMUL)(side, v, mask, w)
     for turn in range(ITERS):
         *sums, first, second = exchange(*sent)
-        (part,) = call(step_kernel, (FIELD,), 10, work=MATMUL)(v, *sums, mask, w, gram, prior)
+        (part,) = call(step_kernel, (FIELD,), 10, work=MATMUL)(v, *sums, mask, wt, gram, prior)
         if turn < ITERS - 1:
             v, *sent = call(project_kernel, (FIELD,) + SENT, 6, True, work=MATMUL)(side, part, first, second, prior, mask, w)
             vectors.append(v)

time: 151 us -> 146 us (0.967)
  Pallas kernels: 32.7 us -> 27.6 us
    pallas_call x4, Pallas kernels: 13.2 us -> 7.19 us  [body(): call(step_kernel, (FIELD,), 10, work=MATMUL)]
    pallas_call x1, Pallas kernels: 7.54 us -> 9.84 us  [body(): call(build_kernel, (shape(SPAN, 2 * CELL, SLOT, dtype=BF16), shape(SPAN,...]
  transfers between devices with their start and end apart: 28 -> 28, of which waited for: 2 -> 1; matrix products, arithmetic and copies ran while one was open for 0% -> 0% of each run, Pallas kernels for 14% -> 12%
where the time goes in v7:
time: 146 us; the launch traced here: 145 us
  starting transfers between devices  67.5 us (46%)
  blocking collectives  46.9 us (32%)
  Pallas kernels  27.6 us (19%)
  waiting for transfers between devices  1.93 us (1%)
    ppermute x20, starting transfers between devices, shift(): lax.ppermute(block, axis, [(i, (i + distance) % size) for i in range(size)])  48.3 us
    all_gather x1, blocking collectives, body(): shards = lax.all_gather(table, 'orbit')  27.5 us
    all_to_all x1, blocking collectives, body(): pairs = lax.all_to_all(pairs, ('lon', 'lat'), 0, 0, tiled=True)  19.4 us
    ppermute x4, starting transfers between devices, exchange(): first = lax.ppermute(first, 'lat', pairs_from(0, n_lat))  16.4 us
    pallas_call x1, Pallas kernels, body(): call(build_kernel, (shape(SPAN, 2 * CELL, SLOT, dtype=BF16), shape(SPAN,...  9.84 us
    pallas_call x4, Pallas kernels, body(): call(step_kernel, (FIELD,), 10, work=MATMUL)  7.19 us
    pallas_call x3, Pallas kernels, body(): call(project_kernel, (FIELD,) + SENT, 6, True, work=MATMUL)  4.65 us
  transfers between devices with their start and end apart: 28, of which 1 were waited for; matrix products, arithmetic and copies ran while one was open for 0% of the time, Pallas kernels for 12%

profile of v7, /device:TPU:1, one launch (start us, length us, event | category | flops | bytes accessed | tf_op | source)
XLA Modules:
  0.0 145.1 jit_solution(13019759062985385174)
XLA Ops:
  1.9 27.5 %all-gather = f32[1344,128]{1,0:T(8,128)S(1)} all-gather(f32[168,128]{1,0:T(8,128)S(1)} %get-tuple-element.53), channel_id=2, replica_groups=mesh['orbit'=8,'lon'=16,'lat'=4] {'orbit'}, dimensions={0}, use_global_device_ids=true | all-gather | bytes 774144 | tf_op jit(solution)/shard_map/all_gather | solution.py:406
  29.3 3.2 %collective-permute-start.3 = (f32[8,1024]{1,0:T(8,128)S(1)}, f32[8,1024]{1,0:T(8,128)S(1)}, u32[]{:S(2)}, u32[]{:S(2)}) collective-permute-start(f32[8,1024]{1,0:T(8,128)S(1)} %shard_map.87.z2), channel_id=1, source_target_pairs={{0,8},{4,12},{8,16},{12,20},{16,24},{20,28},{24,32},{28,36},{32,40... | collective-permute-start | bytes 98312 | tf_op jit(solution)/shard_map/ppermute | solution.py:39
  32.5 7.7 %collective-permute-start.2 = (f32[8,1024]{1,0:T(8,128)S(1)}, f32[8,1024]{1,0:T(8,128)S(1)}, u32[]{:S(2)}, u32[]{:S(2)}) collective-permute-start(f32[8,1024]{1,0:T(8,128)S(1)} %shard_map.87.z2), channel_id=1, source_target_pairs={{0,4},{4,8},{8,12},{12,16},{16,20},{20,24},{24,28},{28,32},{32,36}... | collective-permute-start | bytes 98312 | tf_op jit(solution)/shard_map/ppermute | solution.py:39
  40.2 3.3 %collective-permute-start = (f32[8,1024]{1,0:T(8,128)S(1)}, f32[8,1024]{1,0:T(8,128)S(1)}, u32[]{:S(2)}, u32[]{:S(2)}) collective-permute-start(f32[8,1024]{1,0:T(8,128)S(1)} %shard_map.87.z2), channel_id=1, source_target_pairs={{0,56},{4,60},{8,0},{12,4},{16,8},{20,12},{24,16},{28,20},{32,24},... | collective-permute-start | bytes 98312 | tf_op jit(solution)/shard_map/ppermute | solution.py:39
  43.5 9.8 %shard_map.88 = (bf16[5,1024,1024]{2,1,0:T(8,128)(2,1)S(1)}, bf16[5,1024,1024]{2,1,0:T(8,128)(2,1)S(1)}, s32[5,8,1024]{2,1,0:T(8,128)S(1)}) custom-call(f32[8,168,128]{2,1,0:T(8,128)S(1)} %bitcast.12), custom_call_target="tpu_custom_call" | custom-call | flops 671088640 | bytes 20971520 | tf_op jit(solution)/shard_map/pallas_call | solution.py:410
  58.6 3.6 %collective-permute-start.6 = (f32[3,8,1024]{2,1,0:T(8,128)S(1)}, f32[3,8,1024]{2,1,0:T(8,128)S(1)}, u32[]{:S(2)}, u32[]{:S(2)}) collective-permute-start(f32[3,8,1024]{2,1,0:T(8,128)S(1)} %get-tuple-element.64), channel_id=1, source_target_pairs={{0,56},{4,60},{8,0},{12,4},{16,8},{20,12},{24,16},{28,20},{32,24},... | collective-permute-start | bytes 294920 | tf_op jit(solution)/shard_map/ppermute | solution.py:39
  62.2 1.9 %collective-permute-start.7 = (f32[3,8,1024]{2,1,0:T(8,128)S(1)}, f32[3,8,1024]{2,1,0:T(8,128)S(1)}, u32[]{:S(2)}, u32[]{:S(2)}) collective-permute-start(f32[3,8,1024]{2,1,0:T(8,128)S(1)} %get-tuple-element.65), channel_id=1, source_target_pairs={{0,8},{4,12},{8,16},{12,20},{16,24},{20,28},{24,32},{28,36},{32,40... | collective-permute-start | bytes 294920 | tf_op jit(solution)/shard_map/ppermute | solution.py:39
  64.1 3.1 %collective-permute-start.8 = (f32[8,512]{1,0:T(8,128)S(1)}, f32[8,512]{1,0:T(8,128)S(1)}, u32[]{:S(2)}, u32[]{:S(2)}) collective-permute-start(f32[8,512]{1,0:T(8,128)S(1)} %get-tuple-element.68), channel_id=1, source_target_pairs={{0,1},{2,3},{1,0},{3,2},{4,5},{6,7},{5,4},{7,6},{8,9},{10,11},{9,8... | collective-permute-start | bytes 49160 | tf_op jit(solution)/shard_map/ppermute | solution.py:373
  68.0 1.9 %collective-permute-done.7.minus2 = f32[3,8,1024]{2,1,0:T(8,128)S(1)} collective-permute-done((f32[3,8,1024]{2,1,0:T(8,128)S(1)}, f32[3,8,1024]{2,1,0:T(8,128)S(1)}, u32[]{:S(2)}, u32[]{:S(2)}) %collective-permute-start.7) | collective-permute-done | bytes 98336 | tf_op jit(solution)/shard_map/ppermute | solution.py:39
  69.8 1.8 %shard_map.91.part_ref = f32[64,512]{1,0:T(8,128)S(1)} custom-call(f32[64,512]{1,0:T(8,128)S(1)} %get-tuple-element.56.v_ref.refs_0_.refs_1_, f32[5,8,1024]{2,1,0:T(8,128)S(1)} %get-tuple-element.59.own_ref, f32[5,8,1024]{2,1,0:T(8,128)S(1)} %collective-permute-done.4.plus1, f32[5,8,1024]{2,1,0:T(8,128)S(1)} %collective-permute-done.5.minus1, ...), custom_call_target="tpu_custom_call" | custom-call | flops 1342177280 | bytes 10485760 | tf_op jit(solution)/shard_map/pallas_call | solution.py:416
  75.0 3.9 %collective-permute-start.12 = (f32[3,8,1024]{2,1,0:T(8,128)S(1)}, f32[3,8,1024]{2,1,0:T(8,128)S(1)}, u32[]{:S(2)}, u32[]{:S(2)}) collective-permute-start(f32[3,8,1024]{2,1,0:T(8,128)S(1)} %get-tuple-element.76), channel_id=1, source_target_pairs={{0,56},{4,60},{8,0},{12,4},{16,8},{20,12},{24,16},{28,20},{32,24},... | collective-permute-start | bytes 294920 | tf_op jit(solution)/shard_map/ppermute | solution.py:39
  78.9 1.9 %collective-permute-start.13 = (f32[3,8,1024]{2,1,0:T(8,128)S(1)}, f32[3,8,1024]{2,1,0:T(8,128)S(1)}, u32[]{:S(2)}, u32[]{:S(2)}) collective-permute-start(f32[3,8,1024]{2,1,0:T(8,128)S(1)} %get-tuple-element.77), channel_id=1, source_target_pairs={{0,8},{4,12},{8,16},{12,20},{16,24},{20,28},{24,32},{28,36},{32,40... | collective-permute-start | bytes 294920 | tf_op jit(solution)/shard_map/ppermute | solution.py:39
  80.8 5.3 %collective-permute-start.14 = (f32[8,512]{1,0:T(8,128)S(1)}, f32[8,512]{1,0:T(8,128)S(1)}, u32[]{:S(2)}, u32[]{:S(2)}) collective-permute-start(f32[8,512]{1,0:T(8,128)S(1)} %get-tuple-element.78), channel_id=1, source_target_pairs={{0,1},{2,3},{1,0},{3,2},{4,5},{6,7},{5,4},{7,6},{8,9},{10,11},{9,8... | collective-permute-start | bytes 49160 | tf_op jit(solution)/shard_map/ppermute | solution.py:373
  86.8 1.8 %shard_map.93.part_ref = f32[64,512]{1,0:T(8,128)S(1)} custom-call(f32[64,512]{1,0:T(8,128)S(1)} %get-tuple-element.70.v_ref.refs_1_.refs_2_, f32[5,8,1024]{2,1,0:T(8,128)S(1)} %get-tuple-element.71.own_ref, f32[5,8,1024]{2,1,0:T(8,128)S(1)} %collective-permute-done.10.plus1, f32[5,8,1024]{2,1,0:T(8,128)S(1)} %collective-permute-done.11.minus1, ...), custom_call_target="tpu_custom_call" | custom-call | flops 1342177280 | bytes 10485760 | tf_op jit(solution)/shard_map/pallas_call | solution.py:416
  92.0 5.8 %collective-permute-start.18 = (f32[3,8,1024]{2,1,0:T(8,128)S(1)}, f32[3,8,1024]{2,1,0:T(8,128)S(1)}, u32[]{:S(2)}, u32[]{:S(2)}) collective-permute-start(f32[3,8,1024]{2,1,0:T(8,128)S(1)} %get-tuple-element.86), channel_id=1, source_target_pairs={{0,56},{4,60},{8,0},{12,4},{16,8},{20,12},{24,16},{28,20},{32,24},... | collective-permute-start | bytes 294920 | tf_op jit(solution)/shard_map/ppermute | solution.py:39
  97.8 1.9 %collective-permute-start.19 = (f32[3,8,1024]{2,1,0:T(8,128)S(1)}, f32[3,8,1024]{2,1,0:T(8,128)S(1)}, u32[]{:S(2)}, u32[]{:S(2)}) collective-permute-start(f32[3,8,1024]{2,1,0:T(8,128)S(1)} %get-tuple-element.87), channel_id=1, source_target_pairs={{0,8},{4,12},{8,16},{12,20},{16,24},{20,28},{24,32},{28,36},{32,40... | collective-permute-start | bytes 294920 | tf_op jit(solution)/shard_map/ppermute | solution.py:39
  99.7 3.9 %collective-permute-start.20 = (f32[8,512]{1,0:T(8,128)S(1)}, f32[8,512]{1,0:T(8,128)S(1)}, u32[]{:S(2)}, u32[]{:S(2)}) collective-permute-start(f32[8,512]{1,0:T(8,128)S(1)} %get-tuple-element.88), channel_id=1, source_target_pairs={{0,1},{2,3},{1,0},{3,2},{4,5},{6,7},{5,4},{7,6},{8,9},{10,11},{9,8... | collective-permute-start | bytes 49160 | tf_op jit(solution)/shard_map/ppermute | solution.py:373
  104.5 1.8 %shard_map.95.part_ref = f32[64,512]{1,0:T(8,128)S(1)} custom-call(f32[64,512]{1,0:T(8,128)S(1)} %get-tuple-element.80.v_ref.refs_2_.refs_3_, f32[5,8,1024]{2,1,0:T(8,128)S(1)} %get-tuple-element.81.own_ref, f32[5,8,1024]{2,1,0:T(8,128)S(1)} %collective-permute-done.16.plus1, f32[5,8,1024]{2,1,0:T(8,128)S(1)} %collective-permute-done.17.minus1, ...), custom_call_target="tpu_custom_call" | custom-call | flops 1342177280 | bytes 10485760 | tf_op jit(solution)/shard_map/pallas_call | solution.py:416
  107.9 1.7 %collective-permute-start.23 = (f32[5,8,1024]{2,1,0:T(8,128)S(1)}, f32[5,8,1024]{2,1,0:T(8,128)S(1)}, u32[]{:S(2)}, u32[]{:S(2)}) collective-permute-start(f32[5,8,1024]{2,1,0:T(8,128)S(1)} %get-tuple-element.95), channel_id=1, source_target_pairs={{0,4},{4,8},{8,12},{12,16},{16,20},{20,24},{24,28},{28,32},{32,36}... | collective-permute-start | bytes 491528 | tf_op jit(solution)/shard_map/ppermute | solution.py:39
  109.6 5.8 %collective-permute-start.24 = (f32[3,8,1024]{2,1,0:T(8,128)S(1)}, f32[3,8,1024]{2,1,0:T(8,128)S(1)}, u32[]{:S(2)}, u32[]{:S(2)}) collective-permute-start(f32[3,8,1024]{2,1,0:T(8,128)S(1)} %get-tuple-element.96), channel_id=1, source_target_pairs={{0,56},{4,60},{8,0},{12,4},{16,8},{20,12},{24,16},{28,20},{32,24},... | collective-permute-start | bytes 294920 | tf_op jit(solution)/shard_map/ppermute | solution.py:39
  115.4 1.9 %collective-permute-start.25 = (f32[3,8,1024]{2,1,0:T(8,128)S(1)}, f32[3,8,1024]{2,1,0:T(8,128)S(1)}, u32[]{:S(2)}, u32[]{:S(2)}) collective-permute-start(f32[3,8,1024]{2,1,0:T(8,128)S(1)} %get-tuple-element.97), channel_id=1, source_target_pairs={{0,8},{4,12},{8,16},{12,20},{16,24},{20,28},{24,32},{28,36},{32,40... | collective-permute-start | bytes 294920 | tf_op jit(solution)/shard_map/ppermute | solution.py:39
  117.3 4.2 %collective-permute-start.26 = (f32[8,512]{1,0:T(8,128)S(1)}, f32[8,512]{1,0:T(8,128)S(1)}, u32[]{:S(2)}, u32[]{:S(2)}) collective-permute-start(f32[8,512]{1,0:T(8,128)S(1)} %get-tuple-element.98), channel_id=1, source_target_pairs={{0,1},{2,3},{1,0},{3,2},{4,5},{6,7},{5,4},{7,6},{8,9},{10,11},{9,8... | collective-permute-start | bytes 49160 | tf_op jit(solution)/shard_map/ppermute | solution.py:373
  122.2 1.8 %shard_map.97.part_ref = f32[64,512]{1,0:T(8,128)S(1)} custom-call(f32[64,512]{1,0:T(8,128)S(1)} %get-tuple-element.90.v_ref.refs_3_.refs_4_, f32[5,8,1024]{2,1,0:T(8,128)S(1)} %get-tuple-element.91.own_ref, f32[5,8,1024]{2,1,0:T(8,128)S(1)} %collective-permute-done.22.plus1, f32[5,8,1024]{2,1,0:T(8,128)S(1)} %collective-permute-done.23.minus1, ...), custom_call_target="tpu_custom_call" | custom-call | flops 1342177280 | bytes 10485760 | tf_op jit(solution)/shard_map/pallas_call | solution.py:416
  124.3 19.4 %all_to_all.11 = f32[64,1,128]{2,1,0:T(1,128)S(1)} all-to-all(f32[64,1,128]{2,1,0:T(1,128)S(1)} %bitcast.14), channel_id=1, replica_groups=mesh['orbit'=8,'lon'=16,'lat'=4] {'lon','lat'}, dimensions={0} | all-to-all | bytes 65536 | tf_op jit(solution)/shard_map/all_to_all | solution.py:423
  (48 shorter events, 19.1 us)
Async XLA Ops:
  29.3 24.1 %collective-permute-start.3 = (f32[8,1024]{1,0:T(8,128)S(1)}, f32[8,1024]{1,0:T(8,128)S(1)}, u32[]{:S(2)}, u32[]{:S(2)}) collective-permute-start(f32[8,1024]{1,0:T(8,128)S(1)} %shard_map.87.z2), channel_id=1, source_target_pairs={{0,8},{4,12},{8,16},{12,20},{16,24},{20,28},{24,32},{28,36},{32,40... | collective-permute-start | bytes 98312 | tf_op jit(solution)/shard_map/ppermute | solution.py:39
  32.5 20.9 %collective-permute-start.2 = (f32[8,1024]{1,0:T(8,128)S(1)}, f32[8,1024]{1,0:T(8,128)S(1)}, u32[]{:S(2)}, u32[]{:S(2)}) collective-permute-start(f32[8,1024]{1,0:T(8,128)S(1)} %shard_map.87.z2), channel_id=1, source_target_pairs={{0,4},{4,8},{8,12},{12,16},{16,20},{20,24},{24,28},{28,32},{32,36}... | collective-permute-start | bytes 98312 | tf_op jit(solution)/shard_map/ppermute | solution.py:39
  40.2 13.2 %collective-permute-start.1 = (f32[8,1024]{1,0:T(8,128)S(1)}, f32[8,1024]{1,0:T(8,128)S(1)}, u32[]{:S(2)}, u32[]{:S(2)}) collective-permute-start(f32[8,1024]{1,0:T(8,128)S(1)} %shard_map.87.z2), channel_id=1, source_target_pairs={{0,60},{4,0},{8,4},{12,8},{16,12},{20,16},{24,20},{28,24},{32,28},... | collective-permute-start | bytes 98312 | tf_op jit(solution)/shard_map/ppermute | solution.py:39
  40.2 13.2 %collective-permute-start = (f32[8,1024]{1,0:T(8,128)S(1)}, f32[8,1024]{1,0:T(8,128)S(1)}, u32[]{:S(2)}, u32[]{:S(2)}) collective-permute-start(f32[8,1024]{1,0:T(8,128)S(1)} %shard_map.87.z2), channel_id=1, source_target_pairs={{0,56},{4,60},{8,0},{12,4},{16,8},{20,12},{24,16},{28,20},{32,24},... | collective-permute-start | bytes 98312 | tf_op jit(solution)/shard_map/ppermute | solution.py:39
  56.5 10.8 %collective-permute-start.4 = (f32[5,8,1024]{2,1,0:T(8,128)S(1)}, f32[5,8,1024]{2,1,0:T(8,128)S(1)}, u32[]{:S(2)}, u32[]{:S(2)}) collective-permute-start(f32[5,8,1024]{2,1,0:T(8,128)S(1)} %get-tuple-element.60), channel_id=1, source_target_pairs={{0,60},{4,0},{8,4},{12,8},{16,12},{20,16},{24,20},{28,24},{32,28},... | collective-permute-start | bytes 491528 | tf_op jit(solution)/shard_map/ppermute | solution.py:39
  57.6 12.2 %collective-permute-start.5 = (f32[5,8,1024]{2,1,0:T(8,128)S(1)}, f32[5,8,1024]{2,1,0:T(8,128)S(1)}, u32[]{:S(2)}, u32[]{:S(2)}) collective-permute-start(f32[5,8,1024]{2,1,0:T(8,128)S(1)} %get-tuple-element.63), channel_id=1, source_target_pairs={{0,4},{4,8},{8,12},{12,16},{16,20},{20,24},{24,28},{28,32},{32,36}... | collective-permute-start | bytes 491528 | tf_op jit(solution)/shard_map/ppermute | solution.py:39
  58.6 9.4 %collective-permute-start.6 = (f32[3,8,1024]{2,1,0:T(8,128)S(1)}, f32[3,8,1024]{2,1,0:T(8,128)S(1)}, u32[]{:S(2)}, u32[]{:S(2)}) collective-permute-start(f32[3,8,1024]{2,1,0:T(8,128)S(1)} %get-tuple-element.64), channel_id=1, source_target_pairs={{0,56},{4,60},{8,0},{12,4},{16,8},{20,12},{24,16},{28,20},{32,24},... | collective-permute-start | bytes 294920 | tf_op jit(solution)/shard_map/ppermute | solution.py:39
  62.2 7.6 %collective-permute-start.7 = (f32[3,8,1024]{2,1,0:T(8,128)S(1)}, f32[3,8,1024]{2,1,0:T(8,128)S(1)}, u32[]{:S(2)}, u32[]{:S(2)}) collective-permute-start(f32[3,8,1024]{2,1,0:T(8,128)S(1)} %get-tuple-element.65), channel_id=1, source_target_pairs={{0,8},{4,12},{8,16},{12,20},{16,24},{20,28},{24,32},{28,36},{32,40... | collective-permute-start | bytes 294920 | tf_op jit(solution)/shard_map/ppermute | solution.py:39
  64.1 7.5 %collective-permute-start.8 = (f32[8,512]{1,0:T(8,128)S(1)}, f32[8,512]{1,0:T(8,128)S(1)}, u32[]{:S(2)}, u32[]{:S(2)}) collective-permute-start(f32[8,512]{1,0:T(8,128)S(1)} %get-tuple-element.68), channel_id=1, source_target_pairs={{0,1},{2,3},{1,0},{3,2},{4,5},{6,7},{5,4},{7,6},{8,9},{10,11},{9,8... | collective-permute-start | bytes 49160 | tf_op jit(solution)/shard_map/ppermute | solution.py:373
  73.2 12.9 %collective-permute-start.10 = (f32[5,8,1024]{2,1,0:T(8,128)S(1)}, f32[5,8,1024]{2,1,0:T(8,128)S(1)}, u32[]{:S(2)}, u32[]{:S(2)}) collective-permute-start(f32[5,8,1024]{2,1,0:T(8,128)S(1)} %get-tuple-element.72), channel_id=1, source_target_pairs={{0,60},{4,0},{8,4},{12,8},{16,12},{20,16},{24,20},{28,24},{32,28},... | collective-permute-start | bytes 491528 | tf_op jit(solution)/shard_map/ppermute | solution.py:39
  73.9 12.9 %collective-permute-start.11 = (f32[5,8,1024]{2,1,0:T(8,128)S(1)}, f32[5,8,1024]{2,1,0:T(8,128)S(1)}, u32[]{:S(2)}, u32[]{:S(2)}) collective-permute-start(f32[5,8,1024]{2,1,0:T(8,128)S(1)} %get-tuple-element.75), channel_id=1, source_target_pairs={{0,4},{4,8},{8,12},{12,16},{16,20},{20,24},{24,28},{28,32},{32,36}... | collective-permute-start | bytes 491528 | tf_op jit(solution)/shard_map/ppermute | solution.py:39
  75.0 11.8 %collective-permute-start.12 = (f32[3,8,1024]{2,1,0:T(8,128)S(1)}, f32[3,8,1024]{2,1,0:T(8,128)S(1)}, u32[]{:S(2)}, u32[]{:S(2)}) collective-permute-start(f32[3,8,1024]{2,1,0:T(8,128)S(1)} %get-tuple-element.76), channel_id=1, source_target_pairs={{0,56},{4,60},{8,0},{12,4},{16,8},{20,12},{24,16},{28,20},{32,24},... | collective-permute-start | bytes 294920 | tf_op jit(solution)/shard_map/ppermute | solution.py:39
  78.9 7.9 %collective-permute-start.13 = (f32[3,8,1024]{2,1,0:T(8,128)S(1)}, f32[3,8,1024]{2,1,0:T(8,128)S(1)}, u32[]{:S(2)}, u32[]{:S(2)}) collective-permute-start(f32[3,8,1024]{2,1,0:T(8,128)S(1)} %get-tuple-element.77), channel_id=1, source_target_pairs={{0,8},{4,12},{8,16},{12,20},{16,24},{20,28},{24,32},{28,36},{32,40... | collective-permute-start | bytes 294920 | tf_op jit(solution)/shard_map/ppermute | solution.py:39
  80.8 7.8 %collective-permute-start.14 = (f32[8,512]{1,0:T(8,128)S(1)}, f32[8,512]{1,0:T(8,128)S(1)}, u32[]{:S(2)}, u32[]{:S(2)}) collective-permute-start(f32[8,512]{1,0:T(8,128)S(1)} %get-tuple-element.78), channel_id=1, source_target_pairs={{0,1},{2,3},{1,0},{3,2},{4,5},{6,7},{5,4},{7,6},{8,9},{10,11},{9,8... | collective-permute-start | bytes 49160 | tf_op jit(solution)/shard_map/ppermute | solution.py:373
  90.2 13.3 %collective-permute-start.16 = (f32[5,8,1024]{2,1,0:T(8,128)S(1)}, f32[5,8,1024]{2,1,0:T(8,128)S(1)}, u32[]{:S(2)}, u32[]{:S(2)}) collective-permute-start(f32[5,8,1024]{2,1,0:T(8,128)S(1)} %get-tuple-element.82), channel_id=1, source_target_pairs={{0,60},{4,0},{8,4},{12,8},{16,12},{20,16},{24,20},{28,24},{32,28},... | collective-permute-start | bytes 491528 | tf_op jit(solution)/shard_map/ppermute | solution.py:39
  90.3 14.2 %collective-permute-start.17 = (f32[5,8,1024]{2,1,0:T(8,128)S(1)}, f32[5,8,1024]{2,1,0:T(8,128)S(1)}, u32[]{:S(2)}, u32[]{:S(2)}) collective-permute-start(f32[5,8,1024]{2,1,0:T(8,128)S(1)} %get-tuple-element.85), channel_id=1, source_target_pairs={{0,4},{4,8},{8,12},{12,16},{16,20},{20,24},{24,28},{28,32},{32,36}... | collective-permute-start | bytes 491528 | tf_op jit(solution)/shard_map/ppermute | solution.py:39
  92.0 12.4 %collective-permute-start.18 = (f32[3,8,1024]{2,1,0:T(8,128)S(1)}, f32[3,8,1024]{2,1,0:T(8,128)S(1)}, u32[]{:S(2)}, u32[]{:S(2)}) collective-permute-start(f32[3,8,1024]{2,1,0:T(8,128)S(1)} %get-tuple-element.86), channel_id=1, source_target_pairs={{0,56},{4,60},{8,0},{12,4},{16,8},{20,12},{24,16},{28,20},{32,24},... | collective-permute-start | bytes 294920 | tf_op jit(solution)/shard_map/ppermute | solution.py:39
  97.8 6.7 %collective-permute-start.19 = (f32[3,8,1024]{2,1,0:T(8,128)S(1)}, f32[3,8,1024]{2,1,0:T(8,128)S(1)}, u32[]{:S(2)}, u32[]{:S(2)}) collective-permute-start(f32[3,8,1024]{2,1,0:T(8,128)S(1)} %get-tuple-element.87), channel_id=1, source_target_pairs={{0,8},{4,12},{8,16},{12,20},{16,24},{20,28},{24,32},{28,36},{32,40... | collective-permute-start | bytes 294920 | tf_op jit(solution)/shard_map/ppermute | solution.py:39
  99.7 6.6 %collective-permute-start.20 = (f32[8,512]{1,0:T(8,128)S(1)}, f32[8,512]{1,0:T(8,128)S(1)}, u32[]{:S(2)}, u32[]{:S(2)}) collective-permute-start(f32[8,512]{1,0:T(8,128)S(1)} %get-tuple-element.88), channel_id=1, source_target_pairs={{0,1},{2,3},{1,0},{3,2},{4,5},{6,7},{5,4},{7,6},{8,9},{10,11},{9,8... | collective-permute-start | bytes 49160 | tf_op jit(solution)/shard_map/ppermute | solution.py:373
  107.8 13.6 %collective-permute-start.22 = (f32[5,8,1024]{2,1,0:T(8,128)S(1)}, f32[5,8,1024]{2,1,0:T(8,128)S(1)}, u32[]{:S(2)}, u32[]{:S(2)}) collective-permute-start(f32[5,8,1024]{2,1,0:T(8,128)S(1)} %get-tuple-element.92), channel_id=1, source_target_pairs={{0,60},{4,0},{8,4},{12,8},{16,12},{20,16},{24,20},{28,24},{32,28},... | collective-permute-start | bytes 491528 | tf_op jit(solution)/shard_map/ppermute | solution.py:39
  107.9 14.3 %collective-permute-start.23 = (f32[5,8,1024]{2,1,0:T(8,128)S(1)}, f32[5,8,1024]{2,1,0:T(8,128)S(1)}, u32[]{:S(2)}, u32[]{:S(2)}) collective-permute-start(f32[5,8,1024]{2,1,0:T(8,128)S(1)} %get-tuple-element.95), channel_id=1, source_target_pairs={{0,4},{4,8},{8,12},{12,16},{16,20},{20,24},{24,28},{28,32},{32,36}... | collective-permute-start | bytes 491528 | tf_op jit(solution)/shard_map/ppermute | solution.py:39
  109.6 12.6 %collective-permute-start.24 = (f32[3,8,1024]{2,1,0:T(8,128)S(1)}, f32[3,8,1024]{2,1,0:T(8,128)S(1)}, u32[]{:S(2)}, u32[]{:S(2)}) collective-permute-start(f32[3,8,1024]{2,1,0:T(8,128)S(1)} %get-tuple-element.96), channel_id=1, source_target_pairs={{0,56},{4,60},{8,0},{12,4},{16,8},{20,12},{24,16},{28,20},{32,24},... | collective-permute-start | bytes 294920 | tf_op jit(solution)/shard_map/ppermute | solution.py:39
  115.4 6.8 %collective-permute-start.25 = (f32[3,8,1024]{2,1,0:T(8,128)S(1)}, f32[3,8,1024]{2,1,0:T(8,128)S(1)}, u32[]{:S(2)}, u32[]{:S(2)}) collective-permute-start(f32[3,8,1024]{2,1,0:T(8,128)S(1)} %get-tuple-element.97), channel_id=1, source_target_pairs={{0,8},{4,12},{8,16},{12,20},{16,24},{20,28},{24,32},{28,36},{32,40... | collective-permute-start | bytes 294920 | tf_op jit(solution)/shard_map/ppermute | solution.py:39
  117.3 6.7 %collective-permute-start.26 = (f32[8,512]{1,0:T(8,128)S(1)}, f32[8,512]{1,0:T(8,128)S(1)}, u32[]{:S(2)}, u32[]{:S(2)}) collective-permute-start(f32[8,512]{1,0:T(8,128)S(1)} %get-tuple-element.98), channel_id=1, source_target_pairs={{0,1},{2,3},{1,0},{3,2},{4,5},{6,7},{5,4},{7,6},{8,9},{10,11},{9,8... | collective-permute-start | bytes 49160 | tf_op jit(solution)/shard_map/ppermute | solution.py:373
  (4 other events, 12.1 us)

commit v8 on v7

--- a/solution.py
+++ b/solution.py
@@ -152,7 +152,7 @@
             wt_ref[slot, pl.ds(spot, RAYS), CELL + c * LEV:CELL + (c + 1) * LEV] = jnp.concatenate(low_parts, axis=0).T
         return carry
 
-    lax.fori_loop(0, SPAN * ORB, slot_body, 0)
+    lax.fori_loop(0, SPAN * ORB, slot_body, 0, unroll=2)
 
 
 def masked_rows(values, lat):

time: 146 us -> 145 us (level)
  transfers between devices with their start and end apart: 28 -> 28, of which waited for: 1 -> 1; matrix products, arithmetic and copies ran while one was open for 0% -> 0% of each run, Pallas kernels for 12% -> 11%
where the time goes in v8:
time: 145 us; the launch traced here: 144 us
  starting transfers between devices  67.6 us (47%)
  blocking collectives  46.8 us (32%)
  Pallas kernels  26.6 us (18%)
  waiting for transfers between devices  1.96 us (1%)
    ppermute x20, starting transfers between devices, shift(): lax.ppermute(block, axis, [(i, (i + distance) % size) for i in range(size)])  48.2 us
    all_gather x1, blocking collectives, body(): shards = lax.all_gather(table, 'orbit')  27.5 us
    all_to_all x1, blocking collectives, body(): pairs = lax.all_to_all(pairs, ('lon', 'lat'), 0, 0, tiled=True)  19.3 us
    ppermute x4, starting transfers between devices, exchange(): first = lax.ppermute(first, 'lat', pairs_from(0, n_lat))  16.6 us
    pallas_call x1, Pallas kernels, body(): call(build_kernel, (shape(SPAN, 2 * CELL, SLOT, dtype=BF16), shape(SPAN,...  8.85 us
    pallas_call x4, Pallas kernels, body(): call(step_kernel, (FIELD,), 10, work=MATMUL)  7.2 us
    pallas_call x3, Pallas kernels, body(): call(project_kernel, (FIELD,) + SENT, 6, True, work=MATMUL)  4.64 us
  transfers between devices with their start and end apart: 28, of which 1 were waited for; matrix products, arithmetic and copies ran while one was open for 0% of the time, Pallas kernels for 11%

profile of v8, /device:TPU:1, one launch (start us, length us, event | category | flops | bytes accessed | tf_op | source)
XLA Modules:
  0.0 144.1 jit_solution(9820218543951637445)
XLA Ops:
  1.9 27.5 %all-gather = f32[1344,128]{1,0:T(8,128)S(1)} all-gather(f32[168,128]{1,0:T(8,128)S(1)} %get-tuple-element.53), channel_id=2, replica_groups=mesh['orbit'=8,'lon'=16,'lat'=4] {'orbit'}, dimensions={0}, use_global_device_ids=true | all-gather | bytes 774144 | tf_op jit(solution)/shard_map/all_gather | solution.py:406
  29.3 3.2 %collective-permute-start.3 = (f32[8,1024]{1,0:T(8,128)S(1)}, f32[8,1024]{1,0:T(8,128)S(1)}, u32[]{:S(2)}, u32[]{:S(2)}) collective-permute-start(f32[8,1024]{1,0:T(8,128)S(1)} %shard_map.87.z2), channel_id=1, source_target_pairs={{0,8},{4,12},{8,16},{12,20},{16,24},{20,28},{24,32},{28,36},{32,40... | collective-permute-start | bytes 98312 | tf_op jit(solution)/shard_map/ppermute | solution.py:39
  32.5 7.7 %collective-permute-start.2 = (f32[8,1024]{1,0:T(8,128)S(1)}, f32[8,1024]{1,0:T(8,128)S(1)}, u32[]{:S(2)}, u32[]{:S(2)}) collective-permute-start(f32[8,1024]{1,0:T(8,128)S(1)} %shard_map.87.z2), channel_id=1, source_target_pairs={{0,4},{4,8},{8,12},{12,16},{16,20},{20,24},{24,28},{28,32},{32,36}... | collective-permute-start | bytes 98312 | tf_op jit(solution)/shard_map/ppermute | solution.py:39
  40.2 3.3 %collective-permute-start = (f32[8,1024]{1,0:T(8,128)S(1)}, f32[8,1024]{1,0:T(8,128)S(1)}, u32[]{:S(2)}, u32[]{:S(2)}) collective-permute-start(f32[8,1024]{1,0:T(8,128)S(1)} %shard_map.87.z2), channel_id=1, source_target_pairs={{0,56},{4,60},{8,0},{12,4},{16,8},{20,12},{24,16},{28,20},{32,24},... | collective-permute-start | bytes 98312 | tf_op jit(solution)/shard_map/ppermute | solution.py:39
  43.5 8.8 %shard_map.88 = (bf16[5,1024,1024]{2,1,0:T(8,128)(2,1)S(1)}, bf16[5,1024,1024]{2,1,0:T(8,128)(2,1)S(1)}, s32[5,8,1024]{2,1,0:T(8,128)S(1)}) custom-call(f32[8,168,128]{2,1,0:T(8,128)S(1)} %bitcast.12), custom_call_target="tpu_custom_call" | custom-call | flops 671088640 | bytes 20971520 | tf_op jit(solution)/shard_map/pallas_call | solution.py:410
  57.6 3.6 %collective-permute-start.6 = (f32[3,8,1024]{2,1,0:T(8,128)S(1)}, f32[3,8,1024]{2,1,0:T(8,128)S(1)}, u32[]{:S(2)}, u32[]{:S(2)}) collective-permute-start(f32[3,8,1024]{2,1,0:T(8,128)S(1)} %get-tuple-element.64), channel_id=1, source_target_pairs={{0,56},{4,60},{8,0},{12,4},{16,8},{20,12},{24,16},{28,20},{32,24},... | collective-permute-start | bytes 294920 | tf_op jit(solution)/shard_map/ppermute | solution.py:39
  61.2 1.9 %collective-permute-start.7 = (f32[3,8,1024]{2,1,0:T(8,128)S(1)}, f32[3,8,1024]{2,1,0:T(8,128)S(1)}, u32[]{:S(2)}, u32[]{:S(2)}) collective-permute-start(f32[3,8,1024]{2,1,0:T(8,128)S(1)} %get-tuple-element.65), channel_id=1, source_target_pairs={{0,8},{4,12},{8,16},{12,20},{16,24},{20,28},{24,32},{28,36},{32,40... | collective-permute-start | bytes 294920 | tf_op jit(solution)/shard_map/ppermute | solution.py:39
  63.1 3.1 %collective-permute-start.8 = (f32[8,512]{1,0:T(8,128)S(1)}, f32[8,512]{1,0:T(8,128)S(1)}, u32[]{:S(2)}, u32[]{:S(2)}) collective-permute-start(f32[8,512]{1,0:T(8,128)S(1)} %get-tuple-element.68), channel_id=1, source_target_pairs={{0,1},{2,3},{1,0},{3,2},{4,5},{6,7},{5,4},{7,6},{8,9},{10,11},{9,8... | collective-permute-start | bytes 49160 | tf_op jit(solution)/shard_map/ppermute | solution.py:373
  67.0 1.9 %collective-permute-done.7.minus2 = f32[3,8,1024]{2,1,0:T(8,128)S(1)} collective-permute-done((f32[3,8,1024]{2,1,0:T(8,128)S(1)}, f32[3,8,1024]{2,1,0:T(8,128)S(1)}, u32[]{:S(2)}, u32[]{:S(2)}) %collective-permute-start.7) | collective-permute-done | bytes 98336 | tf_op jit(solution)/shard_map/ppermute | solution.py:39
  68.9 1.8 %shard_map.91.part_ref = f32[64,512]{1,0:T(8,128)S(1)} custom-call(f32[64,512]{1,0:T(8,128)S(1)} %get-tuple-element.56.v_ref.refs_0_.refs_1_, f32[5,8,1024]{2,1,0:T(8,128)S(1)} %get-tuple-element.59.own_ref, f32[5,8,1024]{2,1,0:T(8,128)S(1)} %collective-permute-done.4.plus1, f32[5,8,1024]{2,1,0:T(8,128)S(1)} %collective-permute-done.5.minus1, ...), custom_call_target="tpu_custom_call" | custom-call | flops 1342177280 | bytes 10485760 | tf_op jit(solution)/shard_map/pallas_call | solution.py:416
  74.0 3.9 %collective-permute-start.12 = (f32[3,8,1024]{2,1,0:T(8,128)S(1)}, f32[3,8,1024]{2,1,0:T(8,128)S(1)}, u32[]{:S(2)}, u32[]{:S(2)}) collective-permute-start(f32[3,8,1024]{2,1,0:T(8,128)S(1)} %get-tuple-element.76), channel_id=1, source_target_pairs={{0,56},{4,60},{8,0},{12,4},{16,8},{20,12},{24,16},{28,20},{32,24},... | collective-permute-start | bytes 294920 | tf_op jit(solution)/shard_map/ppermute | solution.py:39
  77.9 1.9 %collective-permute-start.13 = (f32[3,8,1024]{2,1,0:T(8,128)S(1)}, f32[3,8,1024]{2,1,0:T(8,128)S(1)}, u32[]{:S(2)}, u32[]{:S(2)}) collective-permute-start(f32[3,8,1024]{2,1,0:T(8,128)S(1)} %get-tuple-element.77), channel_id=1, source_target_pairs={{0,8},{4,12},{8,16},{12,20},{16,24},{20,28},{24,32},{28,36},{32,40... | collective-permute-start | bytes 294920 | tf_op jit(solution)/shard_map/ppermute | solution.py:39
  79.8 5.3 %collective-permute-start.14 = (f32[8,512]{1,0:T(8,128)S(1)}, f32[8,512]{1,0:T(8,128)S(1)}, u32[]{:S(2)}, u32[]{:S(2)}) collective-permute-start(f32[8,512]{1,0:T(8,128)S(1)} %get-tuple-element.78), channel_id=1, source_target_pairs={{0,1},{2,3},{1,0},{3,2},{4,5},{6,7},{5,4},{7,6},{8,9},{10,11},{9,8... | collective-permute-start | bytes 49160 | tf_op jit(solution)/shard_map/ppermute | solution.py:373
  85.9 1.8 %shard_map.93.part_ref = f32[64,512]{1,0:T(8,128)S(1)} custom-call(f32[64,512]{1,0:T(8,128)S(1)} %get-tuple-element.70.v_ref.refs_1_.refs_2_, f32[5,8,1024]{2,1,0:T(8,128)S(1)} %get-tuple-element.71.own_ref, f32[5,8,1024]{2,1,0:T(8,128)S(1)} %collective-permute-done.10.plus1, f32[5,8,1024]{2,1,0:T(8,128)S(1)} %collective-permute-done.11.minus1, ...), custom_call_target="tpu_custom_call" | custom-call | flops 1342177280 | bytes 10485760 | tf_op jit(solution)/shard_map/pallas_call | solution.py:416
  89.3 1.7 %collective-permute-start.17 = (f32[5,8,1024]{2,1,0:T(8,128)S(1)}, f32[5,8,1024]{2,1,0:T(8,128)S(1)}, u32[]{:S(2)}, u32[]{:S(2)}) collective-permute-start(f32[5,8,1024]{2,1,0:T(8,128)S(1)} %get-tuple-element.85), channel_id=1, source_target_pairs={{0,4},{4,8},{8,12},{12,16},{16,20},{20,24},{24,28},{28,32},{32,36}... | collective-permute-start | bytes 491528 | tf_op jit(solution)/shard_map/ppermute | solution.py:39
  91.0 5.8 %collective-permute-start.18 = (f32[3,8,1024]{2,1,0:T(8,128)S(1)}, f32[3,8,1024]{2,1,0:T(8,128)S(1)}, u32[]{:S(2)}, u32[]{:S(2)}) collective-permute-start(f32[3,8,1024]{2,1,0:T(8,128)S(1)} %get-tuple-element.86), channel_id=1, source_target_pairs={{0,56},{4,60},{8,0},{12,4},{16,8},{20,12},{24,16},{28,20},{32,24},... | collective-permute-start | bytes 294920 | tf_op jit(solution)/shard_map/ppermute | solution.py:39
  96.8 1.9 %collective-permute-start.19 = (f32[3,8,1024]{2,1,0:T(8,128)S(1)}, f32[3,8,1024]{2,1,0:T(8,128)S(1)}, u32[]{:S(2)}, u32[]{:S(2)}) collective-permute-start(f32[3,8,1024]{2,1,0:T(8,128)S(1)} %get-tuple-element.87), channel_id=1, source_target_pairs={{0,8},{4,12},{8,16},{12,20},{16,24},{20,28},{24,32},{28,36},{32,40... | collective-permute-start | bytes 294920 | tf_op jit(solution)/shard_map/ppermute | solution.py:39
  98.7 3.9 %collective-permute-start.20 = (f32[8,512]{1,0:T(8,128)S(1)}, f32[8,512]{1,0:T(8,128)S(1)}, u32[]{:S(2)}, u32[]{:S(2)}) collective-permute-start(f32[8,512]{1,0:T(8,128)S(1)} %get-tuple-element.88), channel_id=1, source_target_pairs={{0,1},{2,3},{1,0},{3,2},{4,5},{6,7},{5,4},{7,6},{8,9},{10,11},{9,8... | collective-permute-start | bytes 49160 | tf_op jit(solution)/shard_map/ppermute | solution.py:373
  103.5 1.8 %shard_map.95.part_ref = f32[64,512]{1,0:T(8,128)S(1)} custom-call(f32[64,512]{1,0:T(8,128)S(1)} %get-tuple-element.80.v_ref.refs_2_.refs_3_, f32[5,8,1024]{2,1,0:T(8,128)S(1)} %get-tuple-element.81.own_ref, f32[5,8,1024]{2,1,0:T(8,128)S(1)} %collective-permute-done.16.plus1, f32[5,8,1024]{2,1,0:T(8,128)S(1)} %collective-permute-done.17.minus1, ...), custom_call_target="tpu_custom_call" | custom-call | flops 1342177280 | bytes 10485760 | tf_op jit(solution)/shard_map/pallas_call | solution.py:416
  108.6 5.8 %collective-permute-start.24 = (f32[3,8,1024]{2,1,0:T(8,128)S(1)}, f32[3,8,1024]{2,1,0:T(8,128)S(1)}, u32[]{:S(2)}, u32[]{:S(2)}) collective-permute-start(f32[3,8,1024]{2,1,0:T(8,128)S(1)} %get-tuple-element.96), channel_id=1, source_target_pairs={{0,56},{4,60},{8,0},{12,4},{16,8},{20,12},{24,16},{28,20},{32,24},... | collective-permute-start | bytes 294920 | tf_op jit(solution)/shard_map/ppermute | solution.py:39
  114.4 1.9 %collective-permute-start.25 = (f32[3,8,1024]{2,1,0:T(8,128)S(1)}, f32[3,8,1024]{2,1,0:T(8,128)S(1)}, u32[]{:S(2)}, u32[]{:S(2)}) collective-permute-start(f32[3,8,1024]{2,1,0:T(8,128)S(1)} %get-tuple-element.97), channel_id=1, source_target_pairs={{0,8},{4,12},{8,16},{12,20},{16,24},{20,28},{24,32},{28,36},{32,40... | collective-permute-start | bytes 294920 | tf_op jit(solution)/shard_map/ppermute | solution.py:39
  116.3 4.2 %collective-permute-start.26 = (f32[8,512]{1,0:T(8,128)S(1)}, f32[8,512]{1,0:T(8,128)S(1)}, u32[]{:S(2)}, u32[]{:S(2)}) collective-permute-start(f32[8,512]{1,0:T(8,128)S(1)} %get-tuple-element.98), channel_id=1, source_target_pairs={{0,1},{2,3},{1,0},{3,2},{4,5},{6,7},{5,4},{7,6},{8,9},{10,11},{9,8... | collective-permute-start | bytes 49160 | tf_op jit(solution)/shard_map/ppermute | solution.py:373
  121.3 1.8 %shard_map.97.part_ref = f32[64,512]{1,0:T(8,128)S(1)} custom-call(f32[64,512]{1,0:T(8,128)S(1)} %get-tuple-element.90.v_ref.refs_3_.refs_4_, f32[5,8,1024]{2,1,0:T(8,128)S(1)} %get-tuple-element.91.own_ref, f32[5,8,1024]{2,1,0:T(8,128)S(1)} %collective-permute-done.22.plus1, f32[5,8,1024]{2,1,0:T(8,128)S(1)} %collective-permute-done.23.minus1, ...), custom_call_target="tpu_custom_call" | custom-call | flops 1342177280 | bytes 10485760 | tf_op jit(solution)/shard_map/pallas_call | solution.py:416
  123.4 19.3 %all_to_all.11 = f32[64,1,128]{2,1,0:T(1,128)S(1)} all-to-all(f32[64,1,128]{2,1,0:T(1,128)S(1)} %bitcast.14), channel_id=1, replica_groups=mesh['orbit'=8,'lon'=16,'lat'=4] {'lon','lat'}, dimensions={0} | all-to-all | bytes 65536 | tf_op jit(solution)/shard_map/all_to_all | solution.py:423
  (48 shorter events, 19.1 us)
Async XLA Ops:
  29.3 23.1 %collective-permute-start.3 = (f32[8,1024]{1,0:T(8,128)S(1)}, f32[8,1024]{1,0:T(8,128)S(1)}, u32[]{:S(2)}, u32[]{:S(2)}) collective-permute-start(f32[8,1024]{1,0:T(8,128)S(1)} %shard_map.87.z2), channel_id=1, source_target_pairs={{0,8},{4,12},{8,16},{12,20},{16,24},{20,28},{24,32},{28,36},{32,40... | collective-permute-start | bytes 98312 | tf_op jit(solution)/shard_map/ppermute | solution.py:39
  32.5 19.9 %collective-permute-start.2 = (f32[8,1024]{1,0:T(8,128)S(1)}, f32[8,1024]{1,0:T(8,128)S(1)}, u32[]{:S(2)}, u32[]{:S(2)}) collective-permute-start(f32[8,1024]{1,0:T(8,128)S(1)} %shard_map.87.z2), channel_id=1, source_target_pairs={{0,4},{4,8},{8,12},{12,16},{16,20},{20,24},{24,28},{28,32},{32,36}... | collective-permute-start | bytes 98312 | tf_op jit(solution)/shard_map/ppermute | solution.py:39
  40.2 12.2 %collective-permute-start.1 = (f32[8,1024]{1,0:T(8,128)S(1)}, f32[8,1024]{1,0:T(8,128)S(1)}, u32[]{:S(2)}, u32[]{:S(2)}) collective-permute-start(f32[8,1024]{1,0:T(8,128)S(1)} %shard_map.87.z2), channel_id=1, source_target_pairs={{0,60},{4,0},{8,4},{12,8},{16,12},{20,16},{24,20},{28,24},{32,28},... | collective-permute-start | bytes 98312 | tf_op jit(solution)/shard_map/ppermute | solution.py:39
  40.2 12.2 %collective-permute-start = (f32[8,1024]{1,0:T(8,128)S(1)}, f32[8,1024]{1,0:T(8,128)S(1)}, u32[]{:S(2)}, u32[]{:S(2)}) collective-permute-start(f32[8,1024]{1,0:T(8,128)S(1)} %shard_map.87.z2), channel_id=1, source_target_pairs={{0,56},{4,60},{8,0},{12,4},{16,8},{20,12},{24,16},{28,20},{32,24},... | collective-permute-start | bytes 98312 | tf_op jit(solution)/shard_map/ppermute | solution.py:39
  55.5 10.8 %collective-permute-start.4 = (f32[5,8,1024]{2,1,0:T(8,128)S(1)}, f32[5,8,1024]{2,1,0:T(8,128)S(1)}, u32[]{:S(2)}, u32[]{:S(2)}) collective-permute-start(f32[5,8,1024]{2,1,0:T(8,128)S(1)} %get-tuple-element.60), channel_id=1, source_target_pairs={{0,60},{4,0},{8,4},{12,8},{16,12},{20,16},{24,20},{28,24},{32,28},... | collective-permute-start | bytes 491528 | tf_op jit(solution)/shard_map/ppermute | solution.py:39
  56.6 12.2 %collective-permute-start.5 = (f32[5,8,1024]{2,1,0:T(8,128)S(1)}, f32[5,8,1024]{2,1,0:T(8,128)S(1)}, u32[]{:S(2)}, u32[]{:S(2)}) collective-permute-start(f32[5,8,1024]{2,1,0:T(8,128)S(1)} %get-tuple-element.63), channel_id=1, source_target_pairs={{0,4},{4,8},{8,12},{12,16},{16,20},{20,24},{24,28},{28,32},{32,36}... | collective-permute-start | bytes 491528 | tf_op jit(solution)/shard_map/ppermute | solution.py:39
  57.6 9.4 %collective-permute-start.6 = (f32[3,8,1024]{2,1,0:T(8,128)S(1)}, f32[3,8,1024]{2,1,0:T(8,128)S(1)}, u32[]{:S(2)}, u32[]{:S(2)}) collective-permute-start(f32[3,8,1024]{2,1,0:T(8,128)S(1)} %get-tuple-element.64), channel_id=1, source_target_pairs={{0,56},{4,60},{8,0},{12,4},{16,8},{20,12},{24,16},{28,20},{32,24},... | collective-permute-start | bytes 294920 | tf_op jit(solution)/shard_map/ppermute | solution.py:39
  61.2 7.6 %collective-permute-start.7 = (f32[3,8,1024]{2,1,0:T(8,128)S(1)}, f32[3,8,1024]{2,1,0:T(8,128)S(1)}, u32[]{:S(2)}, u32[]{:S(2)}) collective-permute-start(f32[3,8,1024]{2,1,0:T(8,128)S(1)} %get-tuple-element.65), channel_id=1, source_target_pairs={{0,8},{4,12},{8,16},{12,20},{16,24},{20,28},{24,32},{28,36},{32,40... | collective-permute-start | bytes 294920 | tf_op jit(solution)/shard_map/ppermute | solution.py:39
  63.1 7.5 %collective-permute-start.8 = (f32[8,512]{1,0:T(8,128)S(1)}, f32[8,512]{1,0:T(8,128)S(1)}, u32[]{:S(2)}, u32[]{:S(2)}) collective-permute-start(f32[8,512]{1,0:T(8,128)S(1)} %get-tuple-element.68), channel_id=1, source_target_pairs={{0,1},{2,3},{1,0},{3,2},{4,5},{6,7},{5,4},{7,6},{8,9},{10,11},{9,8... | collective-permute-start | bytes 49160 | tf_op jit(solution)/shard_map/ppermute | solution.py:373
  72.2 12.9 %collective-permute-start.10 = (f32[5,8,1024]{2,1,0:T(8,128)S(1)}, f32[5,8,1024]{2,1,0:T(8,128)S(1)}, u32[]{:S(2)}, u32[]{:S(2)}) collective-permute-start(f32[5,8,1024]{2,1,0:T(8,128)S(1)} %get-tuple-element.72), channel_id=1, source_target_pairs={{0,60},{4,0},{8,4},{12,8},{16,12},{20,16},{24,20},{28,24},{32,28},... | collective-permute-start | bytes 491528 | tf_op jit(solution)/shard_map/ppermute | solution.py:39
  72.9 12.9 %collective-permute-start.11 = (f32[5,8,1024]{2,1,0:T(8,128)S(1)}, f32[5,8,1024]{2,1,0:T(8,128)S(1)}, u32[]{:S(2)}, u32[]{:S(2)}) collective-permute-start(f32[5,8,1024]{2,1,0:T(8,128)S(1)} %get-tuple-element.75), channel_id=1, source_target_pairs={{0,4},{4,8},{8,12},{12,16},{16,20},{20,24},{24,28},{28,32},{32,36}... | collective-permute-start | bytes 491528 | tf_op jit(solution)/shard_map/ppermute | solution.py:39
  74.0 11.8 %collective-permute-start.12 = (f32[3,8,1024]{2,1,0:T(8,128)S(1)}, f32[3,8,1024]{2,1,0:T(8,128)S(1)}, u32[]{:S(2)}, u32[]{:S(2)}) collective-permute-start(f32[3,8,1024]{2,1,0:T(8,128)S(1)} %get-tuple-element.76), channel_id=1, source_target_pairs={{0,56},{4,60},{8,0},{12,4},{16,8},{20,12},{24,16},{28,20},{32,24},... | collective-permute-start | bytes 294920 | tf_op jit(solution)/shard_map/ppermute | solution.py:39
  77.9 8.0 %collective-permute-start.13 = (f32[3,8,1024]{2,1,0:T(8,128)S(1)}, f32[3,8,1024]{2,1,0:T(8,128)S(1)}, u32[]{:S(2)}, u32[]{:S(2)}) collective-permute-start(f32[3,8,1024]{2,1,0:T(8,128)S(1)} %get-tuple-element.77), channel_id=1, source_target_pairs={{0,8},{4,12},{8,16},{12,20},{16,24},{20,28},{24,32},{28,36},{32,40... | collective-permute-start | bytes 294920 | tf_op jit(solution)/shard_map/ppermute | solution.py:39
  79.8 7.9 %collective-permute-start.14 = (f32[8,512]{1,0:T(8,128)S(1)}, f32[8,512]{1,0:T(8,128)S(1)}, u32[]{:S(2)}, u32[]{:S(2)}) collective-permute-start(f32[8,512]{1,0:T(8,128)S(1)} %get-tuple-element.78), channel_id=1, source_target_pairs={{0,1},{2,3},{1,0},{3,2},{4,5},{6,7},{5,4},{7,6},{8,9},{10,11},{9,8... | collective-permute-start | bytes 49160 | tf_op jit(solution)/shard_map/ppermute | solution.py:373
  89.3 13.3 %collective-permute-start.16 = (f32[5,8,1024]{2,1,0:T(8,128)S(1)}, f32[5,8,1024]{2,1,0:T(8,128)S(1)}, u32[]{:S(2)}, u32[]{:S(2)}) collective-permute-start(f32[5,8,1024]{2,1,0:T(8,128)S(1)} %get-tuple-element.82), channel_id=1, source_target_pairs={{0,60},{4,0},{8,4},{12,8},{16,12},{20,16},{24,20},{28,24},{32,28},... | collective-permute-start | bytes 491528 | tf_op jit(solution)/shard_map/ppermute | solution.py:39
  89.3 14.2 %collective-permute-start.17 = (f32[5,8,1024]{2,1,0:T(8,128)S(1)}, f32[5,8,1024]{2,1,0:T(8,128)S(1)}, u32[]{:S(2)}, u32[]{:S(2)}) collective-permute-start(f32[5,8,1024]{2,1,0:T(8,128)S(1)} %get-tuple-element.85), channel_id=1, source_target_pairs={{0,4},{4,8},{8,12},{12,16},{16,20},{20,24},{24,28},{28,32},{32,36}... | collective-permute-start | bytes 491528 | tf_op jit(solution)/shard_map/ppermute | solution.py:39
  91.0 12.4 %collective-permute-start.18 = (f32[3,8,1024]{2,1,0:T(8,128)S(1)}, f32[3,8,1024]{2,1,0:T(8,128)S(1)}, u32[]{:S(2)}, u32[]{:S(2)}) collective-permute-start(f32[3,8,1024]{2,1,0:T(8,128)S(1)} %get-tuple-element.86), channel_id=1, source_target_pairs={{0,56},{4,60},{8,0},{12,4},{16,8},{20,12},{24,16},{28,20},{32,24},... | collective-permute-start | bytes 294920 | tf_op jit(solution)/shard_map/ppermute | solution.py:39
  96.8 6.7 %collective-permute-start.19 = (f32[3,8,1024]{2,1,0:T(8,128)S(1)}, f32[3,8,1024]{2,1,0:T(8,128)S(1)}, u32[]{:S(2)}, u32[]{:S(2)}) collective-permute-start(f32[3,8,1024]{2,1,0:T(8,128)S(1)} %get-tuple-element.87), channel_id=1, source_target_pairs={{0,8},{4,12},{8,16},{12,20},{16,24},{20,28},{24,32},{28,36},{32,40... | collective-permute-start | bytes 294920 | tf_op jit(solution)/shard_map/ppermute | solution.py:39
  98.7 6.6 %collective-permute-start.20 = (f32[8,512]{1,0:T(8,128)S(1)}, f32[8,512]{1,0:T(8,128)S(1)}, u32[]{:S(2)}, u32[]{:S(2)}) collective-permute-start(f32[8,512]{1,0:T(8,128)S(1)} %get-tuple-element.88), channel_id=1, source_target_pairs={{0,1},{2,3},{1,0},{3,2},{4,5},{6,7},{5,4},{7,6},{8,9},{10,11},{9,8... | collective-permute-start | bytes 49160 | tf_op jit(solution)/shard_map/ppermute | solution.py:373
  106.9 13.7 %collective-permute-start.22 = (f32[5,8,1024]{2,1,0:T(8,128)S(1)}, f32[5,8,1024]{2,1,0:T(8,128)S(1)}, u32[]{:S(2)}, u32[]{:S(2)}) collective-permute-start(f32[5,8,1024]{2,1,0:T(8,128)S(1)} %get-tuple-element.92), channel_id=1, source_target_pairs={{0,60},{4,0},{8,4},{12,8},{16,12},{20,16},{24,20},{28,24},{32,28},... | collective-permute-start | bytes 491528 | tf_op jit(solution)/shard_map/ppermute | solution.py:39
  106.9 14.4 %collective-permute-start.23 = (f32[5,8,1024]{2,1,0:T(8,128)S(1)}, f32[5,8,1024]{2,1,0:T(8,128)S(1)}, u32[]{:S(2)}, u32[]{:S(2)}) collective-permute-start(f32[5,8,1024]{2,1,0:T(8,128)S(1)} %get-tuple-element.95), channel_id=1, source_target_pairs={{0,4},{4,8},{8,12},{12,16},{16,20},{20,24},{24,28},{28,32},{32,36}... | collective-permute-start | bytes 491528 | tf_op jit(solution)/shard_map/ppermute | solution.py:39
  108.6 12.6 %collective-permute-start.24 = (f32[3,8,1024]{2,1,0:T(8,128)S(1)}, f32[3,8,1024]{2,1,0:T(8,128)S(1)}, u32[]{:S(2)}, u32[]{:S(2)}) collective-permute-start(f32[3,8,1024]{2,1,0:T(8,128)S(1)} %get-tuple-element.96), channel_id=1, source_target_pairs={{0,56},{4,60},{8,0},{12,4},{16,8},{20,12},{24,16},{28,20},{32,24},... | collective-permute-start | bytes 294920 | tf_op jit(solution)/shard_map/ppermute | solution.py:39
  114.4 6.9 %collective-permute-start.25 = (f32[3,8,1024]{2,1,0:T(8,128)S(1)}, f32[3,8,1024]{2,1,0:T(8,128)S(1)}, u32[]{:S(2)}, u32[]{:S(2)}) collective-permute-start(f32[3,8,1024]{2,1,0:T(8,128)S(1)} %get-tuple-element.97), channel_id=1, source_target_pairs={{0,8},{4,12},{8,16},{12,20},{16,24},{20,28},{24,32},{28,36},{32,40... | collective-permute-start | bytes 294920 | tf_op jit(solution)/shard_map/ppermute | solution.py:39
  116.3 6.8 %collective-permute-start.26 = (f32[8,512]{1,0:T(8,128)S(1)}, f32[8,512]{1,0:T(8,128)S(1)}, u32[]{:S(2)}, u32[]{:S(2)}) collective-permute-start(f32[8,512]{1,0:T(8,128)S(1)} %get-tuple-element.98), channel_id=1, source_target_pairs={{0,1},{2,3},{1,0},{3,2},{4,5},{6,7},{5,4},{7,6},{8,9},{10,11},{9,8... | collective-permute-start | bytes 49160 | tf_op jit(solution)/shard_map/ppermute | solution.py:373
  (4 other events, 12.1 us)

commit v9 on v8

--- a/solution.py
+++ b/solution.py
@@ -152,7 +152,7 @@
             wt_ref[slot, pl.ds(spot, RAYS), CELL + c * LEV:CELL + (c + 1) * LEV] = jnp.concatenate(low_parts, axis=0).T
         return carry
 
-    lax.fori_loop(0, SPAN * ORB, slot_body, 0, unroll=2)
+    lax.fori_loop(0, SPAN * ORB, slot_body, 0, unroll=4)
 
 
 def masked_rows(values, lat):

time: 145 us -> 144 us (level)
  no operation moved by 1% of the time
where the time goes in v9:
time: 144 us
  starting transfers between devices  67.6 us (47%)
  blocking collectives  46.7 us (32%)
  Pallas kernels  26.2 us (18%)
  waiting for transfers between devices  1.93 us (1%)
    ppermute x20, starting transfers between devices, shift(): lax.ppermute(block, axis, [(i, (i + distance) % size) for i in range(size)])  48.3 us
    all_gather x1, blocking collectives, body(): shards = lax.all_gather(table, 'orbit')  27.5 us
    all_to_all x1, blocking collectives, body(): pairs = lax.all_to_all(pairs, ('lon', 'lat'), 0, 0, tiled=True)  19.3 us
    ppermute x4, starting transfers between devices, exchange(): first = lax.ppermute(first, 'lat', pairs_from(0, n_lat))  16.5 us
    pallas_call x1, Pallas kernels, body(): call(build_kernel, (shape(SPAN, 2 * CELL, SLOT, dtype=BF16), shape(SPAN,...  8.37 us
    pallas_call x4, Pallas kernels, body(): call(step_kernel, (FIELD,), 10, work=MATMUL)  7.2 us
    pallas_call x3, Pallas kernels, body(): call(project_kernel, (FIELD,) + SENT, 6, True, work=MATMUL)  4.64 us
  transfers between devices with their start and end apart: 28, of which 1 were waited for; matrix products, arithmetic and copies ran while one was open for 0% of the time, Pallas kernels for 11%

profile of v9, /device:TPU:1, one launch (start us, length us, event | category | flops | bytes accessed | tf_op | source)
XLA Modules:
  0.0 143.6 jit_solution(18375562462415710476)
XLA Ops:
  1.9 27.5 %all-gather = f32[1344,128]{1,0:T(8,128)S(1)} all-gather(f32[168,128]{1,0:T(8,128)S(1)} %get-tuple-element.53), channel_id=2, replica_groups=mesh['orbit'=8,'lon'=16,'lat'=4] {'orbit'}, dimensions={0}, use_global_device_ids=true | all-gather | bytes 774144 | tf_op jit(solution)/shard_map/all_gather | solution.py:406
  29.3 3.2 %collective-permute-start.3 = (f32[8,1024]{1,0:T(8,128)S(1)}, f32[8,1024]{1,0:T(8,128)S(1)}, u32[]{:S(2)}, u32[]{:S(2)}) collective-permute-start(f32[8,1024]{1,0:T(8,128)S(1)} %shard_map.87.z2), channel_id=1, source_target_pairs={{0,8},{4,12},{8,16},{12,20},{16,24},{20,28},{24,32},{28,36},{32,40... | collective-permute-start | bytes 98312 | tf_op jit(solution)/shard_map/ppermute | solution.py:39
  32.5 7.7 %collective-permute-start.2 = (f32[8,1024]{1,0:T(8,128)S(1)}, f32[8,1024]{1,0:T(8,128)S(1)}, u32[]{:S(2)}, u32[]{:S(2)}) collective-permute-start(f32[8,1024]{1,0:T(8,128)S(1)} %shard_map.87.z2), channel_id=1, source_target_pairs={{0,4},{4,8},{8,12},{12,16},{16,20},{20,24},{24,28},{28,32},{32,36}... | collective-permute-start | bytes 98312 | tf_op jit(solution)/shard_map/ppermute | solution.py:39
  40.2 3.3 %collective-permute-start = (f32[8,1024]{1,0:T(8,128)S(1)}, f32[8,1024]{1,0:T(8,128)S(1)}, u32[]{:S(2)}, u32[]{:S(2)}) collective-permute-start(f32[8,1024]{1,0:T(8,128)S(1)} %shard_map.87.z2), channel_id=1, source_target_pairs={{0,56},{4,60},{8,0},{12,4},{16,8},{20,12},{24,16},{28,20},{32,24},... | collective-permute-start | bytes 98312 | tf_op jit(solution)/shard_map/ppermute | solution.py:39
  43.5 8.4 %shard_map.88 = (bf16[5,1024,1024]{2,1,0:T(8,128)(2,1)S(1)}, bf16[5,1024,1024]{2,1,0:T(8,128)(2,1)S(1)}, s32[5,8,1024]{2,1,0:T(8,128)S(1)}) custom-call(f32[8,168,128]{2,1,0:T(8,128)S(1)} %bitcast.12), custom_call_target="tpu_custom_call" | custom-call | flops 671088640 | bytes 20971520 | tf_op jit(solution)/shard_map/pallas_call | solution.py:410
  57.1 3.6 %collective-permute-start.6 = (f32[3,8,1024]{2,1,0:T(8,128)S(1)}, f32[3,8,1024]{2,1,0:T(8,128)S(1)}, u32[]{:S(2)}, u32[]{:S(2)}) collective-permute-start(f32[3,8,1024]{2,1,0:T(8,128)S(1)} %get-tuple-element.64), channel_id=1, source_target_pairs={{0,56},{4,60},{8,0},{12,4},{16,8},{20,12},{24,16},{28,20},{32,24},... | collective-permute-start | bytes 294920 | tf_op jit(solution)/shard_map/ppermute | solution.py:39
  60.7 1.9 %collective-permute-start.7 = (f32[3,8,1024]{2,1,0:T(8,128)S(1)}, f32[3,8,1024]{2,1,0:T(8,128)S(1)}, u32[]{:S(2)}, u32[]{:S(2)}) collective-permute-start(f32[3,8,1024]{2,1,0:T(8,128)S(1)} %get-tuple-element.65), channel_id=1, source_target_pairs={{0,8},{4,12},{8,16},{12,20},{16,24},{20,28},{24,32},{28,36},{32,40... | collective-permute-start | bytes 294920 | tf_op jit(solution)/shard_map/ppermute | solution.py:39
  62.7 3.1 %collective-permute-start.8 = (f32[8,512]{1,0:T(8,128)S(1)}, f32[8,512]{1,0:T(8,128)S(1)}, u32[]{:S(2)}, u32[]{:S(2)}) collective-permute-start(f32[8,512]{1,0:T(8,128)S(1)} %get-tuple-element.68), channel_id=1, source_target_pairs={{0,1},{2,3},{1,0},{3,2},{4,5},{6,7},{5,4},{7,6},{8,9},{10,11},{9,8... | collective-permute-start | bytes 49160 | tf_op jit(solution)/shard_map/ppermute | solution.py:373
  66.5 1.9 %collective-permute-done.7.minus2 = f32[3,8,1024]{2,1,0:T(8,128)S(1)} collective-permute-done((f32[3,8,1024]{2,1,0:T(8,128)S(1)}, f32[3,8,1024]{2,1,0:T(8,128)S(1)}, u32[]{:S(2)}, u32[]{:S(2)}) %collective-permute-start.7) | collective-permute-done | bytes 98336 | tf_op jit(solution)/shard_map/ppermute | solution.py:39
  68.4 1.8 %shard_map.91.part_ref = f32[64,512]{1,0:T(8,128)S(1)} custom-call(f32[64,512]{1,0:T(8,128)S(1)} %get-tuple-element.56.v_ref.refs_0_.refs_1_, f32[5,8,1024]{2,1,0:T(8,128)S(1)} %get-tuple-element.59.own_ref, f32[5,8,1024]{2,1,0:T(8,128)S(1)} %collective-permute-done.4.plus1, f32[5,8,1024]{2,1,0:T(8,128)S(1)} %collective-permute-done.5.minus1, ...), custom_call_target="tpu_custom_call" | custom-call | flops 1342177280 | bytes 10485760 | tf_op jit(solution)/shard_map/pallas_call | solution.py:416
  73.5 4.0 %collective-permute-start.12 = (f32[3,8,1024]{2,1,0:T(8,128)S(1)}, f32[3,8,1024]{2,1,0:T(8,128)S(1)}, u32[]{:S(2)}, u32[]{:S(2)}) collective-permute-start(f32[3,8,1024]{2,1,0:T(8,128)S(1)} %get-tuple-element.76), channel_id=1, source_target_pairs={{0,56},{4,60},{8,0},{12,4},{16,8},{20,12},{24,16},{28,20},{32,24},... | collective-permute-start | bytes 294920 | tf_op jit(solution)/shard_map/ppermute | solution.py:39
  77.5 1.9 %collective-permute-start.13 = (f32[3,8,1024]{2,1,0:T(8,128)S(1)}, f32[3,8,1024]{2,1,0:T(8,128)S(1)}, u32[]{:S(2)}, u32[]{:S(2)}) collective-permute-start(f32[3,8,1024]{2,1,0:T(8,128)S(1)} %get-tuple-element.77), channel_id=1, source_target_pairs={{0,8},{4,12},{8,16},{12,20},{16,24},{20,28},{24,32},{28,36},{32,40... | collective-permute-start | bytes 294920 | tf_op jit(solution)/shard_map/ppermute | solution.py:39
  79.4 5.3 %collective-permute-start.14 = (f32[8,512]{1,0:T(8,128)S(1)}, f32[8,512]{1,0:T(8,128)S(1)}, u32[]{:S(2)}, u32[]{:S(2)}) collective-permute-start(f32[8,512]{1,0:T(8,128)S(1)} %get-tuple-element.78), channel_id=1, source_target_pairs={{0,1},{2,3},{1,0},{3,2},{4,5},{6,7},{5,4},{7,6},{8,9},{10,11},{9,8... | collective-permute-start | bytes 49160 | tf_op jit(solution)/shard_map/ppermute | solution.py:373
  85.4 1.8 %shard_map.93.part_ref = f32[64,512]{1,0:T(8,128)S(1)} custom-call(f32[64,512]{1,0:T(8,128)S(1)} %get-tuple-element.70.v_ref.refs_1_.refs_2_, f32[5,8,1024]{2,1,0:T(8,128)S(1)} %get-tuple-element.71.own_ref, f32[5,8,1024]{2,1,0:T(8,128)S(1)} %collective-permute-done.10.plus1, f32[5,8,1024]{2,1,0:T(8,128)S(1)} %collective-permute-done.11.minus1, ...), custom_call_target="tpu_custom_call" | custom-call | flops 1342177280 | bytes 10485760 | tf_op jit(solution)/shard_map/pallas_call | solution.py:416
  90.5 5.8 %collective-permute-start.18 = (f32[3,8,1024]{2,1,0:T(8,128)S(1)}, f32[3,8,1024]{2,1,0:T(8,128)S(1)}, u32[]{:S(2)}, u32[]{:S(2)}) collective-permute-start(f32[3,8,1024]{2,1,0:T(8,128)S(1)} %get-tuple-element.86), channel_id=1, source_target_pairs={{0,56},{4,60},{8,0},{12,4},{16,8},{20,12},{24,16},{28,20},{32,24},... | collective-permute-start | bytes 294920 | tf_op jit(solution)/shard_map/ppermute | solution.py:39
  96.3 1.9 %collective-permute-start.19 = (f32[3,8,1024]{2,1,0:T(8,128)S(1)}, f32[3,8,1024]{2,1,0:T(8,128)S(1)}, u32[]{:S(2)}, u32[]{:S(2)}) collective-permute-start(f32[3,8,1024]{2,1,0:T(8,128)S(1)} %get-tuple-element.87), channel_id=1, source_target_pairs={{0,8},{4,12},{8,16},{12,20},{16,24},{20,28},{24,32},{28,36},{32,40... | collective-permute-start | bytes 294920 | tf_op jit(solution)/shard_map/ppermute | solution.py:39
  98.2 3.9 %collective-permute-start.20 = (f32[8,512]{1,0:T(8,128)S(1)}, f32[8,512]{1,0:T(8,128)S(1)}, u32[]{:S(2)}, u32[]{:S(2)}) collective-permute-start(f32[8,512]{1,0:T(8,128)S(1)} %get-tuple-element.88), channel_id=1, source_target_pairs={{0,1},{2,3},{1,0},{3,2},{4,5},{6,7},{5,4},{7,6},{8,9},{10,11},{9,8... | collective-permute-start | bytes 49160 | tf_op jit(solution)/shard_map/ppermute | solution.py:373
  103.0 1.8 %shard_map.95.part_ref = f32[64,512]{1,0:T(8,128)S(1)} custom-call(f32[64,512]{1,0:T(8,128)S(1)} %get-tuple-element.80.v_ref.refs_2_.refs_3_, f32[5,8,1024]{2,1,0:T(8,128)S(1)} %get-tuple-element.81.own_ref, f32[5,8,1024]{2,1,0:T(8,128)S(1)} %collective-permute-done.16.plus1, f32[5,8,1024]{2,1,0:T(8,128)S(1)} %collective-permute-done.17.minus1, ...), custom_call_target="tpu_custom_call" | custom-call | flops 1342177280 | bytes 10485760 | tf_op jit(solution)/shard_map/pallas_call | solution.py:416
  106.4 1.7 %collective-permute-start.23 = (f32[5,8,1024]{2,1,0:T(8,128)S(1)}, f32[5,8,1024]{2,1,0:T(8,128)S(1)}, u32[]{:S(2)}, u32[]{:S(2)}) collective-permute-start(f32[5,8,1024]{2,1,0:T(8,128)S(1)} %get-tuple-element.95), channel_id=1, source_target_pairs={{0,4},{4,8},{8,12},{12,16},{16,20},{20,24},{24,28},{28,32},{32,36}... | collective-permute-start | bytes 491528 | tf_op jit(solution)/shard_map/ppermute | solution.py:39
  108.2 5.8 %collective-permute-start.24 = (f32[3,8,1024]{2,1,0:T(8,128)S(1)}, f32[3,8,1024]{2,1,0:T(8,128)S(1)}, u32[]{:S(2)}, u32[]{:S(2)}) collective-permute-start(f32[3,8,1024]{2,1,0:T(8,128)S(1)} %get-tuple-element.96), channel_id=1, source_target_pairs={{0,56},{4,60},{8,0},{12,4},{16,8},{20,12},{24,16},{28,20},{32,24},... | collective-permute-start | bytes 294920 | tf_op jit(solution)/shard_map/ppermute | solution.py:39
  113.9 1.9 %collective-permute-start.25 = (f32[3,8,1024]{2,1,0:T(8,128)S(1)}, f32[3,8,1024]{2,1,0:T(8,128)S(1)}, u32[]{:S(2)}, u32[]{:S(2)}) collective-permute-start(f32[3,8,1024]{2,1,0:T(8,128)S(1)} %get-tuple-element.97), channel_id=1, source_target_pairs={{0,8},{4,12},{8,16},{12,20},{16,24},{20,28},{24,32},{28,36},{32,40... | collective-permute-start | bytes 294920 | tf_op jit(solution)/shard_map/ppermute | solution.py:39
  115.9 4.2 %collective-permute-start.26 = (f32[8,512]{1,0:T(8,128)S(1)}, f32[8,512]{1,0:T(8,128)S(1)}, u32[]{:S(2)}, u32[]{:S(2)}) collective-permute-start(f32[8,512]{1,0:T(8,128)S(1)} %get-tuple-element.98), channel_id=1, source_target_pairs={{0,1},{2,3},{1,0},{3,2},{4,5},{6,7},{5,4},{7,6},{8,9},{10,11},{9,8... | collective-permute-start | bytes 49160 | tf_op jit(solution)/shard_map/ppermute | solution.py:373
  120.8 1.8 %shard_map.97.part_ref = f32[64,512]{1,0:T(8,128)S(1)} custom-call(f32[64,512]{1,0:T(8,128)S(1)} %get-tuple-element.90.v_ref.refs_3_.refs_4_, f32[5,8,1024]{2,1,0:T(8,128)S(1)} %get-tuple-element.91.own_ref, f32[5,8,1024]{2,1,0:T(8,128)S(1)} %collective-permute-done.22.plus1, f32[5,8,1024]{2,1,0:T(8,128)S(1)} %collective-permute-done.23.minus1, ...), custom_call_target="tpu_custom_call" | custom-call | flops 1342177280 | bytes 10485760 | tf_op jit(solution)/shard_map/pallas_call | solution.py:416
  122.9 19.3 %all_to_all.11 = f32[64,1,128]{2,1,0:T(1,128)S(1)} all-to-all(f32[64,1,128]{2,1,0:T(1,128)S(1)} %bitcast.14), channel_id=1, replica_groups=mesh['orbit'=8,'lon'=16,'lat'=4] {'lon','lat'}, dimensions={0} | all-to-all | bytes 65536 | tf_op jit(solution)/shard_map/all_to_all | solution.py:423
  (48 shorter events, 19.1 us)
Async XLA Ops:
  29.3 22.6 %collective-permute-start.3 = (f32[8,1024]{1,0:T(8,128)S(1)}, f32[8,1024]{1,0:T(8,128)S(1)}, u32[]{:S(2)}, u32[]{:S(2)}) collective-permute-start(f32[8,1024]{1,0:T(8,128)S(1)} %shard_map.87.z2), channel_id=1, source_target_pairs={{0,8},{4,12},{8,16},{12,20},{16,24},{20,28},{24,32},{28,36},{32,40... | collective-permute-start | bytes 98312 | tf_op jit(solution)/shard_map/ppermute | solution.py:39
  32.5 19.4 %collective-permute-start.2 = (f32[8,1024]{1,0:T(8,128)S(1)}, f32[8,1024]{1,0:T(8,128)S(1)}, u32[]{:S(2)}, u32[]{:S(2)}) collective-permute-start(f32[8,1024]{1,0:T(8,128)S(1)} %shard_map.87.z2), channel_id=1, source_target_pairs={{0,4},{4,8},{8,12},{12,16},{16,20},{20,24},{24,28},{28,32},{32,36}... | collective-permute-start | bytes 98312 | tf_op jit(solution)/shard_map/ppermute | solution.py:39
  40.2 11.7 %collective-permute-start.1 = (f32[8,1024]{1,0:T(8,128)S(1)}, f32[8,1024]{1,0:T(8,128)S(1)}, u32[]{:S(2)}, u32[]{:S(2)}) collective-permute-start(f32[8,1024]{1,0:T(8,128)S(1)} %shard_map.87.z2), channel_id=1, source_target_pairs={{0,60},{4,0},{8,4},{12,8},{16,12},{20,16},{24,20},{28,24},{32,28},... | collective-permute-start | bytes 98312 | tf_op jit(solution)/shard_map/ppermute | solution.py:39
  40.2 11.7 %collective-permute-start = (f32[8,1024]{1,0:T(8,128)S(1)}, f32[8,1024]{1,0:T(8,128)S(1)}, u32[]{:S(2)}, u32[]{:S(2)}) collective-permute-start(f32[8,1024]{1,0:T(8,128)S(1)} %shard_map.87.z2), channel_id=1, source_target_pairs={{0,56},{4,60},{8,0},{12,4},{16,8},{20,12},{24,16},{28,20},{32,24},... | collective-permute-start | bytes 98312 | tf_op jit(solution)/shard_map/ppermute | solution.py:39
  55.1 10.7 %collective-permute-start.4 = (f32[5,8,1024]{2,1,0:T(8,128)S(1)}, f32[5,8,1024]{2,1,0:T(8,128)S(1)}, u32[]{:S(2)}, u32[]{:S(2)}) collective-permute-start(f32[5,8,1024]{2,1,0:T(8,128)S(1)} %get-tuple-element.60), channel_id=1, source_target_pairs={{0,60},{4,0},{8,4},{12,8},{16,12},{20,16},{24,20},{28,24},{32,28},... | collective-permute-start | bytes 491528 | tf_op jit(solution)/shard_map/ppermute | solution.py:39
  56.2 12.2 %collective-permute-start.5 = (f32[5,8,1024]{2,1,0:T(8,128)S(1)}, f32[5,8,1024]{2,1,0:T(8,128)S(1)}, u32[]{:S(2)}, u32[]{:S(2)}) collective-permute-start(f32[5,8,1024]{2,1,0:T(8,128)S(1)} %get-tuple-element.63), channel_id=1, source_target_pairs={{0,4},{4,8},{8,12},{12,16},{16,20},{20,24},{24,28},{28,32},{32,36}... | collective-permute-start | bytes 491528 | tf_op jit(solution)/shard_map/ppermute | solution.py:39
  57.1 9.4 %collective-permute-start.6 = (f32[3,8,1024]{2,1,0:T(8,128)S(1)}, f32[3,8,1024]{2,1,0:T(8,128)S(1)}, u32[]{:S(2)}, u32[]{:S(2)}) collective-permute-start(f32[3,8,1024]{2,1,0:T(8,128)S(1)} %get-tuple-element.64), channel_id=1, source_target_pairs={{0,56},{4,60},{8,0},{12,4},{16,8},{20,12},{24,16},{28,20},{32,24},... | collective-permute-start | bytes 294920 | tf_op jit(solution)/shard_map/ppermute | solution.py:39
  60.7 7.6 %collective-permute-start.7 = (f32[3,8,1024]{2,1,0:T(8,128)S(1)}, f32[3,8,1024]{2,1,0:T(8,128)S(1)}, u32[]{:S(2)}, u32[]{:S(2)}) collective-permute-start(f32[3,8,1024]{2,1,0:T(8,128)S(1)} %get-tuple-element.65), channel_id=1, source_target_pairs={{0,8},{4,12},{8,16},{12,20},{16,24},{20,28},{24,32},{28,36},{32,40... | collective-permute-start | bytes 294920 | tf_op jit(solution)/shard_map/ppermute | solution.py:39
  62.7 7.5 %collective-permute-start.8 = (f32[8,512]{1,0:T(8,128)S(1)}, f32[8,512]{1,0:T(8,128)S(1)}, u32[]{:S(2)}, u32[]{:S(2)}) collective-permute-start(f32[8,512]{1,0:T(8,128)S(1)} %get-tuple-element.68), channel_id=1, source_target_pairs={{0,1},{2,3},{1,0},{3,2},{4,5},{6,7},{5,4},{7,6},{8,9},{10,11},{9,8... | collective-permute-start | bytes 49160 | tf_op jit(solution)/shard_map/ppermute | solution.py:373
  71.7 13.0 %collective-permute-start.10 = (f32[5,8,1024]{2,1,0:T(8,128)S(1)}, f32[5,8,1024]{2,1,0:T(8,128)S(1)}, u32[]{:S(2)}, u32[]{:S(2)}) collective-permute-start(f32[5,8,1024]{2,1,0:T(8,128)S(1)} %get-tuple-element.72), channel_id=1, source_target_pairs={{0,60},{4,0},{8,4},{12,8},{16,12},{20,16},{24,20},{28,24},{32,28},... | collective-permute-start | bytes 491528 | tf_op jit(solution)/shard_map/ppermute | solution.py:39
  72.4 13.0 %collective-permute-start.11 = (f32[5,8,1024]{2,1,0:T(8,128)S(1)}, f32[5,8,1024]{2,1,0:T(8,128)S(1)}, u32[]{:S(2)}, u32[]{:S(2)}) collective-permute-start(f32[5,8,1024]{2,1,0:T(8,128)S(1)} %get-tuple-element.75), channel_id=1, source_target_pairs={{0,4},{4,8},{8,12},{12,16},{16,20},{20,24},{24,28},{28,32},{32,36}... | collective-permute-start | bytes 491528 | tf_op jit(solution)/shard_map/ppermute | solution.py:39
  73.5 11.9 %collective-permute-start.12 = (f32[3,8,1024]{2,1,0:T(8,128)S(1)}, f32[3,8,1024]{2,1,0:T(8,128)S(1)}, u32[]{:S(2)}, u32[]{:S(2)}) collective-permute-start(f32[3,8,1024]{2,1,0:T(8,128)S(1)} %get-tuple-element.76), channel_id=1, source_target_pairs={{0,56},{4,60},{8,0},{12,4},{16,8},{20,12},{24,16},{28,20},{32,24},... | collective-permute-start | bytes 294920 | tf_op jit(solution)/shard_map/ppermute | solution.py:39
  77.5 7.9 %collective-permute-start.13 = (f32[3,8,1024]{2,1,0:T(8,128)S(1)}, f32[3,8,1024]{2,1,0:T(8,128)S(1)}, u32[]{:S(2)}, u32[]{:S(2)}) collective-permute-start(f32[3,8,1024]{2,1,0:T(8,128)S(1)} %get-tuple-element.77), channel_id=1, source_target_pairs={{0,8},{4,12},{8,16},{12,20},{16,24},{20,28},{24,32},{28,36},{32,40... | collective-permute-start | bytes 294920 | tf_op jit(solution)/shard_map/ppermute | solution.py:39
  79.4 7.8 %collective-permute-start.14 = (f32[8,512]{1,0:T(8,128)S(1)}, f32[8,512]{1,0:T(8,128)S(1)}, u32[]{:S(2)}, u32[]{:S(2)}) collective-permute-start(f32[8,512]{1,0:T(8,128)S(1)} %get-tuple-element.78), channel_id=1, source_target_pairs={{0,1},{2,3},{1,0},{3,2},{4,5},{6,7},{5,4},{7,6},{8,9},{10,11},{9,8... | collective-permute-start | bytes 49160 | tf_op jit(solution)/shard_map/ppermute | solution.py:373
  88.8 13.3 %collective-permute-start.16 = (f32[5,8,1024]{2,1,0:T(8,128)S(1)}, f32[5,8,1024]{2,1,0:T(8,128)S(1)}, u32[]{:S(2)}, u32[]{:S(2)}) collective-permute-start(f32[5,8,1024]{2,1,0:T(8,128)S(1)} %get-tuple-element.82), channel_id=1, source_target_pairs={{0,60},{4,0},{8,4},{12,8},{16,12},{20,16},{24,20},{28,24},{32,28},... | collective-permute-start | bytes 491528 | tf_op jit(solution)/shard_map/ppermute | solution.py:39
  88.8 14.2 %collective-permute-start.17 = (f32[5,8,1024]{2,1,0:T(8,128)S(1)}, f32[5,8,1024]{2,1,0:T(8,128)S(1)}, u32[]{:S(2)}, u32[]{:S(2)}) collective-permute-start(f32[5,8,1024]{2,1,0:T(8,128)S(1)} %get-tuple-element.85), channel_id=1, source_target_pairs={{0,4},{4,8},{8,12},{12,16},{16,20},{20,24},{24,28},{28,32},{32,36}... | collective-permute-start | bytes 491528 | tf_op jit(solution)/shard_map/ppermute | solution.py:39
  90.5 12.4 %collective-permute-start.18 = (f32[3,8,1024]{2,1,0:T(8,128)S(1)}, f32[3,8,1024]{2,1,0:T(8,128)S(1)}, u32[]{:S(2)}, u32[]{:S(2)}) collective-permute-start(f32[3,8,1024]{2,1,0:T(8,128)S(1)} %get-tuple-element.86), channel_id=1, source_target_pairs={{0,56},{4,60},{8,0},{12,4},{16,8},{20,12},{24,16},{28,20},{32,24},... | collective-permute-start | bytes 294920 | tf_op jit(solution)/shard_map/ppermute | solution.py:39
  96.3 6.7 %collective-permute-start.19 = (f32[3,8,1024]{2,1,0:T(8,128)S(1)}, f32[3,8,1024]{2,1,0:T(8,128)S(1)}, u32[]{:S(2)}, u32[]{:S(2)}) collective-permute-start(f32[3,8,1024]{2,1,0:T(8,128)S(1)} %get-tuple-element.87), channel_id=1, source_target_pairs={{0,8},{4,12},{8,16},{12,20},{16,24},{20,28},{24,32},{28,36},{32,40... | collective-permute-start | bytes 294920 | tf_op jit(solution)/shard_map/ppermute | solution.py:39
  98.2 6.6 %collective-permute-start.20 = (f32[8,512]{1,0:T(8,128)S(1)}, f32[8,512]{1,0:T(8,128)S(1)}, u32[]{:S(2)}, u32[]{:S(2)}) collective-permute-start(f32[8,512]{1,0:T(8,128)S(1)} %get-tuple-element.88), channel_id=1, source_target_pairs={{0,1},{2,3},{1,0},{3,2},{4,5},{6,7},{5,4},{7,6},{8,9},{10,11},{9,8... | collective-permute-start | bytes 49160 | tf_op jit(solution)/shard_map/ppermute | solution.py:373
  106.4 13.7 %collective-permute-start.22 = (f32[5,8,1024]{2,1,0:T(8,128)S(1)}, f32[5,8,1024]{2,1,0:T(8,128)S(1)}, u32[]{:S(2)}, u32[]{:S(2)}) collective-permute-start(f32[5,8,1024]{2,1,0:T(8,128)S(1)} %get-tuple-element.92), channel_id=1, source_target_pairs={{0,60},{4,0},{8,4},{12,8},{16,12},{20,16},{24,20},{28,24},{32,28},... | collective-permute-start | bytes 491528 | tf_op jit(solution)/shard_map/ppermute | solution.py:39
  106.4 14.4 %collective-permute-start.23 = (f32[5,8,1024]{2,1,0:T(8,128)S(1)}, f32[5,8,1024]{2,1,0:T(8,128)S(1)}, u32[]{:S(2)}, u32[]{:S(2)}) collective-permute-start(f32[5,8,1024]{2,1,0:T(8,128)S(1)} %get-tuple-element.95), channel_id=1, source_target_pairs={{0,4},{4,8},{8,12},{12,16},{16,20},{20,24},{24,28},{28,32},{32,36}... | collective-permute-start | bytes 491528 | tf_op jit(solution)/shard_map/ppermute | solution.py:39
  108.2 12.6 %collective-permute-start.24 = (f32[3,8,1024]{2,1,0:T(8,128)S(1)}, f32[3,8,1024]{2,1,0:T(8,128)S(1)}, u32[]{:S(2)}, u32[]{:S(2)}) collective-permute-start(f32[3,8,1024]{2,1,0:T(8,128)S(1)} %get-tuple-element.96), channel_id=1, source_target_pairs={{0,56},{4,60},{8,0},{12,4},{16,8},{20,12},{24,16},{28,20},{32,24},... | collective-permute-start | bytes 294920 | tf_op jit(solution)/shard_map/ppermute | solution.py:39
  113.9 6.9 %collective-permute-start.25 = (f32[3,8,1024]{2,1,0:T(8,128)S(1)}, f32[3,8,1024]{2,1,0:T(8,128)S(1)}, u32[]{:S(2)}, u32[]{:S(2)}) collective-permute-start(f32[3,8,1024]{2,1,0:T(8,128)S(1)} %get-tuple-element.97), channel_id=1, source_target_pairs={{0,8},{4,12},{8,16},{12,20},{16,24},{20,28},{24,32},{28,36},{32,40... | collective-permute-start | bytes 294920 | tf_op jit(solution)/shard_map/ppermute | solution.py:39
  115.9 6.8 %collective-permute-start.26 = (f32[8,512]{1,0:T(8,128)S(1)}, f32[8,512]{1,0:T(8,128)S(1)}, u32[]{:S(2)}, u32[]{:S(2)}) collective-permute-start(f32[8,512]{1,0:T(8,128)S(1)} %get-tuple-element.98), channel_id=1, source_target_pairs={{0,1},{2,3},{1,0},{3,2},{4,5},{6,7},{5,4},{7,6},{8,9},{10,11},{9,8... | collective-permute-start | bytes 49160 | tf_op jit(solution)/shard_map/ppermute | solution.py:373
  (4 other events, 12.1 us)
